TPU v7x, 512 devices: a whole 4x8x8 slice. The times are simulated.
512 devices in a mesh: outer: 16 (over z_hi, x, core), inner: 32 (over z_lo, y).
Axes of the slice: x: 4, y: 8, z: 8 (z_hi: 2, z_lo: 4; z = z_hi * 4 + z_lo), core: 2. Of those that a mesh axis runs over, the one named last changes fastest.
Arguments:
- diag_blocks: float32 [65536, 128], P(('outer', 'inner')), may hold values from -24 to 25, as said below
- left_bases: float32 [9, 65536, 128], P(None, ('outer', 'inner')), may hold values from -6 to 6
- right_bases: float32 [9, 65536, 128], P(None, ('outer', 'inner')), may hold values from -0.0625 to 0.0625, as said below
- sources: float32 [65536, 128], P(('outer', 'inner')), may hold values from -6 to 6
Outputs:
- updated_bases: float32 [9, 65536, 128], P(None, ('outer', 'inner'))
- solution: float32 [65536, 128], P(('outer', 'inner'))
Inputs may be any that keep to these rules, and one draw needn't show every extreme that they name: `diag_blocks`: each leaf block is symmetric with all eigenvalues 1 or more. `right_bases`: the row bases of level l have entries within 8 / (128 * 2 ** (l - 1)) of zero.
All inputs are finite; a program needn't handle non-finite values.
Results may differ from a plain program's by a relative error of at most 0.0001.
Values sent between devices are 32-bit elements; how exact they have to be, the bound alone decides.
No kernel may reach another device: no remote copies, remote signals or barrier semaphores. Data moves between devices by JAX's collectives and lax.ppermute only.
A program may use at most 64 MiB of HBM per device.

v0:
```python
import jax
import jax.numpy as jnp
from jax import lax
from jax.sharding import PartitionSpec as P

HI = lax.Precision.HIGHEST


def partner(block, axis, stride):
    count = lax.axis_size(axis)
    route = []
    for low in range(count):
        high = low | 1 << stride
        if high != low and high < count:
            route += [(low, high), (high, low)]
    return lax.ppermute(block, axis, route)


def solve_lower(factor, target, transpose):
    return lax.linalg.triangular_solve(
        factor, target, left_side=True, lower=True, transpose_a=transpose
    )


def group_total(partial_value, level):
    total = partial_value
    for bit in range(level):
        total = total + partner(total, ("outer", "inner"), bit)
    return total


def level_sums(partial_value, level, is_lower):
    total = group_total(partial_value, level)
    other = partner(total, ("outer", "inner"), level)
    lower_sum = jnp.where(is_lower, total, other)
    upper_sum = jnp.where(is_lower, other, total)
    return (lower_sum, upper_sum)


def per_device(diag_blocks, left_bases, right_bases, sources):
    inner_count = lax.axis_size("inner")
    place = lax.axis_index("outer") * inner_count + lax.axis_index("inner")
    levels = left_bases.shape[0]
    rank = left_bases.shape[2]
    factor = jnp.linalg.cholesky(diag_blocks)
    stacked = jnp.concatenate([left_bases[level] for level in range(levels)] + [sources], axis=1)
    first = solve_lower(factor, stacked, False)
    solved = solve_lower(factor, first, True)
    eye = jnp.eye(rank, dtype=jnp.float32)
    for level in range(levels):
        start = level * rank
        current = solved[:, start : start + rank]
        partial_value = jnp.einsum("nr,nc->rc", right_bases[level], solved[:, start:], precision=HI)
        side = place // 2**level % 2
        is_lower = side == 0
        lower_sum, upper_sum = level_sums(partial_value, level, is_lower)
        lower_g = lower_sum[:, :rank]
        upper_g = upper_sum[:, :rank]
        lower_p = lower_sum[:, rank:]
        upper_p = upper_sum[:, rank:]
        matrix = eye - jnp.dot(lower_g, upper_g, precision=HI)
        normal = jnp.dot(matrix.T, matrix, precision=HI)
        chol = jnp.linalg.cholesky(normal)
        right = lower_p - jnp.dot(lower_g, upper_p, precision=HI)
        right = jnp.dot(matrix.T, right, precision=HI)
        forward = solve_lower(chol, right, False)
        upper_y = solve_lower(chol, forward, True)
        lower_y = upper_p - jnp.dot(upper_g, upper_y, precision=HI)
        own_coef = jnp.where(is_lower, lower_y, upper_y)
        later = solved[:, start + rank :] - jnp.dot(current, own_coef, precision=HI)
        solved = jnp.concatenate([solved[:, : start + rank], later], axis=1)
    width = levels * rank
    updated = solved[:, :width].reshape(solved.shape[0], levels, rank).transpose(1, 0, 2)
    return (updated, solved[:, width:])


def solution(mesh):
    placed = (
        P(("outer", "inner"), None),
        P(None, ("outer", "inner"), None),
        P(None, ("outer", "inner"), None),
        P(("outer", "inner"), None),
    )
    return jax.shard_map(
        per_device,
        mesh=mesh,
        in_specs=placed,
        out_specs=(P(None, ("outer", "inner"), None), P(("outer", "inner"), None)),
        check_vma=False,
    )
```

profile of v0, /device:TPU:6, one launch (start us, length us, event | category | flops | bytes accessed | tf_op | source)
XLA Modules:
  0.0 982.3 jit_solution(2160718254151179725)
XLA Ops:
  1.7 11.7 %cholesky.164 = f32[128,128]{1,0:T(8,128)S(1)} custom-call(f32[128,128]{1,0:T(8,128)S(1)} %fusion.110), custom_call_target="Cholesky" | custom-call | tf_op jit(solution)/shard_map/jit(cholesky)/cholesky | solution.py:45
  33.5 14.7 %collective-permute-done = f32[128,1280]{0,1:T(8,128)S(1)} collective-permute-done((f32[128,1280]{0,1:T(8,128)S(1)}, f32[128,1280]{0,1:T(8,128)S(1)}, u32[]{:S(2)}, u32[]{:S(2)}) %collective-permute-start) | collective-permute-done | bytes 655392 | tf_op jit(solution)/shard_map/ppermute | solution.py:16
  49.6 11.7 %cholesky.175 = f32[128,128]{1,0:T(8,128)S(1)} custom-call(f32[128,128]{1,0:T(8,128)S(1)} %fusion.104), custom_call_target="Cholesky" | custom-call | tf_op jit(solution)/shard_map/jit(cholesky)/cholesky | solution.py:63
  82.2 12.6 %collective-permute-done.1 = f32[128,1152]{0,1:T(8,128)S(1)} collective-permute-done((f32[128,1152]{0,1:T(8,128)S(1)}, f32[128,1152]{0,1:T(8,128)S(1)}, u32[]{:S(2)}, u32[]{:S(2)}) %collective-permute-start.1) | collective-permute-done | bytes 589856 | tf_op jit(solution)/shard_map/ppermute | solution.py:16
  99.4 24.4 %collective-permute-done.2 = f32[128,1152]{0,1:T(8,128)} collective-permute-done((f32[128,1152]{0,1:T(8,128)S(1)}, f32[128,1152]{0,1:T(8,128)}, u32[]{:S(2)}, u32[]{:S(2)}) %collective-permute-start.2) | collective-permute-done | bytes 589856 | tf_op jit(solution)/shard_map/ppermute | solution.py:16
  126.2 11.7 %cholesky.186 = f32[128,128]{1,0:T(8,128)S(1)} custom-call(f32[128,128]{1,0:T(8,128)S(1)} %fusion.98), custom_call_target="Cholesky" | custom-call | tf_op jit(solution)/shard_map/jit(cholesky)/cholesky | solution.py:63
  157.1 12.3 %collective-permute-done.3 = f32[128,1024]{0,1:T(8,128)S(1)} collective-permute-done((f32[128,1024]{0,1:T(8,128)S(1)}, f32[128,1024]{0,1:T(8,128)S(1)}, u32[]{:S(2)}, u32[]{:S(2)}) %collective-permute-start.3) | collective-permute-done | bytes 524320 | tf_op jit(solution)/shard_map/ppermute | solution.py:16
  175.0 22.3 %collective-permute-done.4 = f32[128,1024]{0,1:T(8,128)S(1)} collective-permute-done((f32[128,1024]{0,1:T(8,128)S(1)}, f32[128,1024]{0,1:T(8,128)S(1)}, u32[]{:S(2)}, u32[]{:S(2)}) %collective-permute-start.4) | collective-permute-done | bytes 524320 | tf_op jit(solution)/shard_map/ppermute | solution.py:16
  205.0 23.5 %collective-permute-done.5 = f32[128,1024]{0,1:T(8,128)} collective-permute-done((f32[128,1024]{0,1:T(8,128)S(1)}, f32[128,1024]{0,1:T(8,128)}, u32[]{:S(2)}, u32[]{:S(2)}) %collective-permute-start.5) | collective-permute-done | bytes 524320 | tf_op jit(solution)/shard_map/ppermute | solution.py:16
  277.5 20.0 %collective-permute-done.7 = f32[128,896]{0,1:T(8,128)S(1)} collective-permute-done((f32[128,896]{0,1:T(8,128)S(1)}, f32[128,896]{0,1:T(8,128)S(1)}, u32[]{:S(2)}, u32[]{:S(2)}) %collective-permute-start.7) | collective-permute-done | bytes 458784 | tf_op jit(solution)/shard_map/ppermute | solution.py:16
  302.3 22.5 %collective-permute-done.8 = f32[128,896]{0,1:T(8,128)S(1)} collective-permute-done((f32[128,896]{0,1:T(8,128)S(1)}, f32[128,896]{0,1:T(8,128)S(1)}, u32[]{:S(2)}, u32[]{:S(2)}) %collective-permute-start.8) | collective-permute-done | bytes 458784 | tf_op jit(solution)/shard_map/ppermute | solution.py:16
  346.3 13.2 %cholesky.208 = f32[128,128]{1,0:T(8,128)} custom-call(f32[128,128]{1,0:T(8,128)} %fusion.86), custom_call_target="Cholesky" | custom-call | tf_op jit(solution)/shard_map/jit(cholesky)/cholesky | solution.py:63
  394.4 18.0 %collective-permute-done.11 = f32[128,768]{0,1:T(8,128)S(1)} collective-permute-done((f32[128,768]{0,1:T(8,128)S(1)}, f32[128,768]{0,1:T(8,128)S(1)}, u32[]{:S(2)}, u32[]{:S(2)}) %collective-permute-start.11) | collective-permute-done | bytes 393248 | tf_op jit(solution)/shard_map/ppermute | solution.py:16
  417.1 20.0 %collective-permute-done.12 = f32[128,768]{0,1:T(8,128)S(1)} collective-permute-done((f32[128,768]{0,1:T(8,128)S(1)}, f32[128,768]{0,1:T(8,128)S(1)}, u32[]{:S(2)}, u32[]{:S(2)}) %collective-permute-start.12) | collective-permute-done | bytes 393248 | tf_op jit(solution)/shard_map/ppermute | solution.py:16
  456.9 16.7 %collective-permute-done.14 = f32[128,768]{0,1:T(8,128)} collective-permute-done((f32[128,768]{0,1:T(8,128)S(1)}, f32[128,768]{0,1:T(8,128)}, u32[]{:S(2)}, u32[]{:S(2)}) %collective-permute-start.14) | collective-permute-done | bytes 393248 | tf_op jit(solution)/shard_map/ppermute | solution.py:16
  478.7 12.5 %cholesky.219 = f32[128,128]{1,0:T(8,128)S(1)} custom-call(f32[128,128]{1,0:T(8,128)} %fusion.80), custom_call_target="Cholesky" | custom-call | tf_op jit(solution)/shard_map/jit(cholesky)/cholesky | solution.py:63
  522.8 16.0 %collective-permute-done.16 = f32[128,640]{0,1:T(8,128)S(1)} collective-permute-done((f32[128,640]{0,1:T(8,128)S(1)}, f32[128,640]{0,1:T(8,128)S(1)}, u32[]{:S(2)}, u32[]{:S(2)}) %collective-permute-start.16) | collective-permute-done | bytes 327712 | tf_op jit(solution)/shard_map/ppermute | solution.py:16
  543.8 17.1 %collective-permute-done.17 = f32[128,640]{0,1:T(8,128)S(1)} collective-permute-done((f32[128,640]{0,1:T(8,128)S(1)}, f32[128,640]{0,1:T(8,128)S(1)}, u32[]{:S(2)}, u32[]{:S(2)}) %collective-permute-start.17) | collective-permute-done | bytes 327712 | tf_op jit(solution)/shard_map/ppermute | solution.py:16
  578.1 14.3 %collective-permute-done.19 = f32[128,640]{0,1:T(8,128)S(1)} collective-permute-done((f32[128,640]{0,1:T(8,128)S(1)}, f32[128,640]{0,1:T(8,128)S(1)}, u32[]{:S(2)}, u32[]{:S(2)}) %collective-permute-start.19) | collective-permute-done | bytes 327712 | tf_op jit(solution)/shard_map/ppermute | solution.py:16
  602.2 13.2 %cholesky.230 = f32[128,128]{1,0:T(8,128)} custom-call(f32[128,128]{1,0:T(8,128)} %fusion.74), custom_call_target="Cholesky" | custom-call | tf_op jit(solution)/shard_map/jit(cholesky)/cholesky | solution.py:63
  648.0 14.1 %collective-permute-done.22 = f32[128,512]{0,1:T(8,128)S(1)} collective-permute-done((f32[128,512]{0,1:T(8,128)S(1)}, f32[128,512]{0,1:T(8,128)S(1)}, u32[]{:S(2)}, u32[]{:S(2)}) %collective-permute-start.22) | collective-permute-done | bytes 262176 | tf_op jit(solution)/shard_map/ppermute | solution.py:16
  667.1 14.4 %collective-permute-done.23 = f32[128,512]{0,1:T(8,128)S(1)} collective-permute-done((f32[128,512]{0,1:T(8,128)S(1)}, f32[128,512]{0,1:T(8,128)S(1)}, u32[]{:S(2)}, u32[]{:S(2)}) %collective-permute-start.23) | collective-permute-done | bytes 262176 | tf_op jit(solution)/shard_map/ppermute | solution.py:16
  727.6 13.2 %cholesky.241 = f32[128,128]{1,0:T(8,128)} custom-call(f32[128,128]{1,0:T(8,128)} %fusion.68), custom_call_target="Cholesky" | custom-call | tf_op jit(solution)/shard_map/jit(cholesky)/cholesky | solution.py:63
  847.1 12.5 %cholesky.252 = f32[128,128]{1,0:T(8,128)S(1)} custom-call(f32[128,128]{1,0:T(8,128)} %fusion.62), custom_call_target="Cholesky" | custom-call | tf_op jit(solution)/shard_map/jit(cholesky)/cholesky | solution.py:63
  (332 shorter events, 596.8 us)
Async XLA Ops:
  29.8 18.4 %collective-permute-start = (f32[128,1280]{0,1:T(8,128)S(1)}, f32[128,1280]{0,1:T(8,128)S(1)}, u32[]{:S(2)}, u32[]{:S(2)}) collective-permute-start(f32[128,1280]{0,1:T(8,128)S(1)} %convolution_bitcast_fusion.1), channel_id=1, source_target_pairs={{0,1},{1,0},{2,3},{3,2},{4,5},{5,4},{6,7},{7,6},{8,9},{9,8},{10,11... | collective-permute-start | bytes 1966088 | tf_op jit(solution)/shard_map/ppermute | solution.py:16
  78.7 16.1 %collective-permute-start.1 = (f32[128,1152]{0,1:T(8,128)S(1)}, f32[128,1152]{0,1:T(8,128)S(1)}, u32[]{:S(2)}, u32[]{:S(2)}) collective-permute-start(f32[128,1152]{0,1:T(8,128)S(1)} %convolution_bitcast_fusion), channel_id=1, source_target_pairs={{0,1},{1,0},{2,3},{3,2},{4,5},{5,4},{6,7},{7,6},{8,9},{9,8},{10,11... | collective-permute-start | bytes 1769480 | tf_op jit(solution)/shard_map/ppermute | solution.py:16
  94.9 28.9 %collective-permute-start.2 = (f32[128,1152]{0,1:T(8,128)S(1)}, f32[128,1152]{0,1:T(8,128)}, u32[]{:S(2)}, u32[]{:S(2)}) collective-permute-start(f32[128,1152]{0,1:T(8,128)S(1)} %add.198), channel_id=1, source_target_pairs={{0,2},{2,0},{1,3},{3,1},{4,6},{6,4},{5,7},{7,5},{8,10},{10,8},{9,1... | collective-permute-start | bytes 1769480 | tf_op jit(solution)/shard_map/ppermute | solution.py:16
  154.6 14.7 %collective-permute-start.3 = (f32[128,1024]{0,1:T(8,128)S(1)}, f32[128,1024]{0,1:T(8,128)S(1)}, u32[]{:S(2)}, u32[]{:S(2)}) collective-permute-start(f32[128,1024]{0,1:T(8,128)S(1)} %convolution_bitcast_fusion.2), channel_id=1, source_target_pairs={{0,1},{1,0},{2,3},{3,2},{4,5},{5,4},{6,7},{7,6},{8,9},{9,8},{10,11... | collective-permute-start | bytes 1572872 | tf_op jit(solution)/shard_map/ppermute | solution.py:16
  169.4 28.0 %collective-permute-start.4 = (f32[128,1024]{0,1:T(8,128)S(1)}, f32[128,1024]{0,1:T(8,128)S(1)}, u32[]{:S(2)}, u32[]{:S(2)}) collective-permute-start(f32[128,1024]{0,1:T(8,128)S(1)} %add.200), channel_id=1, source_target_pairs={{0,2},{2,0},{1,3},{3,1},{4,6},{6,4},{5,7},{7,5},{8,10},{10,8},{9,1... | collective-permute-start | bytes 1572872 | tf_op jit(solution)/shard_map/ppermute | solution.py:16
  197.4 31.1 %collective-permute-start.5 = (f32[128,1024]{0,1:T(8,128)S(1)}, f32[128,1024]{0,1:T(8,128)}, u32[]{:S(2)}, u32[]{:S(2)}) collective-permute-start(f32[128,1024]{0,1:T(8,128)S(1)} %add.201), channel_id=1, source_target_pairs={{0,4},{4,0},{1,5},{5,1},{2,6},{6,2},{3,7},{7,3},{8,12},{12,8},{9,1... | collective-permute-start | bytes 1572872 | tf_op jit(solution)/shard_map/ppermute | solution.py:16
  260.9 13.4 %collective-permute-start.6 = (f32[128,896]{0,1:T(8,128)S(1)}, f32[128,896]{0,1:T(8,128)S(1)}, u32[]{:S(2)}, u32[]{:S(2)}) collective-permute-start(f32[128,896]{0,1:T(8,128)S(1)} %convolution_bitcast_fusion.3), channel_id=1, source_target_pairs={{0,1},{1,0},{2,3},{3,2},{4,5},{5,4},{6,7},{7,6},{8,9},{9,8},{10,11... | collective-permute-start | bytes 1376264 | tf_op jit(solution)/shard_map/ppermute | solution.py:16
  274.3 23.2 %collective-permute-start.7 = (f32[128,896]{0,1:T(8,128)S(1)}, f32[128,896]{0,1:T(8,128)S(1)}, u32[]{:S(2)}, u32[]{:S(2)}) collective-permute-start(f32[128,896]{0,1:T(8,128)S(1)} %add.203), channel_id=1, source_target_pairs={{0,2},{2,0},{1,3},{3,1},{4,6},{6,4},{5,7},{7,5},{8,10},{10,8},{9,1... | collective-permute-start | bytes 1376264 | tf_op jit(solution)/shard_map/ppermute | solution.py:16
  297.5 27.3 %collective-permute-start.8 = (f32[128,896]{0,1:T(8,128)S(1)}, f32[128,896]{0,1:T(8,128)S(1)}, u32[]{:S(2)}, u32[]{:S(2)}) collective-permute-start(f32[128,896]{0,1:T(8,128)S(1)} %add.204), channel_id=1, source_target_pairs={{0,4},{4,0},{1,5},{5,1},{2,6},{6,2},{3,7},{7,3},{8,12},{12,8},{9,1... | collective-permute-start | bytes 1376264 | tf_op jit(solution)/shard_map/ppermute | solution.py:16
  324.9 15.3 %collective-permute-start.9 = (f32[128,896]{0,1:T(8,128)S(1)}, f32[128,896]{0,1:T(8,128)}, u32[]{:S(2)}, u32[]{:S(2)}) collective-permute-start(f32[128,896]{0,1:T(8,128)S(1)} %add.205), channel_id=1, source_target_pairs={{0,8},{8,0},{1,9},{9,1},{2,10},{10,2},{3,11},{11,3},{4,12},{12,4},... | collective-permute-start | bytes 1376264 | tf_op jit(solution)/shard_map/ppermute | solution.py:16
  379.2 12.3 %collective-permute-start.10 = (f32[128,768]{0,1:T(8,128)S(1)}, f32[128,768]{0,1:T(8,128)S(1)}, u32[]{:S(2)}, u32[]{:S(2)}) collective-permute-start(f32[128,768]{0,1:T(8,128)S(1)} %convolution_bitcast_fusion.4), channel_id=1, source_target_pairs={{0,1},{1,0},{2,3},{3,2},{4,5},{5,4},{6,7},{7,6},{8,9},{9,8},{10,11... | collective-permute-start | bytes 1179656 | tf_op jit(solution)/shard_map/ppermute | solution.py:16
  391.6 20.8 %collective-permute-start.11 = (f32[128,768]{0,1:T(8,128)S(1)}, f32[128,768]{0,1:T(8,128)S(1)}, u32[]{:S(2)}, u32[]{:S(2)}) collective-permute-start(f32[128,768]{0,1:T(8,128)S(1)} %add.207), channel_id=1, source_target_pairs={{0,2},{2,0},{1,3},{3,1},{4,6},{6,4},{5,7},{7,5},{8,10},{10,8},{9,1... | collective-permute-start | bytes 1179656 | tf_op jit(solution)/shard_map/ppermute | solution.py:16
  412.4 24.6 %collective-permute-start.12 = (f32[128,768]{0,1:T(8,128)S(1)}, f32[128,768]{0,1:T(8,128)S(1)}, u32[]{:S(2)}, u32[]{:S(2)}) collective-permute-start(f32[128,768]{0,1:T(8,128)S(1)} %add.208), channel_id=1, source_target_pairs={{0,4},{4,0},{1,5},{5,1},{2,6},{6,2},{3,7},{7,3},{8,12},{12,8},{9,1... | collective-permute-start | bytes 1179656 | tf_op jit(solution)/shard_map/ppermute | solution.py:16
  437.1 12.9 %collective-permute-start.13 = (f32[128,768]{0,1:T(8,128)S(1)}, f32[128,768]{0,1:T(8,128)S(1)}, u32[]{:S(2)}, u32[]{:S(2)}) collective-permute-start(f32[128,768]{0,1:T(8,128)S(1)} %add.209), channel_id=1, source_target_pairs={{0,8},{8,0},{1,9},{9,1},{2,10},{10,2},{3,11},{11,3},{4,12},{12,4},... | collective-permute-start | bytes 1179656 | tf_op jit(solution)/shard_map/ppermute | solution.py:16
  450.1 23.6 %collective-permute-start.14 = (f32[128,768]{0,1:T(8,128)S(1)}, f32[128,768]{0,1:T(8,128)}, u32[]{:S(2)}, u32[]{:S(2)}) collective-permute-start(f32[128,768]{0,1:T(8,128)S(1)} %add.210), channel_id=1, source_target_pairs={{0,16},{16,0},{1,17},{17,1},{2,18},{18,2},{3,19},{19,3},{4,20},{20... | collective-permute-start | bytes 1179656 | tf_op jit(solution)/shard_map/ppermute | solution.py:16
  520.8 18.0 %collective-permute-start.16 = (f32[128,640]{0,1:T(8,128)S(1)}, f32[128,640]{0,1:T(8,128)S(1)}, u32[]{:S(2)}, u32[]{:S(2)}) collective-permute-start(f32[128,640]{0,1:T(8,128)S(1)} %add.212), channel_id=1, source_target_pairs={{0,2},{2,0},{1,3},{3,1},{4,6},{6,4},{5,7},{7,5},{8,10},{10,8},{9,1... | collective-permute-start | bytes 983048 | tf_op jit(solution)/shard_map/ppermute | solution.py:16
  538.9 22.1 %collective-permute-start.17 = (f32[128,640]{0,1:T(8,128)S(1)}, f32[128,640]{0,1:T(8,128)S(1)}, u32[]{:S(2)}, u32[]{:S(2)}) collective-permute-start(f32[128,640]{0,1:T(8,128)S(1)} %add.213), channel_id=1, source_target_pairs={{0,4},{4,0},{1,5},{5,1},{2,6},{6,2},{3,7},{7,3},{8,12},{12,8},{9,1... | collective-permute-start | bytes 983048 | tf_op jit(solution)/shard_map/ppermute | solution.py:16
  572.6 19.9 %collective-permute-start.19 = (f32[128,640]{0,1:T(8,128)S(1)}, f32[128,640]{0,1:T(8,128)S(1)}, u32[]{:S(2)}, u32[]{:S(2)}) collective-permute-start(f32[128,640]{0,1:T(8,128)S(1)} %add.215), channel_id=1, source_target_pairs={{0,16},{16,0},{1,17},{17,1},{2,18},{18,2},{3,19},{19,3},{4,20},{20... | collective-permute-start | bytes 983048 | tf_op jit(solution)/shard_map/ppermute | solution.py:16
  646.1 16.0 %collective-permute-start.22 = (f32[128,512]{0,1:T(8,128)S(1)}, f32[128,512]{0,1:T(8,128)S(1)}, u32[]{:S(2)}, u32[]{:S(2)}) collective-permute-start(f32[128,512]{0,1:T(8,128)S(1)} %add.218), channel_id=1, source_target_pairs={{0,2},{2,0},{1,3},{3,1},{4,6},{6,4},{5,7},{7,5},{8,10},{10,8},{9,1... | collective-permute-start | bytes 786440 | tf_op jit(solution)/shard_map/ppermute | solution.py:16
  662.1 19.3 %collective-permute-start.23 = (f32[128,512]{0,1:T(8,128)S(1)}, f32[128,512]{0,1:T(8,128)S(1)}, u32[]{:S(2)}, u32[]{:S(2)}) collective-permute-start(f32[128,512]{0,1:T(8,128)S(1)} %add.219), channel_id=1, source_target_pairs={{0,4},{4,0},{1,5},{5,1},{2,6},{6,2},{3,7},{7,3},{8,12},{12,8},{9,1... | collective-permute-start | bytes 786440 | tf_op jit(solution)/shard_map/ppermute | solution.py:16
  691.6 15.8 %collective-permute-start.25 = (f32[128,512]{0,1:T(8,128)S(1)}, f32[128,512]{0,1:T(8,128)S(1)}, u32[]{:S(2)}, u32[]{:S(2)}) collective-permute-start(f32[128,512]{0,1:T(8,128)S(1)} %add.221), channel_id=1, source_target_pairs={{0,16},{16,0},{1,17},{17,1},{2,18},{18,2},{3,19},{19,3},{4,20},{20... | collective-permute-start | bytes 786440 | tf_op jit(solution)/shard_map/ppermute | solution.py:16
  769.2 12.2 %collective-permute-start.29 = (f32[128,384]{0,1:T(8,128)S(1)}, f32[128,384]{0,1:T(8,128)S(1)}, u32[]{:S(2)}, u32[]{:S(2)}) collective-permute-start(f32[128,384]{0,1:T(8,128)S(1)} %add.225), channel_id=1, source_target_pairs={{0,2},{2,0},{1,3},{3,1},{4,6},{6,4},{5,7},{7,5},{8,10},{10,8},{9,1... | collective-permute-start | bytes 589832 | tf_op jit(solution)/shard_map/ppermute | solution.py:16
  781.5 16.3 %collective-permute-start.30 = (f32[128,384]{0,1:T(8,128)S(1)}, f32[128,384]{0,1:T(8,128)S(1)}, u32[]{:S(2)}, u32[]{:S(2)}) collective-permute-start(f32[128,384]{0,1:T(8,128)S(1)} %add.226), channel_id=1, source_target_pairs={{0,4},{4,0},{1,5},{5,1},{2,6},{6,2},{3,7},{7,3},{8,12},{12,8},{9,1... | collective-permute-start | bytes 589832 | tf_op jit(solution)/shard_map/ppermute | solution.py:16
  806.6 13.0 %collective-permute-start.32 = (f32[128,384]{0,1:T(8,128)S(1)}, f32[128,384]{0,1:T(8,128)S(1)}, u32[]{:S(2)}, u32[]{:S(2)}) collective-permute-start(f32[128,384]{0,1:T(8,128)S(1)} %add.228), channel_id=1, source_target_pairs={{0,16},{16,0},{1,17},{17,1},{2,18},{18,2},{3,19},{19,3},{4,20},{20... | collective-permute-start | bytes 589832 | tf_op jit(solution)/shard_map/ppermute | solution.py:16
  (42 other events, 242.4 us)
where the time goes:
time: 992 us; the launch traced here: 982 us
  waiting for transfers between devices  480 us (48%)
  other arithmetic  267 us (27%)
  starting transfers between devices  155 us (16%)
  matrix products  62 us (6%)
  local copies, waits for them, and re-layouts  15.8 us (2%)
    ppermute x45, waiting for transfers between devices, partner(): return lax.ppermute(block, axis, route)  480 us
    ppermute x45, starting transfers between devices, partner(): return lax.ppermute(block, axis, route)  155 us
    another operation x27, other arithmetic, per_device(): chol = jnp.linalg.cholesky(normal)  121 us
    another operation x20, other arithmetic, solve_lower(): lax.linalg.triangular_solve(factor, target, left_side=True, lower=True, t...  114 us
  transfers between devices with their start and end apart: 45, of which 45 were waited for; matrix products, arithmetic and copies ran while one was open for 0% of the time, Pallas kernels for 0%

commit v1 on v0

v1 whole, which is shorter than its diff:
```python
import jax
import jax.numpy as jnp
from jax import lax
from jax.experimental import pallas as pl
from jax.experimental.pallas import tpu as pltpu
from jax.sharding import Mesh, PartitionSpec as P

HI = lax.Precision.HIGHEST
BITS = 9
NAMES = tuple("b%d" % bit for bit in reversed(range(BITS)))
TOP = 5
N = 128


def axes(low, high):
    return tuple("b%d" % bit for bit in reversed(range(low, high)))


def dot(a, b):
    return jnp.dot(a, b, precision=HI, preferred_element_type=jnp.float32)


def tdot(a, b):
    return lax.dot_general(a, b, (((0,), (0,)), ((), ())), precision=HI, preferred_element_type=jnp.float32)


def quick(a, b):
    return jnp.dot(a.astype(jnp.bfloat16), b.astype(jnp.bfloat16), preferred_element_type=jnp.float32)


def eye():
    row = lax.broadcasted_iota(jnp.int32, (N, N), 0)
    col = lax.broadcasted_iota(jnp.int32, (N, N), 1)
    return (row == col).astype(jnp.float32)


def wide(ref, first, last):
    return jnp.concatenate([ref[i] for i in range(first, last)], axis=1)


def invert(matrix, start, rounds, out_ref):
    one = eye()
    value = start
    for _ in range(rounds):
        value = value + quick(value, one - quick(matrix, value))
    for _ in range(2):
        rest = one - dot(matrix, value)
        value = value + quick(value, rest)
    out_ref[...] = value
    left = jnp.sum(rest * rest)

    @pl.when(jnp.logical_not(left < 1e-6))
    def _():
        out_ref[...] = start

        def more(state):
            step, left = state
            return jnp.logical_and(step < 60, jnp.logical_not(left < 1e-9))

        def body(state):
            step, _ = state
            now = out_ref[...]
            rest = eye() - dot(matrix, now)
            out_ref[...] = now + dot(now, rest)
            return step + 1, jnp.sum(rest * rest)

        lax.while_loop(more, body, (jnp.int32(0), jnp.float32(1.0)))


def general_start(matrix):
    size = jnp.abs(matrix)
    by_col = jnp.max(jnp.sum(size, axis=0, keepdims=True), axis=1, keepdims=True)
    by_row = jnp.max(jnp.sum(size, axis=1, keepdims=True), axis=0, keepdims=True)
    return matrix.T * (1.9 / (by_col * by_row))


def leaf_kernel(diag_ref, left_ref, right_ref, source_ref, work_ref, panel_ref, inv_ref):
    levels = left_ref.shape[0]
    diag = diag_ref[...]
    bound = jnp.max(jnp.sum(jnp.abs(diag), axis=0, keepdims=True), axis=1, keepdims=True)
    invert(diag, eye() * (2.0 / (1.0 + bound)), 6, inv_ref)
    rhs = jnp.concatenate([left_ref[i] for i in range(levels)] + [source_ref[...]], axis=1)
    work = dot(inv_ref[...], rhs)
    panel = tdot(right_ref[...], work)
    for i in range(levels + 1):
        work_ref[i] = work[:, i * N : (i + 1) * N]
        panel_ref[i] = panel[:, i * N : (i + 1) * N]


def own_coef(own_ref, other_ref, count, inv_ref):
    own_g = own_ref[0]
    other_g = other_ref[0]
    matrix = eye() - dot(other_g, own_g)
    invert(matrix, general_start(matrix), 7, inv_ref)
    own_p = wide(own_ref, 1, count)
    right = wide(other_ref, 1, count) - dot(other_g, own_p)
    return dot(inv_ref[...], right)


def level_kernel(level, count, own_ref, other_ref, work_ref, right_ref, next_ref, panel_ref, inv_ref):
    coef = own_coef(own_ref, other_ref, count, inv_ref)
    later = wide(work_ref, level + 1, level + count) - dot(work_ref[level], coef)
    for i in range(level + 1):
        next_ref[i] = work_ref[i]
    for i in range(count - 1):
        next_ref[level + 1 + i] = later[:, i * N : (i + 1) * N]
    rows = right_ref.shape[0]
    for k in range(rows):
        panel = tdot(right_ref[k], later)
        for i in range(count - 1):
            panel_ref[k * (count - 1) + i] = panel[:, i * N : (i + 1) * N]


def front_kernel(count, own_ref, other_ref, coef_ref, front_ref, inv_ref):
    coef = own_coef(own_ref, other_ref, count, inv_ref)
    for i in range(count - 1):
        coef_ref[i] = coef[:, i * N : (i + 1) * N]
    other_coef = wide(own_ref, 1, count) - dot(own_ref[0], coef)
    for k in range(1, count - 1):
        base = k * count
        total = wide(own_ref, base + 1, base + count) + wide(other_ref, base + 1, base + count)
        total = total - dot(own_ref[base], coef) - dot(other_ref[base], other_coef)
        for i in range(count - 1):
            front_ref[(k - 1) * (count - 1) + i] = total[:, i * N : (i + 1) * N]


def last_front_kernel(count, own_ref, other_ref, coef_ref, inv_ref):
    coef_ref[0] = own_coef(own_ref, other_ref, count, inv_ref)


def apply_kernel(level, count, work_ref, coef_ref, next_ref):
    coef = wide(coef_ref, 0, count - 1)
    later = wide(work_ref, level + 1, level + count) - dot(work_ref[level], coef)
    for i in range(level + 1):
        next_ref[i] = work_ref[i]
    for i in range(count - 1):
        next_ref[level + 1 + i] = later[:, i * N : (i + 1) * N]


def blocks(count):
    return jax.ShapeDtypeStruct((count, N, N), jnp.float32)


def call(body, name, outs, *args, scratch=True):
    return pl.pallas_call(
        body,
        out_shape=outs,
        scratch_shapes=[pltpu.VMEM((N, N), jnp.float32)] if scratch else [],
        name=name,
    )(*args)


def partner(value, bit):
    return lax.ppermute(value, "b%d" % bit, [(0, 1), (1, 0)])


def exchange(value, names):
    return lax.all_to_all(value, names, 0, 0)


def half_sums(panel, level):
    count = panel.shape[0]
    size = 2 ** (level + 1)
    rows = count * N // size
    names = axes(0, level + 1)
    pieces = exchange(panel.reshape(size, rows, N), names)
    sums = pieces.reshape(2, size // 2, rows, N).sum(axis=1)
    both = exchange(jnp.broadcast_to(sums[None], (size, 2, rows, N)), names)
    return both[:, 0].reshape(count, N, N), both[:, 1].reshape(count, N, N)


def total(panel, level):
    count = panel.shape[0]
    size = 2**level
    rows = count * N // size
    names = axes(0, level)
    pieces = exchange(panel.reshape(size, rows, N), names)
    part = pieces.sum(axis=0)
    return exchange(jnp.broadcast_to(part[None], (size, rows, N)), names).reshape(count, N, N)


def per_device(diag_blocks, left_bases, right_bases, sources):
    levels = left_bases.shape[0]
    targets = levels + 1
    work, panel = call(leaf_kernel, "leaf", (blocks(targets), blocks(targets)), diag_blocks, left_bases, right_bases[0], sources)
    for level in range(TOP):
        count = targets - level
        if level == 0:
            own, other = panel, partner(panel, 0)
        else:
            lower, upper = half_sums(panel, level)
            is_lower = lax.axis_index("b%d" % level) == 0
            own = jnp.where(is_lower, lower, upper)
            other = jnp.where(is_lower, upper, lower)
        rows = 1 if level + 1 < TOP else levels - TOP

        def body(*refs, level=level, count=count):
            level_kernel(level, count, *refs)

        work, panel = call(
            body,
            "level%d" % level,
            (blocks(targets), blocks(rows * (count - 1))),
            own,
            other,
            work,
            right_bases[level + 1 : level + 1 + rows],
        )
    front = total(panel, TOP)
    for level in range(TOP, levels):
        count = targets - level
        other = partner(front, level)
        if level + 1 < levels:

            def body(*refs, count=count):
                front_kernel(count, *refs)

            coef, front = call(body, "front%d" % level, (blocks(count - 1), blocks((count - 2) * (count - 1))), front, other)
        else:

            def body(*refs, count=count):
                last_front_kernel(count, *refs)

            coef = call(body, "front%d" % level, blocks(1), front, other)

        def apply(*refs, level=level, count=count):
            apply_kernel(level, count, *refs)

        work = call(apply, "apply%d" % level, blocks(targets), work, coef, scratch=False)
    return work[:levels], work[levels]


def solution(mesh):
    fine = Mesh(mesh.devices.reshape((2,) * BITS), NAMES)
    rows = P(NAMES, None)
    stacked = P(None, NAMES, None)
    return jax.shard_map(
        per_device,
        mesh=fine,
        in_specs=(rows, stacked, stacked, rows),
        out_specs=(stacked, rows),
        check_vma=False,
    )
```

time: 992 us -> 437 us (0.44)
  waiting for transfers between devices: 480 us -> 143 us
  other arithmetic: 267 us -> 4.29 us
  blocking collectives: 0 us -> 154 us
  starting transfers between devices: 155 us -> 36.6 us
  Pallas kernels: 0 us -> 81 us
  matrix products: 62 us -> 0 us
    ppermute x45 -> x5, waiting for transfers between devices: 480 us -> 47.7 us  [partner(): return lax.ppermute(value, 'b%d' % bit, [(0, 1), (1, 0)])]
    another operation x50 -> x0, other arithmetic: 247 us -> none  [the longest x27 121 us: per_device(): chol = jnp.linalg.cholesky(normal)]
    all_to_all x0 -> x6, blocking collectives: none -> 154 us  [exchange(): return lax.all_to_all(value, names, 0, 0)]
    ppermute x45 -> x5, starting transfers between devices: 155 us -> 20.9 us  [partner(): return lax.ppermute(value, 'b%d' % bit, [(0, 1), (1, 0)])]
    all_to_all x0 -> x4, waiting for transfers between devices: none -> 95.5 us  [exchange(): return lax.all_to_all(value, names, 0, 0)]
    pallas_call x0 -> x14, Pallas kernels: none -> 81 us  [call(): pl.pallas_call(body, out_shape=outs, scratch_shapes=[pltpu.VMEM((N, N), j...]
    dot_general x63 -> x0, matrix products: 51.8 us -> none  [the longest x9 14.9 us: per_device(): jnp.einsum('nr,nc->rc', right_bases[level], solved[:, start:], precision=HI)]
    all_to_all x0 -> x4, starting transfers between devices: none -> 15.7 us  [exchange(): return lax.all_to_all(value, names, 0, 0)]
  transfers between devices with their start and end apart: 45 -> 9, of which waited for: 45 -> 8; matrix products, arithmetic and copies ran while one was open for 0% -> 0% of each run, Pallas kernels for 0% -> 2%
where the time goes in v1:
time: 437 us; the launch traced here: 436 us
  blocking collectives  154 us (35%)
  waiting for transfers between devices  143 us (33%)
  Pallas kernels  81 us (19%)
  starting transfers between devices  36.6 us (8%)
  local copies, waits for them, and re-layouts  15.2 us (3%)
    all_to_all x6, blocking collectives, exchange(): return lax.all_to_all(value, names, 0, 0)  154 us
    all_to_all x4, waiting for transfers between devices, exchange(): return lax.all_to_all(value, names, 0, 0)  95.5 us
    pallas_call x14, Pallas kernels, call(): pl.pallas_call(body, out_shape=outs, scratch_shapes=[pltpu.VMEM((N, N), j...  81 us
    ppermute x5, waiting for transfers between devices, partner(): return lax.ppermute(value, 'b%d' % bit, [(0, 1), (1, 0)])  47.7 us
    ppermute x5, starting transfers between devices, partner(): return lax.ppermute(value, 'b%d' % bit, [(0, 1), (1, 0)])  20.9 us
    all_to_all x4, starting transfers between devices, exchange(): return lax.all_to_all(value, names, 0, 0)  15.7 us
  transfers between devices with their start and end apart: 9, of which 8 were waited for; matrix products, arithmetic and copies ran while one was open for 0% of the time, Pallas kernels for 2%

profile of v1, /device:TPU:6, one launch (start us, length us, event | category | flops | bytes accessed | tf_op | source)
XLA Modules:
  0.0 435.7 jit_solution(10741321582419790209)
XLA Ops:
  2.3 5.6 %leaf.1 = (f32[10,128,128]{2,1,0:T(8,128)}, f32[10,128,128]{2,1,0:T(8,128)}) custom-call(f32[128,128]{1,0:T(8,128)} %diag_ref.1, f32[9,128,128]{2,1,0:T(8,128)} %left_ref.1, f32[128,128]{1,0:T(8,128)} %get-tuple-element.50.right_ref, f32[128,128]{1,0:T(8,128)} %source_ref.1), custom_call_target="tpu_custom_call" | custom-call | tf_op jit(solution)/shard_map/leaf/pallas_call | solution.py:145
  11.3 15.1 %collective-permute-done.refs_1_ = f32[10,128,128]{2,1,0:T(8,128)S(1)} collective-permute-done((f32[10,128,128]{2,1,0:T(8,128)}, f32[10,128,128]{2,1,0:T(8,128)S(1)}, u32[]{:S(2)}, u32[]{:S(2)}) %collective-permute-start) | collective-permute-done | bytes 655392 | tf_op jit(solution)/shard_map/ppermute | solution.py:154
  27.3 12.3 %level0.1 = (f32[10,128,128]{2,1,0:T(8,128)}, f32[9,128,128]{2,1,0:T(8,128)}) custom-call(f32[10,128,128]{2,1,0:T(8,128)} %get-tuple-element.20.refs_0_, f32[10,128,128]{2,1,0:T(8,128)} %copy-done.3, f32[10,128,128]{2,1,0:T(8,128)} %get-tuple-element.21.refs_2_, f32[1,128,128]{2,1,0:T(8,128)} %get-tuple-element.49.refs_3_), custom_call_target="tpu_custom_call" | custom-call | tf_op jit(solution)/shard_map/level0/pallas_call | solution.py:145
  39.6 19.9 %all_to_all.50 = f32[4,288,128]{2,1,0:T(8,128)S(1)} all-to-all(f32[4,288,128]{2,1,0:T(8,128)} %bitcast.48), channel_id=1, replica_groups=mesh['b8'=2,'b7'=2,'b6'=2,'b5'=2,'b4'=2,'b3'=2,'b2'=2,'b1'=2,'b0'=2] {'b..., dimensions={0} | all-to-all | bytes 1179648 | tf_op jit(solution)/shard_map/all_to_all | solution.py:158
  64.2 27.8 %all-to-all-done.1 = f32[4,2,288,128]{3,2,1,0:T(8,128)S(1)} async-done(((f32[4,2,288,128]{3,2,1,0:T(8,128)}), f32[4,2,288,128]{3,2,1,0:T(8,128)S(1)}, u32[]{:S(2)}, u32[]{:S(2)}) %all-to-all-start.1) | async-done | bytes 1179680 | tf_op jit(solution)/shard_map/all_to_all | solution.py:158
  93.1 7.1 %level1.1 = (f32[10,128,128]{2,1,0:T(8,128)}, f32[8,128,128]{2,1,0:T(8,128)}) custom-call(f32[9,128,128]{2,1,0:T(8,128)} %bitcast.42, f32[9,128,128]{2,1,0:T(8,128)} %bitcast.41, f32[10,128,128]{2,1,0:T(8,128)} %get-tuple-element.23.refs_2_, f32[1,128,128]{2,1,0:T(8,128)} %get-tuple-element.48.refs_3_), custom_call_target="tpu_custom_call" | custom-call | tf_op jit(solution)/shard_map/level1/pallas_call | solution.py:145
  100.3 22.7 %all_to_all.51 = f32[8,128,128]{2,1,0:T(8,128)S(1)} all-to-all(f32[8,128,128]{2,1,0:T(8,128)} %get-tuple-element.24), channel_id=1, replica_groups=mesh['b8'=2,'b7'=2,'b6'=2,'b5'=2,'b4'=2,'b3'=2,'b2'=2,'b1'=2,'b0'=2] {'b..., dimensions={0} | all-to-all | bytes 1048576 | tf_op jit(solution)/shard_map/all_to_all | solution.py:158
  127.7 26.3 %all-to-all-done.3 = f32[8,2,128,128]{3,2,1,0:T(8,128)S(1)} async-done(((f32[8,2,128,128]{3,2,1,0:T(8,128)}), f32[8,2,128,128]{3,2,1,0:T(8,128)S(1)}, u32[]{:S(2)}, u32[]{:S(2)}) %all-to-all-start.3) | async-done | bytes 1048608 | tf_op jit(solution)/shard_map/all_to_all | solution.py:158
  155.1 6.9 %level2.1 = (f32[10,128,128]{2,1,0:T(8,128)}, f32[7,128,128]{2,1,0:T(8,128)}) custom-call(f32[8,128,128]{2,1,0:T(8,128)} %get-tuple-element.41.refs_0_, f32[8,128,128]{2,1,0:T(8,128)} %get-tuple-element.40.refs_1_, f32[10,128,128]{2,1,0:T(8,128)} %get-tuple-element.25.refs_2_, f32[1,128,128]{2,1,0:T(8,128)} %get-tuple-element.47.refs_3_), custom_call_target="tpu_custom_call" | custom-call | tf_op jit(solution)/shard_map/level2/pallas_call | solution.py:145
  162.0 16.1 %all_to_all.52 = f32[16,56,128]{2,1,0:T(8,128)S(1)} all-to-all(f32[16,56,128]{2,1,0:T(8,128)} %bitcast.49), channel_id=1, replica_groups=mesh['b8'=2,'b7'=2,'b6'=2,'b5'=2,'b4'=2,'b3'=2,'b2'=2,'b1'=2,'b0'=2] {'b..., dimensions={0} | all-to-all | bytes 917504 | tf_op jit(solution)/shard_map/all_to_all | solution.py:158
  183.4 21.5 %all-to-all-done.5 = f32[16,2,56,128]{3,2,1,0:T(8,128)S(1)} async-done(((f32[16,2,56,128]{3,2,1,0:T(8,128)}), f32[16,2,56,128]{3,2,1,0:T(8,128)S(1)}, u32[]{:S(2)}, u32[]{:S(2)}) %all-to-all-start.5) | async-done | bytes 917536 | tf_op jit(solution)/shard_map/all_to_all | solution.py:158
  205.9 6.7 %level3.1 = (f32[10,128,128]{2,1,0:T(8,128)}, f32[6,128,128]{2,1,0:T(8,128)}) custom-call(f32[7,128,128]{2,1,0:T(8,128)} %bitcast.44, f32[7,128,128]{2,1,0:T(8,128)} %bitcast.43, f32[10,128,128]{2,1,0:T(8,128)} %get-tuple-element.27.refs_2_, f32[1,128,128]{2,1,0:T(8,128)} %get-tuple-element.46.refs_3_), custom_call_target="tpu_custom_call" | custom-call | tf_op jit(solution)/shard_map/level3/pallas_call | solution.py:145
  212.6 22.4 %all_to_all.53 = f32[32,24,128]{2,1,0:T(8,128)S(1)} all-to-all(f32[32,24,128]{2,1,0:T(8,128)} %bitcast.50), channel_id=1, replica_groups=mesh['b8'=2,'b7'=2,'b6'=2,'b5'=2,'b4'=2,'b3'=2,'b2'=2,'b1'=2,'b0'=2] {'b..., dimensions={0} | all-to-all | bytes 786432 | tf_op jit(solution)/shard_map/all_to_all | solution.py:158
  242.0 19.9 %all-to-all-done.7 = f32[32,2,24,128]{3,2,1,0:T(8,128)S(1)} async-done(((f32[32,2,24,128]{3,2,1,0:T(8,128)}), f32[32,2,24,128]{3,2,1,0:T(8,128)S(1)}, u32[]{:S(2)}, u32[]{:S(2)}) %all-to-all-start.7) | async-done | bytes 786464 | tf_op jit(solution)/shard_map/all_to_all | solution.py:158
  262.9 7.7 %level4.1 = (f32[10,128,128]{2,1,0:T(8,128)}, f32[20,128,128]{2,1,0:T(8,128)}) custom-call(f32[6,128,128]{2,1,0:T(8,128)} %bitcast.46, f32[6,128,128]{2,1,0:T(8,128)} %bitcast.45, f32[10,128,128]{2,1,0:T(8,128)} %get-tuple-element.29.refs_2_, f32[4,128,128]{2,1,0:T(8,128)} %slice.61.refs_3_), custom_call_target="tpu_custom_call" | custom-call | tf_op jit(solution)/shard_map/level4/pallas_call | solution.py:145
  270.6 36.8 %all_to_all.54 = f32[32,80,128]{2,1,0:T(8,128)S(1)} all-to-all(f32[32,80,128]{2,1,0:T(8,128)} %bitcast.47), channel_id=1, replica_groups=mesh['b8'=2,'b7'=2,'b6'=2,'b5'=2,'b4'=2,'b3'=2,'b2'=2,'b1'=2,'b0'=2] {'b..., dimensions={0} | all-to-all | bytes 2621440 | tf_op jit(solution)/shard_map/all_to_all | solution.py:158
  307.6 36.5 %all_to_all.55 = f32[32,80,128]{2,1,0:T(8,128)S(1)} all-to-all(f32[32,80,128]{2,1,0:T(8,128)S(1)} %broadcast_in_dim.14), channel_id=1, replica_groups=mesh['b8'=2,'b7'=2,'b6'=2,'b5'=2,'b4'=2,'b3'=2,'b2'=2,'b1'=2,'b0'=2] {'b..., dimensions={0} | all-to-all | bytes 2621440 | tf_op jit(solution)/shard_map/all_to_all | solution.py:158
  350.1 7.8 %front5.1 = (f32[4,128,128]{2,1,0:T(8,128)}, f32[12,128,128]{2,1,0:T(8,128)}) custom-call(f32[20,128,128]{2,1,0:T(8,128)} %bitcast.40, f32[20,128,128]{2,1,0:T(8,128)} %copy-done.1), custom_call_target="tpu_custom_call" | custom-call | tf_op jit(solution)/shard_map/front5/pallas_call | solution.py:145
  360.6 19.0 %collective-permute-done.2.refs_1_ = f32[12,128,128]{2,1,0:T(8,128)S(1)} collective-permute-done((f32[12,128,128]{2,1,0:T(8,128)}, f32[12,128,128]{2,1,0:T(8,128)S(1)}, u32[]{:S(2)}, u32[]{:S(2)}) %collective-permute-start.2) | collective-permute-done | bytes 786464 | tf_op jit(solution)/shard_map/ppermute | solution.py:154
  380.5 6.9 %front6.1 = (f32[3,128,128]{2,1,0:T(8,128)}, f32[6,128,128]{2,1,0:T(8,128)}) custom-call(f32[12,128,128]{2,1,0:T(8,128)} %get-tuple-element.33.refs_0_, f32[12,128,128]{2,1,0:T(8,128)} %copy-done.2), custom_call_target="tpu_custom_call" | custom-call | tf_op jit(solution)/shard_map/front6/pallas_call | solution.py:145
  390.6 10.6 %collective-permute-done.3.refs_1_ = f32[6,128,128]{2,1,0:T(8,128)S(1)} collective-permute-done((f32[6,128,128]{2,1,0:T(8,128)}, f32[6,128,128]{2,1,0:T(8,128)S(1)}, u32[]{:S(2)}, u32[]{:S(2)}) %collective-permute-start.3) | collective-permute-done | bytes 393248 | tf_op jit(solution)/shard_map/ppermute | solution.py:154
  402.0 5.9 %front7.1 = (f32[2,128,128]{2,1,0:T(8,128)}, f32[2,128,128]{2,1,0:T(8,128)}) custom-call(f32[6,128,128]{2,1,0:T(8,128)} %get-tuple-element.35.refs_0_, f32[6,128,128]{2,1,0:T(8,128)} %copy-done.4), custom_call_target="tpu_custom_call" | custom-call | tf_op jit(solution)/shard_map/front7/pallas_call | solution.py:145
  408.0 9.6 %collective-permute-start.4 = (f32[2,128,128]{2,1,0:T(8,128)}, f32[2,128,128]{2,1,0:T(8,128)S(1)}, u32[]{:S(2)}, u32[]{:S(2)}) collective-permute-start(f32[2,128,128]{2,1,0:T(8,128)} %get-tuple-element.37.refs_0_), channel_id=1, source_target_pairs={{0,256},{256,0},{1,257},{257,1},{2,258},{258,2},{3,259},{259,3},{4... | collective-permute-start | bytes 393224 | tf_op jit(solution)/shard_map/ppermute | solution.py:154
  425.1 5.0 %front8.1.refs_1_ = f32[1,128,128]{2,1,0:T(8,128)} custom-call(f32[2,128,128]{2,1,0:T(8,128)} %get-tuple-element.37.refs_0_, f32[2,128,128]{2,1,0:T(8,128)} %copy-done.5), custom_call_target="tpu_custom_call" | custom-call | tf_op jit(solution)/shard_map/front8/pallas_call | solution.py:145
  (44 shorter events, 58.5 us)
Async XLA Ops:
  7.9 18.6 %collective-permute-start = (f32[10,128,128]{2,1,0:T(8,128)}, f32[10,128,128]{2,1,0:T(8,128)S(1)}, u32[]{:S(2)}, u32[]{:S(2)}) collective-permute-start(f32[10,128,128]{2,1,0:T(8,128)} %get-tuple-element.20.refs_0_), channel_id=1, source_target_pairs={{0,1},{1,0},{2,3},{3,2},{4,5},{5,4},{6,7},{7,6},{8,9},{9,8},{10,11... | collective-permute-start | bytes 1966088 | tf_op jit(solution)/shard_map/ppermute | solution.py:154
  26.4 0.8 copy-start.3
  60.7 31.3 %all-to-all-start.1 = ((f32[4,2,288,128]{3,2,1,0:T(8,128)}), f32[4,2,288,128]{3,2,1,0:T(8,128)S(1)}, u32[]{:S(2)}, u32[]{:S(2)}) async-start(f32[4,2,288,128]{3,2,1,0:T(8,128)} %broadcast_in_dim.10), calls=%async_computation.1 | async-start | bytes 2359296 | tf_op jit(solution)/shard_map/all_to_all | solution.py:158
  124.1 29.9 %all-to-all-start.3 = ((f32[8,2,128,128]{3,2,1,0:T(8,128)}), f32[8,2,128,128]{3,2,1,0:T(8,128)S(1)}, u32[]{:S(2)}, u32[]{:S(2)}) async-start(f32[8,2,128,128]{3,2,1,0:T(8,128)} %broadcast_in_dim.11), calls=%async_computation.3 | async-start | bytes 2097152 | tf_op jit(solution)/shard_map/all_to_all | solution.py:158
  179.1 25.8 %all-to-all-start.5 = ((f32[16,2,56,128]{3,2,1,0:T(8,128)}), f32[16,2,56,128]{3,2,1,0:T(8,128)S(1)}, u32[]{:S(2)}, u32[]{:S(2)}) async-start(f32[16,2,56,128]{3,2,1,0:T(8,128)} %broadcast_in_dim.12), calls=%async_computation.5 | async-start | bytes 1835008 | tf_op jit(solution)/shard_map/all_to_all | solution.py:158
  236.0 25.9 %all-to-all-start.7 = ((f32[32,2,24,128]{3,2,1,0:T(8,128)}), f32[32,2,24,128]{3,2,1,0:T(8,128)S(1)}, u32[]{:S(2)}, u32[]{:S(2)}) async-start(f32[32,2,24,128]{3,2,1,0:T(8,128)} %broadcast_in_dim.13), calls=%async_computation.7 | async-start | bytes 1572864 | tf_op jit(solution)/shard_map/all_to_all | solution.py:158
  344.1 4.9 %copy-start = (f32[32,80,128]{2,1,0:T(8,128)}, f32[32,80,128]{2,1,0:T(8,128)S(1)}, u32[]{:S(2)}) copy-start(f32[32,80,128]{2,1,0:T(8,128)S(1)} %all_to_all.55) | copy-start | bytes 3932164
  344.1 4.9 %collective-permute-start.1 = (f32[20,128,128]{2,1,0:T(8,128)S(1)}, f32[20,128,128]{2,1,0:T(8,128)S(1)}, u32[]{:S(2)}, u32[]{:S(2)}) collective-permute-start(f32[20,128,128]{2,1,0:T(8,128)S(1)} %bitcast.39), channel_id=1, source_target_pairs={{0,32},{32,0},{1,33},{33,1},{2,34},{34,2},{3,35},{35,3},{4,36},{36... | collective-permute-start | bytes 3932168 | tf_op jit(solution)/shard_map/ppermute | solution.py:154
  349.0 1.1 copy-start.1
  357.9 21.7 %collective-permute-start.2 = (f32[12,128,128]{2,1,0:T(8,128)}, f32[12,128,128]{2,1,0:T(8,128)S(1)}, u32[]{:S(2)}, u32[]{:S(2)}) collective-permute-start(f32[12,128,128]{2,1,0:T(8,128)} %get-tuple-element.33.refs_0_), channel_id=1, source_target_pairs={{0,64},{64,0},{1,65},{65,1},{2,66},{66,2},{3,67},{67,3},{4,68},{68... | collective-permute-start | bytes 2359304 | tf_op jit(solution)/shard_map/ppermute | solution.py:154
  379.6 0.9 copy-start.2
  387.4 13.9 %collective-permute-start.3 = (f32[6,128,128]{2,1,0:T(8,128)}, f32[6,128,128]{2,1,0:T(8,128)S(1)}, u32[]{:S(2)}, u32[]{:S(2)}) collective-permute-start(f32[6,128,128]{2,1,0:T(8,128)} %get-tuple-element.35.refs_0_), channel_id=1, source_target_pairs={{0,128},{128,0},{1,129},{129,1},{2,130},{130,2},{3,131},{131,3},{4... | collective-permute-start | bytes 1179656 | tf_op jit(solution)/shard_map/ppermute | solution.py:154
  401.3 0.8 copy-start.4
  408.0 16.5 %collective-permute-start.4 = (f32[2,128,128]{2,1,0:T(8,128)}, f32[2,128,128]{2,1,0:T(8,128)S(1)}, u32[]{:S(2)}, u32[]{:S(2)}) collective-permute-start(f32[2,128,128]{2,1,0:T(8,128)} %get-tuple-element.37.refs_0_), channel_id=1, source_target_pairs={{0,256},{256,0},{1,257},{257,1},{2,258},{258,2},{3,259},{259,3},{4... | collective-permute-start | bytes 393224 | tf_op jit(solution)/shard_map/ppermute | solution.py:154
  424.5 0.7 copy-start.5

commit v2 on v1

v2 whole, which is shorter than its diff:
```python
import jax
import jax.numpy as jnp
from jax import lax
from jax.experimental import pallas as pl
from jax.experimental.pallas import tpu as pltpu
from jax.sharding import Mesh, PartitionSpec as P

HI = lax.Precision.HIGHEST
BITS = 9
NAMES = tuple("b%d" % bit for bit in reversed(range(BITS)))
TOP = 5
ROUNDS = (9, 7, 6, 6, 5, 5, 5, 5, 5)
N = 128


def axes(low, high):
    return tuple("b%d" % bit for bit in reversed(range(low, high)))


def dot(a, b):
    return jnp.dot(a, b, precision=HI, preferred_element_type=jnp.float32)


def tdot(a, b):
    return lax.dot_general(a, b, (((0,), (0,)), ((), ())), precision=HI, preferred_element_type=jnp.float32)


def quick(a, b):
    return jnp.dot(a.astype(jnp.bfloat16), b.astype(jnp.bfloat16), preferred_element_type=jnp.float32)


def eye():
    row = lax.broadcasted_iota(jnp.int32, (N, N), 0)
    col = lax.broadcasted_iota(jnp.int32, (N, N), 1)
    return (row == col).astype(jnp.float32)


def wide(ref, first, last):
    return jnp.concatenate([ref[i] for i in range(first, last)], axis=1)


def invert(matrix, start, rounds, out_ref):
    one = eye()
    value = start
    for _ in range(rounds):
        value = value + quick(value, one - quick(matrix, value))
    for _ in range(2):
        rest = one - dot(matrix, value)
        value = value + quick(value, rest)
    out_ref[...] = value
    left = jnp.sum(rest * rest)

    @pl.when(jnp.logical_not(left < 1e-6))
    def _():
        out_ref[...] = jnp.where(left < 0.25, value, start)

        def more(state):
            step, left = state
            return jnp.logical_and(step < 60, jnp.logical_not(left < 1e-9))

        def body(state):
            step, _ = state
            now = out_ref[...]
            rest = eye() - dot(matrix, now)
            out_ref[...] = now + dot(now, rest)
            return step + 1, jnp.sum(rest * rest)

        lax.while_loop(more, body, (jnp.int32(0), jnp.float32(1.0)))


def general_start(matrix):
    size = jnp.abs(matrix)
    by_col = jnp.max(jnp.sum(size, axis=0, keepdims=True), axis=1, keepdims=True)
    by_row = jnp.max(jnp.sum(size, axis=1, keepdims=True), axis=0, keepdims=True)
    return matrix.T * (1.9 / (by_col * by_row))


def spread(ref, base, value):
    for i in range(value.shape[1] // N):
        ref[base + i] = value[:, i * N : (i + 1) * N]


def side(blocks):
    return jnp.concatenate(blocks, axis=1)


def leaf_kernel(diag_ref, left_ref, right_ref, source_ref, work_ref, first_ref, second_ref, inv_ref):
    levels = left_ref.shape[0]
    diag = diag_ref[...]
    bound = jnp.max(jnp.sum(jnp.abs(diag), axis=0, keepdims=True), axis=1, keepdims=True)
    invert(diag, eye() * (2.0 / (1.0 + bound)), 6, inv_ref)
    rhs = jnp.concatenate([left_ref[i] for i in range(levels)] + [source_ref[...]], axis=1)
    work = dot(inv_ref[...], rhs)
    spread(work_ref, 0, work)
    spread(first_ref, 0, tdot(right_ref[0], work))
    spread(second_ref, 0, tdot(right_ref[1], work))


def own_coef(level, own, other, inv_ref):
    matrix = eye() - dot(other[0], own[0])
    invert(matrix, general_start(matrix), ROUNDS[level], inv_ref)
    right = side(other[1:]) - dot(other[0], side(own[1:]))
    return dot(inv_ref[...], right)


def advance(work_ref, coef, right_ref, next_ref, panel_ref):
    count = work_ref.shape[0]
    later = wide(work_ref, 1, count) - dot(work_ref[0], coef)
    spread(next_ref, 0, later)
    for k in range(right_ref.shape[0]):
        spread(panel_ref, k * (count - 1), tdot(right_ref[k], later))


def pair_kernel(own_ref, other_ref, work_ref, coef_ref, other_coef_ref, next_ref, inv_ref):
    count = work_ref.shape[0]
    coef = own_coef(0, [own_ref[i] for i in range(count)], [other_ref[i] for i in range(count)], inv_ref)
    coef_ref[...] = coef
    other_coef_ref[...] = wide(own_ref, 1, count) - dot(own_ref[0], coef)
    spread(next_ref, 0, wide(work_ref, 1, count) - dot(work_ref[0], coef))


def merge_kernel(flag_ref, own_ref, other_ref, coef_ref, other_coef_ref, front_ref, part_ref):
    count = own_ref.shape[0]
    total = wide(own_ref, 1, count) + wide(other_ref, 1, count)
    total = total - dot(own_ref[0], coef_ref[...]) - dot(other_ref[0], other_coef_ref[...])
    for i in range(count - 1):
        front_ref[i * N : (i + 1) * N] = total[:, i * N : (i + 1) * N]
    rows = part_ref.shape[0]
    part_ref[...] = front_ref[pl.ds(pl.multiple_of(flag_ref[0] * rows, 8), rows)]


def join(flag, mine_ref, swapped_ref, full_ref):
    rows = mine_ref.shape[0]
    full_ref[pl.ds(pl.multiple_of(flag * rows, 8), rows)] = mine_ref[...]
    full_ref[pl.ds(pl.multiple_of((1 - flag) * rows, 8), rows)] = swapped_ref[...]
    return [full_ref[i * N : (i + 1) * N] for i in range(2 * rows // N)]


def quad_kernel(flag_ref, own_ref, mine_ref, swapped_ref, work_ref, right_ref, next_ref, panel_ref, inv_ref, full_ref):
    count = work_ref.shape[0]
    own = [own_ref[i * N : (i + 1) * N] for i in range(count)]
    other = join(flag_ref[0], mine_ref, swapped_ref, full_ref)
    advance(work_ref, own_coef(1, own, other, inv_ref), right_ref, next_ref, panel_ref)


def level_kernel(level, flag_ref, both_ref, work_ref, right_ref, next_ref, panel_ref, inv_ref):
    count = work_ref.shape[0]
    half = flag_ref[level]
    own = both_ref[:, half].reshape(count, N, N)
    other = both_ref[:, 1 - half].reshape(count, N, N)
    coef = own_coef(level, [own[i] for i in range(count)], [other[i] for i in range(count)], inv_ref)
    advance(work_ref, coef, right_ref, next_ref, panel_ref)


def front_step(level, own, other, coef_ref, inv_ref):
    count = 10 - level
    coef = own_coef(level, own[:count], other[:count], inv_ref)
    spread(coef_ref, 0, coef)
    other_coef = side(own[1:count]) - dot(own[0], coef)
    merged = []
    for base in range(count, len(own), count):
        total = side(own[base + 1 : base + count]) + side(other[base + 1 : base + count])
        merged.append(total - dot(own[base], coef) - dot(other[base], other_coef))
    return merged


def core_kernel(flag_ref, own_ref, other_ref, coef_ref, front_ref, part_ref, inv_ref):
    size = own_ref.shape[0]
    merged = front_step(5, [own_ref[i] for i in range(size)], [other_ref[i] for i in range(size)], coef_ref, inv_ref)
    at = 0
    for total in merged:
        for i in range(total.shape[1] // N):
            front_ref[at * N : (at + 1) * N] = total[:, i * N : (i + 1) * N]
            at += 1
    rows = part_ref.shape[0]
    part_ref[...] = front_ref[pl.ds(pl.multiple_of(flag_ref[5] * rows, 8), rows)]


def joined_kernel(flag_ref, own_ref, mine_ref, swapped_ref, coef_ref, front_ref, inv_ref, full_ref):
    own = [own_ref[i * N : (i + 1) * N] for i in range(own_ref.shape[0] // N)]
    other = join(flag_ref[5], mine_ref, swapped_ref, full_ref)
    for k, total in enumerate(front_step(6, own, other, coef_ref, inv_ref)):
        spread(front_ref, 3 * k, total)


def front_kernel(own_ref, other_ref, coef_ref, front_ref, inv_ref):
    size = own_ref.shape[0]
    for k, total in enumerate(front_step(7, [own_ref[i] for i in range(size)], [other_ref[i] for i in range(size)], coef_ref, inv_ref)):
        spread(front_ref, 2 * k, total)


def last_kernel(own_ref, other_ref, work_ref, out_ref, inv_ref):
    coef = own_coef(8, [own_ref[0], own_ref[1]], [other_ref[0], other_ref[1]], inv_ref)
    out_ref[...] = work_ref[1] - dot(work_ref[0], coef)


def apply_kernel(work_ref, coef_ref, next_ref):
    count = work_ref.shape[0]
    spread(next_ref, 0, wide(work_ref, 1, count) - dot(work_ref[0], wide(coef_ref, 0, count - 1)))


def blocks(count):
    return jax.ShapeDtypeStruct((count, N, N), jnp.float32)


def flat(rows, cols=N):
    return jax.ShapeDtypeStruct((rows, cols), jnp.float32)


def call(body, name, outs, *args, flags=None, full=0, inverse=True):
    scratch = [pltpu.VMEM((N, N), jnp.float32)] if inverse else []
    if full:
        scratch.append(pltpu.VMEM((full, N), jnp.float32))
    specs = [pl.BlockSpec(memory_space=pltpu.VMEM) for _ in args]
    if flags is not None:
        specs = [pl.BlockSpec(memory_space=pltpu.SMEM)] + specs
        args = (flags,) + args
    return pl.pallas_call(body, out_shape=outs, in_specs=specs, scratch_shapes=scratch, name=name)(*args)


def partner(value, bit):
    return lax.ppermute(value, "b%d" % bit, [(0, 1), (1, 0)])


def exchange(value, names):
    return lax.all_to_all(value, names, 0, 0)


def tie(*values):
    return lax.optimization_barrier(values)


def half_sums(panel, level):
    size = 2 ** (level + 1)
    rows = panel.shape[0] * N // size
    names = axes(0, level + 1)
    pieces = exchange(panel.reshape(size, rows, N), names)
    sums = pieces.reshape(2, size // 2, rows, N).sum(axis=1)
    return exchange(jnp.broadcast_to(sums[None], (size, 2, rows, N)), names)


def total(panel, level):
    count = panel.shape[0]
    size = 2**level
    rows = count * N // size
    names = axes(0, level)
    pieces = exchange(panel.reshape(size, rows, N), names)
    part = pieces.sum(axis=0)
    return exchange(jnp.broadcast_to(part[None], (size, rows, N)), names).reshape(count, N, N)


def per_device(diag_blocks, left_bases, right_bases, sources):
    levels = left_bases.shape[0]
    targets = levels + 1
    flags = jnp.stack([lax.axis_index("b%d" % bit) for bit in range(BITS)]).astype(jnp.int32)
    done = []

    work, first, second = call(leaf_kernel, "leaf", (blocks(10), blocks(10), blocks(10)), diag_blocks, left_bases, right_bases[:2], sources)
    first_other = partner(first, 0)
    second_other = partner(second, 0)
    done.append(work[0])
    coef, other_coef, work = call(pair_kernel, "pair", (flat(N, 9 * N), flat(N, 9 * N), blocks(9)), first, first_other, work)
    front, part = call(merge_kernel, "merge", (flat(9 * N), flat(9 * N // 2)), second, second_other, coef, other_coef, flags=flags, inverse=False)
    mine = partner(part, 1)
    swapped = partner(mine, 0)
    done.append(work[0])
    work, panel = call(quad_kernel, "quad", (blocks(8), blocks(8)), front, mine, swapped, work, right_bases[2:3], flags=flags, full=9 * N)

    for level in range(2, TOP):
        count = targets - level
        both = half_sums(panel, level)
        rows = 1 if level + 1 < TOP else levels - TOP

        def body(*refs, level=level):
            level_kernel(level, *refs)

        done.append(work[0])
        work, panel = call(
            body,
            "level%d" % level,
            (blocks(count - 1), blocks(rows * (count - 1))),
            both,
            work,
            right_bases[level + 1 : level + 1 + rows],
            flags=flags,
        )

    front = total(panel, TOP)
    other = partner(front, 5)
    done.append(work[0])
    coef, front, part = call(core_kernel, "front5", (blocks(4), flat(12 * N), flat(6 * N)), front, other, flags=flags)
    mine = partner(part, 6)
    work = call(apply_kernel, "apply5", blocks(4), work, coef, inverse=False)
    done.append(work[0])
    mine, work = tie(mine, work)
    swapped = partner(mine, 5)
    coef, front = call(joined_kernel, "front6", (blocks(3), blocks(6)), front, mine, swapped, flags=flags, full=12 * N)
    other = partner(front, 7)
    work = call(apply_kernel, "apply6", blocks(3), work, coef, inverse=False)
    done.append(work[0])
    other, work = tie(other, work)
    coef, front = call(front_kernel, "front7", (blocks(2), blocks(2)), front, other)
    other = partner(front, 8)
    work = call(apply_kernel, "apply7", blocks(2), work, coef, inverse=False)
    done.append(work[0])
    updated = jnp.stack(done)
    other, work, updated = tie(other, work, updated)
    out = call(last_kernel, "front8", flat(N), front, other, work)
    return updated, out


def solution(mesh):
    fine = Mesh(mesh.devices.reshape((2,) * BITS), NAMES)
    rows = P(NAMES, None)
    stacked = P(None, NAMES, None)
    return jax.shard_map(
        per_device,
        mesh=fine,
        in_specs=(rows, stacked, stacked, rows),
        out_specs=(stacked, rows),
        check_vma=False,
    )
```

time: 437 us -> 406 us (0.929)
  waiting for transfers between devices: 143 us -> 76.1 us
  blocking collectives: 154 us -> 197 us
  Pallas kernels: 81 us -> 75.2 us
    all_to_all x4 -> x1, waiting for transfers between devices: 95.5 us -> 21.9 us  [exchange(): return lax.all_to_all(value, names, 0, 0)]
    all_to_all x6 -> x7, blocking collectives: 154 us -> 197 us  [exchange(): return lax.all_to_all(value, names, 0, 0)]
    all_to_all x4 -> x1, starting transfers between devices: 15.7 us -> 4.54 us  [exchange(): return lax.all_to_all(value, names, 0, 0)]
    unnamed x12 -> x34, local copies, waits for them, and re-layouts: 4.21 us -> 13.3 us
    ppermute x5 -> x9, starting transfers between devices: 20.9 us -> 29.6 us  [partner(): return lax.ppermute(value, 'b%d' % bit, [(0, 1), (1, 0)])]
    ppermute x5 -> x9, waiting for transfers between devices: 47.7 us -> 54.2 us  [partner(): return lax.ppermute(value, 'b%d' % bit, [(0, 1), (1, 0)])]
    pallas_call x14, Pallas kernels: 81 us -> 75.2 us  [call(): pl.pallas_call(body, out_shape=outs, in_specs=specs, scratch_shapes=scrat...]
  transfers between devices with their start and end apart: 9 -> 10, of which waited for: 8 -> 9; matrix products, arithmetic and copies ran while one was open for 0% -> 2% of each run, Pallas kernels for 2% -> 3%
where the time goes in v2:
time: 406 us; the launch traced here: 403 us
  blocking collectives  197 us (49%)
  waiting for transfers between devices  76.1 us (19%)
  Pallas kernels  75.2 us (19%)
  starting transfers between devices  34.2 us (8%)
  local copies, waits for them, and re-layouts  18.9 us (5%)
    all_to_all x7, blocking collectives, exchange(): return lax.all_to_all(value, names, 0, 0)  197 us
    pallas_call x14, Pallas kernels, call(): pl.pallas_call(body, out_shape=outs, in_specs=specs, scratch_shapes=scrat...  75.2 us
    ppermute x9, waiting for transfers between devices, partner(): return lax.ppermute(value, 'b%d' % bit, [(0, 1), (1, 0)])  54.2 us
    ppermute x9, starting transfers between devices, partner(): return lax.ppermute(value, 'b%d' % bit, [(0, 1), (1, 0)])  29.6 us
    all_to_all x1, waiting for transfers between devices, exchange(): return lax.all_to_all(value, names, 0, 0)  21.9 us
    unnamed x34, local copies, waits for them, and re-layouts  13.3 us
  transfers between devices with their start and end apart: 10, of which 9 were waited for; matrix products, arithmetic and copies ran while one was open for 2% of the time, Pallas kernels for 3%

profile of v2, /device:TPU:6, one launch (start us, length us, event | category | flops | bytes accessed | tf_op | source)
XLA Modules:
  0.0 402.8 jit_solution(16913469171370435019)
XLA Ops:
  2.2 6.1 %leaf.1 = (f32[10,128,128]{2,1,0:T(8,128)}, f32[10,128,128]{2,1,0:T(8,128)}, f32[10,128,128]{2,1,0:T(8,128)}) custom-call(f32[128,128]{1,0:T(8,128)} %diag_ref.1, f32[9,128,128]{2,1,0:T(8,128)} %left_ref.1, f32[2,128,128]{2,1,0:T(8,128)} %slice.42.right_ref, f32[128,128]{1,0:T(8,128)} %source_ref.1), custom_call_target="tpu_custom_call" | custom-call | tf_op jit(solution)/shard_map/leaf/pallas_call | solution.py:218
  14.9 13.2 %collective-permute-done.1.other_ref = f32[10,128,128]{2,1,0:T(8,128)S(1)} collective-permute-done((f32[10,128,128]{2,1,0:T(8,128)}, f32[10,128,128]{2,1,0:T(8,128)S(1)}, u32[]{:S(2)}, u32[]{:S(2)}) %collective-permute-start.1) | collective-permute-done | bytes 655392 | tf_op jit(solution)/shard_map/ppermute | solution.py:222
  28.9 7.9 %pair.1 = (f32[128,1152]{1,0:T(8,128)}, f32[128,1152]{1,0:T(8,128)}, f32[9,128,128]{2,1,0:T(8,128)}) custom-call(f32[10,128,128]{2,1,0:T(8,128)} %get-tuple-element.33.own_ref, f32[10,128,128]{2,1,0:T(8,128)} %copy-done.4, f32[10,128,128]{2,1,0:T(8,128)} %get-tuple-element.34.work_ref), custom_call_target="tpu_custom_call" | custom-call | tf_op jit(solution)/shard_map/pair/pallas_call | solution.py:218
  50.0 12.7 %collective-permute-done.2.mine_ref = f32[576,128]{1,0:T(8,128)S(1)} collective-permute-done((f32[576,128]{1,0:T(8,128)}, f32[576,128]{1,0:T(8,128)S(1)}, u32[]{:S(2)}, u32[]{:S(2)}) %collective-permute-start.2) | collective-permute-done | bytes 294944 | tf_op jit(solution)/shard_map/ppermute | solution.py:222
  66.0 6.5 %collective-permute-done.3.swapped_ref = f32[576,128]{1,0:T(8,128)S(1)} collective-permute-done((f32[576,128]{1,0:T(8,128)S(1)}, f32[576,128]{1,0:T(8,128)S(1)}, u32[]{:S(2)}, u32[]{:S(2)}) %collective-permute-start.3) | collective-permute-done | bytes 294944 | tf_op jit(solution)/shard_map/ppermute | solution.py:222
  73.3 7.1 %quad.1 = (f32[8,128,128]{2,1,0:T(8,128)}, f32[8,128,128]{2,1,0:T(8,128)}) custom-call(s32[9]{0:T(128)} %stack.42.flag_ref.refs_0_, f32[1152,128]{1,0:T(8,128)} %get-tuple-element.37.own_ref, f32[576,128]{1,0:T(8,128)} %copy-done.9, f32[576,128]{1,0:T(8,128)} %copy-done.10, f32[9,128,128]{2,1,0:T(8,128)} %get-tuple-element.39.work_ref, ...), custom_call_target="tpu_custom_call" | custom-call | tf_op jit(solution)/shard_map/quad/pallas_call | solution.py:218
  80.3 24.6 %all_to_all.40 = f32[8,128,128]{2,1,0:T(8,128)S(1)} all-to-all(f32[8,128,128]{2,1,0:T(8,128)} %get-tuple-element.40), channel_id=1, replica_groups=mesh['b8'=2,'b7'=2,'b6'=2,'b5'=2,'b4'=2,'b3'=2,'b2'=2,'b1'=2,'b0'=2] {'b..., dimensions={0} | all-to-all | bytes 1048576 | tf_op jit(solution)/shard_map/all_to_all | solution.py:226
  105.1 29.5 %all_to_all.41.refs_1_ = f32[8,2,128,128]{3,2,1,0:T(8,128)} all-to-all(f32[8,2,128,128]{3,2,1,0:T(8,128)S(1)} %broadcast_in_dim.8), channel_id=1, replica_groups=mesh['b8'=2,'b7'=2,'b6'=2,'b5'=2,'b4'=2,'b3'=2,'b2'=2,'b1'=2,'b0'=2] {'b..., dimensions={0} | all-to-all | bytes 2097152 | tf_op jit(solution)/shard_map/all_to_all | solution.py:226
  134.6 6.7 %level2.1 = (f32[7,128,128]{2,1,0:T(8,128)}, f32[7,128,128]{2,1,0:T(8,128)}) custom-call(s32[9]{0:T(128)} %stack.42.flag_ref.refs_0_, f32[8,2,128,128]{3,2,1,0:T(8,128)} %all_to_all.41.refs_1_, f32[8,128,128]{2,1,0:T(8,128)} %get-tuple-element.41.refs_2_, f32[1,128,128]{2,1,0:T(8,128)} %get-tuple-element.63.refs_3_), custom_call_target="tpu_custom_call" | custom-call | tf_op jit(solution)/shard_map/level2/pallas_call | solution.py:218
  141.4 16.2 %all_to_all.42 = f32[16,56,128]{2,1,0:T(8,128)S(1)} all-to-all(f32[16,56,128]{2,1,0:T(8,128)} %bitcast.22), channel_id=1, replica_groups=mesh['b8'=2,'b7'=2,'b6'=2,'b5'=2,'b4'=2,'b3'=2,'b2'=2,'b1'=2,'b0'=2] {'b..., dimensions={0} | all-to-all | bytes 917504 | tf_op jit(solution)/shard_map/all_to_all | solution.py:226
  157.7 27.4 %all_to_all.43.refs_1_ = f32[16,2,56,128]{3,2,1,0:T(8,128)} all-to-all(f32[16,2,56,128]{3,2,1,0:T(8,128)S(1)} %broadcast_in_dim.9), channel_id=1, replica_groups=mesh['b8'=2,'b7'=2,'b6'=2,'b5'=2,'b4'=2,'b3'=2,'b2'=2,'b1'=2,'b0'=2] {'b..., dimensions={0} | all-to-all | bytes 1835008 | tf_op jit(solution)/shard_map/all_to_all | solution.py:226
  185.1 6.4 %level3.1 = (f32[6,128,128]{2,1,0:T(8,128)}, f32[6,128,128]{2,1,0:T(8,128)}) custom-call(s32[9]{0:T(128)} %stack.42.flag_ref.refs_0_, f32[16,2,56,128]{3,2,1,0:T(8,128)} %all_to_all.43.refs_1_, f32[7,128,128]{2,1,0:T(8,128)} %get-tuple-element.43.refs_2_, f32[1,128,128]{2,1,0:T(8,128)} %get-tuple-element.62.refs_3_), custom_call_target="tpu_custom_call" | custom-call | tf_op jit(solution)/shard_map/level3/pallas_call | solution.py:218
  191.4 22.4 %all_to_all.44 = f32[32,24,128]{2,1,0:T(8,128)S(1)} all-to-all(f32[32,24,128]{2,1,0:T(8,128)} %bitcast.23), channel_id=1, replica_groups=mesh['b8'=2,'b7'=2,'b6'=2,'b5'=2,'b4'=2,'b3'=2,'b2'=2,'b1'=2,'b0'=2] {'b..., dimensions={0} | all-to-all | bytes 786432 | tf_op jit(solution)/shard_map/all_to_all | solution.py:226
  220.1 21.9 %all-to-all-done.5.refs_1_ = f32[32,2,24,128]{3,2,1,0:T(8,128)S(1)} async-done(((f32[32,2,24,128]{3,2,1,0:T(8,128)}), f32[32,2,24,128]{3,2,1,0:T(8,128)S(1)}, u32[]{:S(2)}, u32[]{:S(2)}) %all-to-all-start.5) | async-done | bytes 786464 | tf_op jit(solution)/shard_map/all_to_all | solution.py:226
  242.9 7.0 %level4.1 = (f32[5,128,128]{2,1,0:T(8,128)}, f32[20,128,128]{2,1,0:T(8,128)}) custom-call(s32[9]{0:T(128)} %stack.42.flag_ref.refs_0_, f32[32,2,24,128]{3,2,1,0:T(8,128)} %copy-done.1, f32[6,128,128]{2,1,0:T(8,128)} %get-tuple-element.45.refs_2_, f32[4,128,128]{2,1,0:T(8,128)} %slice.46.refs_3_), custom_call_target="tpu_custom_call" | custom-call | tf_op jit(solution)/shard_map/level4/pallas_call | solution.py:218
  249.9 38.7 %all_to_all.45 = f32[32,80,128]{2,1,0:T(8,128)S(1)} all-to-all(f32[32,80,128]{2,1,0:T(8,128)} %bitcast.21), channel_id=1, replica_groups=mesh['b8'=2,'b7'=2,'b6'=2,'b5'=2,'b4'=2,'b3'=2,'b2'=2,'b1'=2,'b0'=2] {'b..., dimensions={0} | all-to-all | bytes 2621440 | tf_op jit(solution)/shard_map/all_to_all | solution.py:226
  288.8 38.5 %all_to_all.46 = f32[32,80,128]{2,1,0:T(8,128)S(1)} all-to-all(f32[32,80,128]{2,1,0:T(8,128)S(1)} %broadcast_in_dim.11), channel_id=1, replica_groups=mesh['b8'=2,'b7'=2,'b6'=2,'b5'=2,'b4'=2,'b3'=2,'b2'=2,'b1'=2,'b0'=2] {'b..., dimensions={0} | all-to-all | bytes 2621440 | tf_op jit(solution)/shard_map/all_to_all | solution.py:226
  333.2 7.9 %front5.1 = (f32[4,128,128]{2,1,0:T(8,128)}, f32[1536,128]{1,0:T(8,128)}, f32[768,128]{1,0:T(8,128)}) custom-call(s32[9]{0:T(128)} %stack.42.flag_ref.refs_0_, f32[20,128,128]{2,1,0:T(8,128)} %bitcast.20, f32[20,128,128]{2,1,0:T(8,128)} %copy-done.2), custom_call_target="tpu_custom_call" | custom-call | tf_op jit(solution)/shard_map/front5/pallas_call | solution.py:218
  347.7 6.7 %collective-permute-done.5.mine_ref = f32[768,128]{1,0:T(8,128)S(1)} collective-permute-done((f32[768,128]{1,0:T(8,128)}, f32[768,128]{1,0:T(8,128)S(1)}, u32[]{:S(2)}, u32[]{:S(2)}) %collective-permute-start.5) | collective-permute-done | bytes 393248 | tf_op jit(solution)/shard_map/ppermute | solution.py:222
  358.7 6.2 %front6.1 = (f32[3,128,128]{2,1,0:T(8,128)}, f32[6,128,128]{2,1,0:T(8,128)}) custom-call(s32[9]{0:T(128)} %stack.42.flag_ref.refs_0_, f32[1536,128]{1,0:T(8,128)} %get-tuple-element.47.own_ref, f32[768,128]{1,0:T(8,128)} %copy-done.7, f32[768,128]{1,0:T(8,128)} %copy-done.8), custom_call_target="tpu_custom_call" | custom-call | tf_op jit(solution)/shard_map/front6/pallas_call | solution.py:218
  372.0 8.1 %collective-permute-done.7.other_ref = f32[6,128,128]{2,1,0:T(8,128)S(1)} collective-permute-done((f32[6,128,128]{2,1,0:T(8,128)}, f32[6,128,128]{2,1,0:T(8,128)S(1)}, u32[]{:S(2)}, u32[]{:S(2)}) %collective-permute-start.7) | collective-permute-done | bytes 393248 | tf_op jit(solution)/shard_map/ppermute | solution.py:222
  380.8 5.5 %front7.1 = (f32[2,128,128]{2,1,0:T(8,128)}, f32[2,128,128]{2,1,0:T(8,128)}) custom-call(f32[6,128,128]{2,1,0:T(8,128)} %get-tuple-element.52.own_ref, f32[6,128,128]{2,1,0:T(8,128)} %copy-done.6), custom_call_target="tpu_custom_call" | custom-call | tf_op jit(solution)/shard_map/front7/pallas_call | solution.py:218
  386.3 6.8 %collective-permute-start.8 = (f32[2,128,128]{2,1,0:T(8,128)}, f32[2,128,128]{2,1,0:T(8,128)S(1)}, u32[]{:S(2)}, u32[]{:S(2)}) collective-permute-start(f32[2,128,128]{2,1,0:T(8,128)} %get-tuple-element.56.own_ref), channel_id=1, source_target_pairs={{0,256},{256,0},{1,257},{257,1},{2,258},{258,2},{3,259},{259,3},{4... | collective-permute-start | bytes 393224 | tf_op jit(solution)/shard_map/ppermute | solution.py:222
  398.1 4.7 %front8.1 = f32[128,128]{1,0:T(8,128)} custom-call(f32[2,128,128]{2,1,0:T(8,128)} %get-tuple-element.56.own_ref, f32[2,128,128]{2,1,0:T(8,128)} %copy-done.11, f32[2,128,128]{2,1,0:T(8,128)} %apply7.1.work_ref), custom_call_target="tpu_custom_call" | custom-call | tf_op jit(solution)/shard_map/front8/pallas_call | solution.py:218
  (64 shorter events, 63.3 us)
Async XLA Ops:
  8.3 19.7 %collective-permute-start.1 = (f32[10,128,128]{2,1,0:T(8,128)}, f32[10,128,128]{2,1,0:T(8,128)S(1)}, u32[]{:S(2)}, u32[]{:S(2)}) collective-permute-start(f32[10,128,128]{2,1,0:T(8,128)} %get-tuple-element.33.own_ref), channel_id=1, source_target_pairs={{0,1},{1,0},{2,3},{3,2},{4,5},{5,4},{6,7},{7,6},{8,9},{9,8},{10,11... | collective-permute-start | bytes 1966088 | tf_op jit(solution)/shard_map/ppermute | solution.py:222
  11.8 29.1 %collective-permute-start = (f32[10,128,128]{2,1,0:T(8,128)}, f32[10,128,128]{2,1,0:T(8,128)S(1)}, u32[]{:S(2)}, u32[]{:S(2)}) collective-permute-start(f32[10,128,128]{2,1,0:T(8,128)} %get-tuple-element.32.own_ref), channel_id=1, source_target_pairs={{0,1},{1,0},{2,3},{3,2},{4,5},{5,4},{6,7},{7,6},{8,9},{9,8},{10,11... | collective-permute-start | bytes 1966088 | tf_op jit(solution)/shard_map/ppermute | solution.py:222
  28.0 0.9 copy-start.4
  36.8 28.6 %copy-start.5 = (f32[9,128,128]{2,1,0:T(8,128)S(1)}, f32[9,128,128]{2,1,0:T(8,128)}, u32[]{:S(2)}) copy-start(f32[9,128,128]{2,1,0:T(8,128)} %param.6) | copy-start | bytes 1769476
  40.9 0.9 copy-start.3
  45.5 17.2 %collective-permute-start.2 = (f32[576,128]{1,0:T(8,128)}, f32[576,128]{1,0:T(8,128)S(1)}, u32[]{:S(2)}, u32[]{:S(2)}) collective-permute-start(f32[576,128]{1,0:T(8,128)} %get-tuple-element.38), channel_id=1, source_target_pairs={{0,2},{2,0},{1,3},{3,1},{4,6},{6,4},{5,7},{7,5},{8,10},{10,8},{9,1... | collective-permute-start | bytes 884744 | tf_op jit(solution)/shard_map/ppermute | solution.py:222
  62.7 9.9 %copy-start.9 = (f32[576,128]{1,0:T(8,128)}, f32[576,128]{1,0:T(8,128)S(1)}, u32[]{:S(2)}) copy-start(f32[576,128]{1,0:T(8,128)S(1)} %collective-permute-done.2.mine_ref) | copy-start | bytes 884740
  62.7 9.9 %collective-permute-start.3 = (f32[576,128]{1,0:T(8,128)S(1)}, f32[576,128]{1,0:T(8,128)S(1)}, u32[]{:S(2)}, u32[]{:S(2)}) collective-permute-start(f32[576,128]{1,0:T(8,128)S(1)} %collective-permute-done.2.mine_ref), channel_id=1, source_target_pairs={{0,1},{1,0},{2,3},{3,2},{4,5},{5,4},{6,7},{7,6},{8,9},{9,8},{10,11... | collective-permute-start | bytes 884744 | tf_op jit(solution)/shard_map/ppermute | solution.py:222
  72.5 0.7 copy-start.10
  214.8 27.2 %all-to-all-start.5 = ((f32[32,2,24,128]{3,2,1,0:T(8,128)}), f32[32,2,24,128]{3,2,1,0:T(8,128)S(1)}, u32[]{:S(2)}, u32[]{:S(2)}) async-start(f32[32,2,24,128]{3,2,1,0:T(8,128)} %broadcast_in_dim.10), calls=%async_computation.5 | async-start | bytes 1572864 | tf_op jit(solution)/shard_map/all_to_all | solution.py:226
  242.0 0.9 copy-start.1
  327.3 4.9 %copy-start = (f32[32,80,128]{2,1,0:T(8,128)}, f32[32,80,128]{2,1,0:T(8,128)S(1)}, u32[]{:S(2)}) copy-start(f32[32,80,128]{2,1,0:T(8,128)S(1)} %all_to_all.46) | copy-start | bytes 3932164
  327.3 4.9 %collective-permute-start.4 = (f32[20,128,128]{2,1,0:T(8,128)S(1)}, f32[20,128,128]{2,1,0:T(8,128)S(1)}, u32[]{:S(2)}, u32[]{:S(2)}) collective-permute-start(f32[20,128,128]{2,1,0:T(8,128)S(1)} %bitcast.19), channel_id=1, source_target_pairs={{0,32},{32,0},{1,33},{33,1},{2,34},{34,2},{3,35},{35,3},{4,36},{36... | collective-permute-start | bytes 3932168 | tf_op jit(solution)/shard_map/ppermute | solution.py:222
  332.2 1.1 copy-start.2
  341.1 13.3 %collective-permute-start.5 = (f32[768,128]{1,0:T(8,128)}, f32[768,128]{1,0:T(8,128)S(1)}, u32[]{:S(2)}, u32[]{:S(2)}) collective-permute-start(f32[768,128]{1,0:T(8,128)} %get-tuple-element.48), channel_id=1, source_target_pairs={{0,64},{64,0},{1,65},{65,1},{2,66},{66,2},{3,67},{67,3},{4,68},{68... | collective-permute-start | bytes 1179656 | tf_op jit(solution)/shard_map/ppermute | solution.py:222
  354.4 3.6 copy-start.7
  354.4 3.6 collective-permute-start.6
  358.0 0.7 copy-start.8
  365.0 15.1 %collective-permute-start.7 = (f32[6,128,128]{2,1,0:T(8,128)}, f32[6,128,128]{2,1,0:T(8,128)S(1)}, u32[]{:S(2)}, u32[]{:S(2)}) collective-permute-start(f32[6,128,128]{2,1,0:T(8,128)} %get-tuple-element.52.own_ref), channel_id=1, source_target_pairs={{0,128},{128,0},{1,129},{129,1},{2,130},{130,2},{3,131},{131,3},{4... | collective-permute-start | bytes 1179656 | tf_op jit(solution)/shard_map/ppermute | solution.py:222
  380.1 0.7 copy-start.6
  386.3 11.1 %collective-permute-start.8 = (f32[2,128,128]{2,1,0:T(8,128)}, f32[2,128,128]{2,1,0:T(8,128)S(1)}, u32[]{:S(2)}, u32[]{:S(2)}) collective-permute-start(f32[2,128,128]{2,1,0:T(8,128)} %get-tuple-element.56.own_ref), channel_id=1, source_target_pairs={{0,256},{256,0},{1,257},{257,1},{2,258},{258,2},{3,259},{259,3},{4... | collective-permute-start | bytes 393224 | tf_op jit(solution)/shard_map/ppermute | solution.py:222
  395.8 7.0 %copy-start.12 = (f32[9,128,128]{2,1,0:T(8,128)}, f32[9,128,128]{2,1,0:T(8,128)S(1)}, u32[]{:S(2)}) copy-start(f32[9,128,128]{2,1,0:T(8,128)S(1)} %slice_dynamic-update-slice_fusion) | copy-start | bytes 1769476
  397.4 0.7 copy-start.11

commit v3 on v2

v3 whole, which is shorter than its diff:
```python
import jax
import jax.numpy as jnp
from jax import lax
from jax.experimental import pallas as pl
from jax.experimental.pallas import tpu as pltpu
from jax.sharding import Mesh, PartitionSpec as P

HI = lax.Precision.HIGHEST
BITS = 9
NAMES = tuple("b%d" % bit for bit in reversed(range(BITS)))
TOP = 5
ROUNDS = (9, 7, 6, 6, 5, 5, 5, 5, 5)
N = 128


def axes(low, high):
    return tuple("b%d" % bit for bit in reversed(range(low, high)))


def dot(a, b):
    return jnp.dot(a, b, precision=HI, preferred_element_type=jnp.float32)


def tdot(a, b):
    return lax.dot_general(a, b, (((0,), (0,)), ((), ())), precision=HI, preferred_element_type=jnp.float32)


def quick(a, b):
    return jnp.dot(a.astype(jnp.bfloat16), b.astype(jnp.bfloat16), preferred_element_type=jnp.float32)


def eye():
    row = lax.broadcasted_iota(jnp.int32, (N, N), 0)
    col = lax.broadcasted_iota(jnp.int32, (N, N), 1)
    return (row == col).astype(jnp.float32)


def wide(ref, first, last):
    return jnp.concatenate([ref[i] for i in range(first, last)], axis=1)


def invert(matrix, start, rounds, out_ref):
    one = eye()
    value = start
    for _ in range(rounds):
        value = value + quick(value, one - quick(matrix, value))
    for _ in range(2):
        rest = one - dot(matrix, value)
        value = value + quick(value, rest)
    out_ref[...] = value
    left = jnp.sum(rest * rest)

    @pl.when(jnp.logical_not(left < 1e-6))
    def _():
        out_ref[...] = jnp.where(left < 0.25, value, start)

        def more(state):
            step, left = state
            return jnp.logical_and(step < 60, jnp.logical_not(left < 1e-9))

        def body(state):
            step, _ = state
            now = out_ref[...]
            rest = eye() - dot(matrix, now)
            out_ref[...] = now + dot(now, rest)
            return step + 1, jnp.sum(rest * rest)

        lax.while_loop(more, body, (jnp.int32(0), jnp.float32(1.0)))


def general_start(matrix):
    size = jnp.abs(matrix)
    by_col = jnp.max(jnp.sum(size, axis=0, keepdims=True), axis=1, keepdims=True)
    by_row = jnp.max(jnp.sum(size, axis=1, keepdims=True), axis=0, keepdims=True)
    return matrix.T * (1.9 / (by_col * by_row))


def spread(ref, base, value):
    for i in range(value.shape[1] // N):
        ref[base + i] = value[:, i * N : (i + 1) * N]


def side(blocks):
    return jnp.concatenate(blocks, axis=1)


class Fetch:
    def __init__(self, source, low, cuts, buffer, sems):
        self.buffer = buffer
        self.copies = [
            pltpu.make_async_copy(source.at[pl.ds(low + at, end - at)], buffer.at[pl.ds(at, end - at)], sems.at[i])
            for i, (at, end) in enumerate(zip(cuts[:-1], cuts[1:]))
        ]
        self.waited = 0

    def need(self, pieces=None):
        pieces = len(self.copies) if pieces is None else pieces
        while self.waited < pieces:
            self.copies[self.waited].wait()
            self.waited += 1
        return self.buffer


def call(body, name, outs, *args, flags=None, full=0, inverse=True):
    arrays, lows, cuts = [], [], []
    for arg in args:
        array, low, cut = arg if isinstance(arg, tuple) else (arg, 0, (0, arg.shape[0]))
        arrays.append(array)
        lows.append(low)
        cuts.append(cut)
    count = len(arrays)
    scratch = [pltpu.VMEM((cut[-1],) + array.shape[1:], jnp.float32) for array, cut in zip(arrays, cuts)]
    scratch += [pltpu.SemaphoreType.DMA((len(cut) - 1,)) for cut in cuts]
    if inverse:
        scratch.append(pltpu.VMEM((N, N), jnp.float32))
    if full:
        scratch.append(pltpu.VMEM((full, N), jnp.float32))
    results = outs if isinstance(outs, tuple) else (outs,)

    def kernel(*refs):
        flag_ref = None
        if flags is not None:
            flag_ref, refs = refs[0], refs[1:]
        sources, refs = refs[:count], refs[count:]
        targets, refs = refs[: len(results)], refs[len(results) :]
        buffers, sems, extra = refs[:count], refs[count : 2 * count], refs[2 * count :]
        fetches = [Fetch(*one) for one in zip(sources, lows, cuts, buffers, sems)]
        for piece in range(max(len(cut) - 1 for cut in cuts)):
            for fetch in fetches:
                if piece < len(fetch.copies):
                    fetch.copies[piece].start()
        body(flag_ref, fetches, targets, *extra)
        for fetch in fetches:
            fetch.need()

    specs = [pl.BlockSpec(memory_space=pl.ANY) for _ in arrays]
    if flags is not None:
        specs = [pl.BlockSpec(memory_space=pltpu.SMEM)] + specs
        arrays = [flags] + arrays
    return pl.pallas_call(kernel, out_shape=outs, in_specs=specs, scratch_shapes=scratch, name=name)(*arrays)


def stacked_first(array):
    return (array, 0, (0, 1, array.shape[0]))


def flat_first(array):
    return (array, 0, (0, N, array.shape[0]))


def flat_wide(ref, first, last):
    return side([ref[i * N : (i + 1) * N] for i in range(first, last)])


def put_flat(ref, base, value):
    for i in range(value.shape[1] // N):
        ref[(base + i) * N : (base + i + 1) * N] = value[:, i * N : (i + 1) * N]


def leaf_body(flag_ref, fetches, outs, inv_ref):
    diag_f, left_f, source_f, right_f = fetches
    diag = diag_f.need()[...]
    bound = jnp.max(jnp.sum(jnp.abs(diag), axis=0, keepdims=True), axis=1, keepdims=True)
    start = eye() * (2.0 / (1.0 + bound))
    left = left_f.need()
    source = source_f.need()
    right = right_f.need()
    invert(diag, start, 6, inv_ref)
    rhs = jnp.concatenate([left[i] for i in range(left.shape[0])] + [source[...]], axis=1)
    work = dot(inv_ref[...], rhs)
    spread(outs[0], 0, work)
    for k in range(right.shape[0]):
        spread(outs[1 + k], 0, tdot(right[k], work))


def solve(level, own_g, other_g, rest, inv_ref):
    matrix = eye() - dot(other_g, own_g)
    start = general_start(matrix)
    own_p, other_p = rest()
    right = other_p - dot(other_g, own_p)
    invert(matrix, start, ROUNDS[level], inv_ref)
    return own_p, dot(inv_ref[...], right)


def pair_body(flag_ref, fetches, outs, inv_ref):
    own_f, other_f, work_f = fetches
    count = work_f.buffer.shape[0]
    own_g, other_g = own_f.need(1)[0], other_f.need(1)[0]

    def rest():
        own, other = wide(own_f.need(), 1, count), wide(other_f.need(), 1, count)
        work_f.need()
        return own, other

    own_p, coef = solve(0, own_g, other_g, rest, inv_ref)
    outs[0][...] = coef
    outs[1][...] = own_p - dot(own_g, coef)
    work = work_f.buffer
    spread(outs[2], 0, wide(work, 1, count) - dot(work[0], coef))


def merge_body(flag_ref, fetches, outs):
    coef_f, other_coef_f, own_f, other_f = fetches
    coef, other_coef, own, other = (fetch.need() for fetch in fetches)
    count = own.shape[0]
    merged = wide(own, 1, count) + wide(other, 1, count) - dot(own[0], coef[...]) - dot(other[0], other_coef[...])
    put_flat(outs[0], 0, merged)
    rows = outs[1].shape[0]
    outs[1][...] = outs[0][pl.ds(pl.multiple_of(flag_ref[0] * rows, 8), rows)]


def join(flag, mine_f, swapped_f, full_ref):
    rows = mine_f.buffer.shape[0]
    full_ref[pl.ds(pl.multiple_of(flag * rows, 8), rows)] = mine_f.need()[...]
    full_ref[pl.ds(pl.multiple_of((1 - flag) * rows, 8), rows)] = swapped_f.need()[...]
    return full_ref


def quad_body(flag_ref, fetches, outs, inv_ref, full_ref):
    own_f, mine_f, swapped_f, work_f = fetches
    count = work_f.buffer.shape[0]
    other = join(flag_ref[0], mine_f, swapped_f, full_ref)
    own = own_f.need()

    def rest():
        work_f.need()
        return flat_wide(own, 1, count), flat_wide(other, 1, count)

    own_p, coef = solve(1, own[:N], other[:N], rest, inv_ref)
    outs[0][...] = coef
    outs[1][...] = own_p - dot(own[:N], coef)
    work = work_f.buffer
    spread(outs[2], 0, wide(work, 1, count) - dot(work[0], coef))


def quad_merge_body(flag_ref, fetches, outs, full_ref):
    coef_f, other_coef_f, own_f, mine_f, swapped_f = fetches
    other = join(flag_ref[0], mine_f, swapped_f, full_ref)
    own, coef, other_coef = own_f.need(), coef_f.need(), other_coef_f.need()
    count = own.shape[0] // N
    merged = flat_wide(own, 1, count) + flat_wide(other, 1, count) - dot(own[:N], coef[...]) - dot(other[:N], other_coef[...])
    put_flat(outs[0], 0, merged)
    rows = outs[1].shape[0]
    outs[1][...] = outs[0][pl.ds(pl.multiple_of((2 * flag_ref[1] + flag_ref[0]) * rows, 8), rows)]


def finish(level, own_g, other_g, panels, work_f, right_f, outs, inv_ref):
    count = work_f.buffer.shape[0]
    before = []

    def rest():
        own_p, other_p = panels()
        work, right = work_f.need(), right_f.need()
        for k in range(right.shape[0]):
            before.append(tdot(right[k], wide(work, 0, count)))
        return own_p, other_p

    _, coef = solve(level, own_g, other_g, rest, inv_ref)
    for k, product in enumerate(before):
        spread(outs[1], k * (count - 1), product[:, N:] - dot(product[:, :N], coef))
    work = work_f.buffer
    spread(outs[0], 0, wide(work, 1, count) - dot(work[0], coef))


def octet_body(flag_ref, fetches, outs, inv_ref):
    own_f, other_f, work_f, right_f = fetches
    count = work_f.buffer.shape[0]
    own_g, other_g = own_f.need(1)[:N], other_f.need(1)[:N]

    def panels():
        return flat_wide(own_f.need(), 1, count), flat_wide(other_f.need(), 1, count)

    finish(2, own_g, other_g, panels, work_f, right_f, outs, inv_ref)


def level_body(level, flag_ref, fetches, outs, inv_ref):
    both_f, work_f, right_f = fetches
    count = work_f.buffer.shape[0]
    half = flag_ref[level]
    rows = both_f.buffer.shape[2]
    lead = -(-N // rows)
    first = both_f.need(1)
    own_g = first[:lead, half].reshape(lead * rows, N)[:N]
    other_g = first[:lead, 1 - half].reshape(lead * rows, N)[:N]

    def panels():
        both = both_f.need()
        return tuple(
            side([value[i] for i in range(1, count)])
            for value in (both[:, half].reshape(count, N, N), both[:, 1 - half].reshape(count, N, N))
        )

    finish(level, own_g, other_g, panels, work_f, right_f, outs, inv_ref)


def front_step(level, own_g, other_g, own, other, coef_ref, inv_ref):
    count = 10 - level
    readers = []

    def rest():
        readers.extend([own(), other()])
        return tuple(side([read(i) for i in range(1, count)]) for read in readers)

    own_p, coef = solve(level, own_g, other_g, rest, inv_ref)
    spread(coef_ref, 0, coef)
    other_coef = own_p - dot(own_g, coef)
    mine, yours = readers
    for base in range(count, count * (count - 1), count):
        both = side([mine(base + i) + yours(base + i) for i in range(1, count)])
        yield both - dot(mine(base), coef) - dot(yours(base), other_coef)


def stacked_reader(fetch):
    ref = fetch.need()
    return lambda i: ref[i]


def core_body(flag_ref, fetches, outs, inv_ref):
    own_f, other_f = fetches
    own_g, other_g = own_f.need(1)[0], other_f.need(1)[0]
    readers = [lambda fetch=fetch: stacked_reader(fetch) for fetch in fetches]
    for k, merged in enumerate(front_step(5, own_g, other_g, *readers, outs[0], inv_ref)):
        put_flat(outs[1], 4 * k, merged)
    rows = outs[2].shape[0]
    outs[2][...] = outs[1][pl.ds(pl.multiple_of(flag_ref[5] * rows, 8), rows)]


def joined_body(flag_ref, fetches, outs, inv_ref, full_ref):
    own_f, mine_f, swapped_f = fetches
    other = join(flag_ref[5], mine_f, swapped_f, full_ref)
    own = own_f.need()
    readers = [lambda ref=ref: (lambda i: ref[i * N : (i + 1) * N]) for ref in (own, other)]
    for k, merged in enumerate(front_step(6, own[:N], other[:N], *readers, outs[0], inv_ref)):
        spread(outs[1], 3 * k, merged)


def front_body(flag_ref, fetches, outs, inv_ref):
    own_f, other_f = fetches
    own_g, other_g = own_f.need(1)[0], other_f.need(1)[0]
    readers = [lambda fetch=fetch: stacked_reader(fetch) for fetch in fetches]
    for k, merged in enumerate(front_step(7, own_g, other_g, *readers, outs[0], inv_ref)):
        spread(outs[1], 2 * k, merged)


def last_body(flag_ref, fetches, outs, inv_ref):
    own_f, other_f, work_f = fetches
    own_g, other_g = own_f.need()[0], other_f.need()[0]

    def rest():
        work_f.need()
        return own_f.buffer[1], other_f.buffer[1]

    _, coef = solve(8, own_g, other_g, rest, inv_ref)
    outs[0][...] = work_f.buffer[1] - dot(work_f.buffer[0], coef)


def apply_body(flag_ref, fetches, outs):
    work, coef = (fetch.need() for fetch in fetches)
    count = work.shape[0]
    spread(outs[0], 0, wide(work, 1, count) - dot(work[0], wide(coef, 0, count - 1)))


def blocks(count):
    return jax.ShapeDtypeStruct((count, N, N), jnp.float32)


def flat(rows, cols=N):
    return jax.ShapeDtypeStruct((rows, cols), jnp.float32)


def partner(value, bit):
    return lax.ppermute(value, "b%d" % bit, [(0, 1), (1, 0)])


def exchange(value, names):
    return lax.all_to_all(value, names, 0, 0)


def tie(*values):
    return lax.optimization_barrier(values)


def half_sums(panel, level):
    size = 2 ** (level + 1)
    rows = panel.shape[0] * N // size
    names = axes(0, level + 1)
    pieces = exchange(panel.reshape(size, rows, N), names)
    sums = pieces.reshape(2, size // 2, rows, N).sum(axis=1)
    return exchange(jnp.broadcast_to(sums[None], (size, 2, rows, N)), names)


def total(panel, level):
    count = panel.shape[0]
    size = 2**level
    rows = count * N // size
    names = axes(0, level)
    pieces = exchange(panel.reshape(size, rows, N), names)
    part = pieces.sum(axis=0)
    return exchange(jnp.broadcast_to(part[None], (size, rows, N)), names).reshape(count, N, N)


def per_device(diag_blocks, left_bases, right_bases, sources):
    levels = left_bases.shape[0]
    targets = levels + 1
    flags = jnp.stack([lax.axis_index("b%d" % bit) for bit in range(BITS)]).astype(jnp.int32)
    done = []

    def some_right(low, high):
        return (right_bases, low, (0, high - low))

    work, *panels = call(
        leaf_body, "leaf", (blocks(10), blocks(10), blocks(10), blocks(10)), diag_blocks, left_bases, sources, some_right(0, 3)
    )
    others = [partner(panel, 0) for panel in panels]
    done.append(work[0])
    coef, other_coef, work = call(
        pair_body, "pair", (flat(N, 9 * N), flat(N, 9 * N), blocks(9)), stacked_first(panels[0]), stacked_first(others[0]), work
    )
    done.append(work[0])
    fronts, mine = [], []
    for k in (1, 2):
        front, part = call(
            merge_body, "merge%d" % k, (flat(9 * N), flat(9 * N // 2)), coef, other_coef, panels[k], others[k], flags=flags, inverse=False
        )
        fronts.append(front)
        mine.append(partner(part, 1))
    swapped = [partner(part, 0) for part in mine]
    coef, other_coef, work = call(
        quad_body, "quad", (flat(N, 8 * N), flat(N, 8 * N), blocks(8)), fronts[0], mine[0], swapped[0], work, flags=flags, full=9 * N
    )
    done.append(work[0])
    front, part = call(
        quad_merge_body,
        "quadmerge",
        (flat(8 * N), flat(2 * N)),
        coef,
        other_coef,
        fronts[1],
        mine[1],
        swapped[1],
        flags=flags,
        full=9 * N,
        inverse=False,
    )
    part = partner(part, 2)
    other = exchange(jnp.broadcast_to(part[None], (4, 2 * N, N)), axes(0, 2)).reshape(8 * N, N)
    work, panel = call(
        octet_body, "octet", (blocks(7), blocks(7)), flat_first(front), flat_first(other), work, some_right(3, 4)
    )
    done.append(work[0])

    for level in range(3, TOP):
        count = targets - level
        both = half_sums(panel, level)
        size, _, piece, _ = both.shape
        rows = 1 if level + 1 < TOP else levels - TOP

        def body(*refs, level=level):
            level_body(level, *refs)

        work, panel = call(
            body,
            "level%d" % level,
            (blocks(count - 1), blocks(rows * (count - 1))),
            (both, 0, (0, -(-N // piece), size)),
            work,
            some_right(level + 1, level + 1 + rows),
            flags=flags,
        )
        done.append(work[0])

    front = total(panel, TOP)
    other = partner(front, 5)
    coef, front, part = call(
        core_body, "front5", (blocks(4), flat(12 * N), flat(6 * N)), stacked_first(front), stacked_first(other), flags=flags
    )
    mine = partner(part, 6)
    work = call(apply_body, "apply5", blocks(4), work, coef, inverse=False)
    done.append(work[0])
    mine, work = tie(mine, work)
    swapped = partner(mine, 5)
    coef, front = call(joined_body, "front6", (blocks(3), blocks(6)), front, mine, swapped, flags=flags, full=12 * N)
    other = partner(front, 7)
    work = call(apply_body, "apply6", blocks(3), work, coef, inverse=False)
    done.append(work[0])
    other, work = tie(other, work)
    coef, front = call(front_body, "front7", (blocks(2), blocks(2)), stacked_first(front), stacked_first(other))
    other = partner(front, 8)
    work = call(apply_body, "apply7", blocks(2), work, coef, inverse=False)
    done.append(work[0])
    updated = jnp.stack(done)
    other, work, updated = tie(other, work, updated)
    out = call(last_body, "front8", flat(N), front, other, work)
    return updated, out


def solution(mesh):
    fine = Mesh(mesh.devices.reshape((2,) * BITS), NAMES)
    rows = P(NAMES, None)
    stacked = P(None, NAMES, None)
    return jax.shard_map(
        per_device,
        mesh=fine,
        in_specs=(rows, stacked, stacked, rows),
        out_specs=(stacked, rows),
        check_vma=False,
    )
```

time: 406 us -> 406 us (level)
  waiting for transfers between devices: 76.1 us -> 57.1 us
  starting transfers between devices: 34.2 us -> 46.3 us
  Pallas kernels: 75.2 us -> 86.6 us
    all_to_all x1 -> x0, waiting for transfers between devices: 21.9 us -> none  [exchange(): return lax.all_to_all(value, names, 0, 0)]
    ppermute x9 -> x13, starting transfers between devices: 29.6 us -> 46.3 us  [partner(): return lax.ppermute(value, 'b%d' % bit, [(0, 1), (1, 0)])]
    pallas_call x14 -> x16, Pallas kernels: 75.2 us -> 86.6 us  [call(): pl.pallas_call(kernel, out_shape=outs, in_specs=specs, scratch_shapes=scr...]
    all_to_all x1 -> x0, starting transfers between devices: 4.54 us -> none  [exchange(): return lax.all_to_all(value, names, 0, 0)]
    ppermute x9 -> x13, waiting for transfers between devices: 54.2 us -> 57.1 us  [partner(): return lax.ppermute(value, 'b%d' % bit, [(0, 1), (1, 0)])]
    unnamed x34 -> x36, local copies, waits for them, and re-layouts: 13.3 us -> 14 us
  transfers between devices with their start and end apart: 10 -> 13, of which waited for: 9 -> 10; matrix products, arithmetic and copies ran while one was open for 2% -> 2% of each run, Pallas kernels for 3% -> 7%
where the time goes in v3:
time: 406 us; the launch traced here: 402 us
  blocking collectives  195 us (48%)
  Pallas kernels  86.6 us (21%)
  waiting for transfers between devices  57.1 us (14%)
  starting transfers between devices  46.3 us (11%)
  local copies, waits for them, and re-layouts  15.7 us (4%)
    all_to_all x7, blocking collectives, exchange(): return lax.all_to_all(value, names, 0, 0)  195 us
    pallas_call x16, Pallas kernels, call(): pl.pallas_call(kernel, out_shape=outs, in_specs=specs, scratch_shapes=scr...  86.6 us
    ppermute x13, waiting for transfers between devices, partner(): return lax.ppermute(value, 'b%d' % bit, [(0, 1), (1, 0)])  57.1 us
    ppermute x13, starting transfers between devices, partner(): return lax.ppermute(value, 'b%d' % bit, [(0, 1), (1, 0)])  46.3 us
    unnamed x36, local copies, waits for them, and re-layouts  14 us
  transfers between devices with their start and end apart: 13, of which 10 were waited for; matrix products, arithmetic and copies ran while one was open for 2% of the time, Pallas kernels for 7%

profile of v3, /device:TPU:6, one launch (start us, length us, event | category | flops | bytes accessed | tf_op | source)
XLA Modules:
  0.0 402.2 jit_solution(6276760487957559024)
XLA Ops:
  0.6 6.6 %leaf.1 = (f32[10,128,128]{2,1,0:T(8,128)}, f32[10,128,128]{2,1,0:T(8,128)}, f32[10,128,128]{2,1,0:T(8,128)}, f32[10,128,128]{2,1,0:T(8,128)}) custom-call(f32[128,128]{1,0:T(8,128)} %refs_0_.1, f32[9,128,128]{2,1,0:T(8,128)} %refs_1_.1, f32[128,128]{1,0:T(8,128)} %refs_2_.1, f32[9,128,128]{2,1,0:T(8,128)} %refs_3_.7), custom_call_target="tpu_custom_call" | custom-call | tf_op jit(solution)/shard_map/leaf/pallas_call | solution.py:140
  17.3 9.7 %collective-permute-done.refs_1_ = f32[10,128,128]{2,1,0:T(8,128)S(1)} collective-permute-done((f32[10,128,128]{2,1,0:T(8,128)}, f32[10,128,128]{2,1,0:T(8,128)S(1)}, u32[]{:S(2)}, u32[]{:S(2)}) %collective-permute-start) | collective-permute-done | bytes 655392 | tf_op jit(solution)/shard_map/ppermute | solution.py:372
  27.8 7.5 %pair.1 = (f32[128,1152]{1,0:T(8,128)}, f32[128,1152]{1,0:T(8,128)}, f32[9,128,128]{2,1,0:T(8,128)}) custom-call(f32[10,128,128]{2,1,0:T(8,128)} %get-tuple-element.38.refs_0_, f32[10,128,128]{2,1,0:T(8,128)} %copy-done.4, f32[10,128,128]{2,1,0:T(8,128)} %get-tuple-element.39.refs_2_), custom_call_target="tpu_custom_call" | custom-call | tf_op jit(solution)/shard_map/pair/pallas_call | solution.py:140
  35.3 5.7 %collective-permute-done.1.refs_4_ = f32[10,128,128]{2,1,0:T(8,128)S(1)} collective-permute-done((f32[10,128,128]{2,1,0:T(8,128)}, f32[10,128,128]{2,1,0:T(8,128)S(1)}, u32[]{:S(2)}, u32[]{:S(2)}) %collective-permute-start.1) | collective-permute-done | bytes 655392 | tf_op jit(solution)/shard_map/ppermute | solution.py:372
  50.7 9.5 %collective-permute-done.4.refs_4_ = f32[10,128,128]{2,1,0:T(8,128)S(1)} collective-permute-done((f32[10,128,128]{2,1,0:T(8,128)}, f32[10,128,128]{2,1,0:T(8,128)S(1)}, u32[]{:S(2)}, u32[]{:S(2)}) %collective-permute-start.4) | collective-permute-done | bytes 655392 | tf_op jit(solution)/shard_map/ppermute | solution.py:372
  71.2 10.6 %collective-permute-done.5.refs_4_ = f32[576,128]{1,0:T(8,128)S(1)} collective-permute-done((f32[576,128]{1,0:T(8,128)}, f32[576,128]{1,0:T(8,128)S(1)}, u32[]{:S(2)}, u32[]{:S(2)}) %collective-permute-start.5) | collective-permute-done | bytes 294944 | tf_op jit(solution)/shard_map/ppermute | solution.py:372
  84.5 7.7 %quad.1 = (f32[128,1024]{1,0:T(8,128)}, f32[128,1024]{1,0:T(8,128)}, f32[8,128,128]{2,1,0:T(8,128)}) custom-call(s32[9]{0:T(128)} %stack.42.refs_0_, f32[1152,128]{1,0:T(8,128)} %get-tuple-element.43.refs_1_, f32[576,128]{1,0:T(8,128)} %copy-done.10, f32[576,128]{1,0:T(8,128)} %copy-done.11, f32[9,128,128]{2,1,0:T(8,128)} %get-tuple-element.45.refs_4_), custom_call_target="tpu_custom_call" | custom-call | tf_op jit(solution)/shard_map/quad/pallas_call | solution.py:140
  97.5 6.5 %collective-permute-start.7 = (f32[256,128]{1,0:T(8,128)}, f32[256,128]{1,0:T(8,128)S(1)}, u32[]{:S(2)}, u32[]{:S(2)}) collective-permute-start(f32[256,128]{1,0:T(8,128)} %get-tuple-element.52), channel_id=1, source_target_pairs={{0,4},{4,0},{1,5},{5,1},{2,6},{6,2},{3,7},{7,3},{8,12},{12,8},{9,1... | collective-permute-start | bytes 393224 | tf_op jit(solution)/shard_map/ppermute | solution.py:372
  108.6 20.9 %all_to_all.35 = f32[4,256,128]{2,1,0:T(8,128)} all-to-all(f32[4,256,128]{2,1,0:T(8,128)S(1)} %broadcast_in_dim.8), channel_id=1, replica_groups=mesh['b8'=2,'b7'=2,'b6'=2,'b5'=2,'b4'=2,'b3'=2,'b2'=2,'b1'=2,'b0'=2] {'b..., dimensions={0} | all-to-all | bytes 1048576 | tf_op jit(solution)/shard_map/all_to_all | solution.py:376
  129.5 6.7 %octet.1 = (f32[7,128,128]{2,1,0:T(8,128)}, f32[7,128,128]{2,1,0:T(8,128)}) custom-call(f32[1024,128]{1,0:T(8,128)} %get-tuple-element.51.refs_0_, f32[1024,128]{1,0:T(8,128)} %bitcast.20, f32[8,128,128]{2,1,0:T(8,128)} %get-tuple-element.53.refs_2_, f32[9,128,128]{2,1,0:T(8,128)} %refs_3_.7), custom_call_target="tpu_custom_call" | custom-call | tf_op jit(solution)/shard_map/octet/pallas_call | solution.py:140
  136.2 19.6 %all_to_all.36 = f32[16,56,128]{2,1,0:T(8,128)S(1)} all-to-all(f32[16,56,128]{2,1,0:T(8,128)} %bitcast.22), channel_id=1, replica_groups=mesh['b8'=2,'b7'=2,'b6'=2,'b5'=2,'b4'=2,'b3'=2,'b2'=2,'b1'=2,'b0'=2] {'b..., dimensions={0} | all-to-all | bytes 917504 | tf_op jit(solution)/shard_map/all_to_all | solution.py:376
  155.9 27.7 %all_to_all.37.refs_1_ = f32[16,2,56,128]{3,2,1,0:T(8,128)} all-to-all(f32[16,2,56,128]{3,2,1,0:T(8,128)S(1)} %broadcast_in_dim.9), channel_id=1, replica_groups=mesh['b8'=2,'b7'=2,'b6'=2,'b5'=2,'b4'=2,'b3'=2,'b2'=2,'b1'=2,'b0'=2] {'b..., dimensions={0} | all-to-all | bytes 1835008 | tf_op jit(solution)/shard_map/all_to_all | solution.py:376
  183.6 7.1 %level3.1 = (f32[6,128,128]{2,1,0:T(8,128)}, f32[6,128,128]{2,1,0:T(8,128)}) custom-call(s32[9]{0:T(128)} %stack.42.refs_0_, f32[16,2,56,128]{3,2,1,0:T(8,128)} %all_to_all.37.refs_1_, f32[7,128,128]{2,1,0:T(8,128)} %get-tuple-element.55.refs_2_, f32[9,128,128]{2,1,0:T(8,128)} %refs_3_.7), custom_call_target="tpu_custom_call" | custom-call | tf_op jit(solution)/shard_map/level3/pallas_call | solution.py:140
  190.7 22.6 %all_to_all.38 = f32[32,24,128]{2,1,0:T(8,128)S(1)} all-to-all(f32[32,24,128]{2,1,0:T(8,128)} %bitcast.23), channel_id=1, replica_groups=mesh['b8'=2,'b7'=2,'b6'=2,'b5'=2,'b4'=2,'b3'=2,'b2'=2,'b1'=2,'b0'=2] {'b..., dimensions={0} | all-to-all | bytes 786432 | tf_op jit(solution)/shard_map/all_to_all | solution.py:376
  213.4 27.1 %all_to_all.39.refs_1_ = f32[32,2,24,128]{3,2,1,0:T(8,128)} all-to-all(f32[32,2,24,128]{3,2,1,0:T(8,128)S(1)} %broadcast_in_dim.10), channel_id=1, replica_groups=mesh['b8'=2,'b7'=2,'b6'=2,'b5'=2,'b4'=2,'b3'=2,'b2'=2,'b1'=2,'b0'=2] {'b..., dimensions={0} | all-to-all | bytes 1572864 | tf_op jit(solution)/shard_map/all_to_all | solution.py:376
  240.5 8.4 %level4.1 = (f32[5,128,128]{2,1,0:T(8,128)}, f32[20,128,128]{2,1,0:T(8,128)}) custom-call(s32[9]{0:T(128)} %stack.42.refs_0_, f32[32,2,24,128]{3,2,1,0:T(8,128)} %all_to_all.39.refs_1_, f32[6,128,128]{2,1,0:T(8,128)} %get-tuple-element.57.refs_2_, f32[9,128,128]{2,1,0:T(8,128)} %refs_3_.7), custom_call_target="tpu_custom_call" | custom-call | tf_op jit(solution)/shard_map/level4/pallas_call | solution.py:140
  248.9 38.7 %all_to_all.40 = f32[32,80,128]{2,1,0:T(8,128)S(1)} all-to-all(f32[32,80,128]{2,1,0:T(8,128)} %bitcast.21), channel_id=1, replica_groups=mesh['b8'=2,'b7'=2,'b6'=2,'b5'=2,'b4'=2,'b3'=2,'b2'=2,'b1'=2,'b0'=2] {'b..., dimensions={0} | all-to-all | bytes 2621440 | tf_op jit(solution)/shard_map/all_to_all | solution.py:376
  287.7 38.6 %all_to_all.41 = f32[32,80,128]{2,1,0:T(8,128)S(1)} all-to-all(f32[32,80,128]{2,1,0:T(8,128)S(1)} %broadcast_in_dim.11), channel_id=1, replica_groups=mesh['b8'=2,'b7'=2,'b6'=2,'b5'=2,'b4'=2,'b3'=2,'b2'=2,'b1'=2,'b0'=2] {'b..., dimensions={0} | all-to-all | bytes 2621440 | tf_op jit(solution)/shard_map/all_to_all | solution.py:376
  332.3 7.7 %front5.1 = (f32[4,128,128]{2,1,0:T(8,128)}, f32[1536,128]{1,0:T(8,128)}, f32[768,128]{1,0:T(8,128)}) custom-call(s32[9]{0:T(128)} %stack.42.refs_0_, f32[20,128,128]{2,1,0:T(8,128)} %bitcast.19, f32[20,128,128]{2,1,0:T(8,128)} %copy-done.1), custom_call_target="tpu_custom_call" | custom-call | tf_op jit(solution)/shard_map/front5/pallas_call | solution.py:140
  346.6 6.7 %collective-permute-done.9.refs_2_ = f32[768,128]{1,0:T(8,128)S(1)} collective-permute-done((f32[768,128]{1,0:T(8,128)}, f32[768,128]{1,0:T(8,128)S(1)}, u32[]{:S(2)}, u32[]{:S(2)}) %collective-permute-start.9) | collective-permute-done | bytes 393248 | tf_op jit(solution)/shard_map/ppermute | solution.py:372
  357.6 6.5 %front6.1 = (f32[3,128,128]{2,1,0:T(8,128)}, f32[6,128,128]{2,1,0:T(8,128)}) custom-call(s32[9]{0:T(128)} %stack.42.refs_0_, f32[1536,128]{1,0:T(8,128)} %get-tuple-element.59.refs_1_, f32[768,128]{1,0:T(8,128)} %copy-done.6, f32[768,128]{1,0:T(8,128)} %copy-done.7), custom_call_target="tpu_custom_call" | custom-call | tf_op jit(solution)/shard_map/front6/pallas_call | solution.py:140
  371.5 7.8 %collective-permute-done.11.refs_1_ = f32[6,128,128]{2,1,0:T(8,128)S(1)} collective-permute-done((f32[6,128,128]{2,1,0:T(8,128)}, f32[6,128,128]{2,1,0:T(8,128)S(1)}, u32[]{:S(2)}, u32[]{:S(2)}) %collective-permute-start.11) | collective-permute-done | bytes 393248 | tf_op jit(solution)/shard_map/ppermute | solution.py:372
  380.1 5.0 %front7.1 = (f32[2,128,128]{2,1,0:T(8,128)}, f32[2,128,128]{2,1,0:T(8,128)}) custom-call(f32[6,128,128]{2,1,0:T(8,128)} %get-tuple-element.64.refs_0_, f32[6,128,128]{2,1,0:T(8,128)} %copy-done.5), custom_call_target="tpu_custom_call" | custom-call | tf_op jit(solution)/shard_map/front7/pallas_call | solution.py:140
  385.1 8.2 %collective-permute-start.12 = (f32[2,128,128]{2,1,0:T(8,128)}, f32[2,128,128]{2,1,0:T(8,128)S(1)}, u32[]{:S(2)}, u32[]{:S(2)}) collective-permute-start(f32[2,128,128]{2,1,0:T(8,128)} %get-tuple-element.68.refs_0_), channel_id=1, source_target_pairs={{0,256},{256,0},{1,257},{257,1},{2,258},{258,2},{3,259},{259,3},{4... | collective-permute-start | bytes 393224 | tf_op jit(solution)/shard_map/ppermute | solution.py:372
  (70 shorter events, 78.0 us)
Async XLA Ops:
  7.2 19.7 %collective-permute-start = (f32[10,128,128]{2,1,0:T(8,128)}, f32[10,128,128]{2,1,0:T(8,128)S(1)}, u32[]{:S(2)}, u32[]{:S(2)}) collective-permute-start(f32[10,128,128]{2,1,0:T(8,128)} %get-tuple-element.38.refs_0_), channel_id=1, source_target_pairs={{0,1},{1,0},{2,3},{3,2},{4,5},{5,4},{6,7},{7,6},{8,9},{9,8},{10,11... | collective-permute-start | bytes 1966088 | tf_op jit(solution)/shard_map/ppermute | solution.py:372
  10.7 30.3 %collective-permute-start.1 = (f32[10,128,128]{2,1,0:T(8,128)}, f32[10,128,128]{2,1,0:T(8,128)S(1)}, u32[]{:S(2)}, u32[]{:S(2)}) collective-permute-start(f32[10,128,128]{2,1,0:T(8,128)} %get-tuple-element.42.refs_3_), channel_id=1, source_target_pairs={{0,1},{1,0},{2,3},{3,2},{4,5},{5,4},{6,7},{7,6},{8,9},{9,8},{10,11... | collective-permute-start | bytes 1966088 | tf_op jit(solution)/shard_map/ppermute | solution.py:372
  13.1 47.1 %collective-permute-start.4 = (f32[10,128,128]{2,1,0:T(8,128)}, f32[10,128,128]{2,1,0:T(8,128)S(1)}, u32[]{:S(2)}, u32[]{:S(2)}) collective-permute-start(f32[10,128,128]{2,1,0:T(8,128)} %get-tuple-element.48.refs_3_), channel_id=1, source_target_pairs={{0,1},{1,0},{2,3},{3,2},{4,5},{5,4},{6,7},{7,6},{8,9},{9,8},{10,11... | collective-permute-start | bytes 1966088 | tf_op jit(solution)/shard_map/ppermute | solution.py:372
  26.9 0.8 copy-start.4
  41.0 0.9 copy-start.3
  46.2 21.2 %collective-permute-start.2 = (f32[576,128]{1,0:T(8,128)}, f32[576,128]{1,0:T(8,128)S(1)}, u32[]{:S(2)}, u32[]{:S(2)}) collective-permute-start(f32[576,128]{1,0:T(8,128)} %get-tuple-element.44), channel_id=1, source_target_pairs={{0,2},{2,0},{1,3},{3,1},{4,6},{6,4},{5,7},{7,5},{8,10},{10,8},{9,1... | collective-permute-start | bytes 884744 | tf_op jit(solution)/shard_map/ppermute | solution.py:372
  60.2 0.9 copy-start.2
  65.4 16.4 %collective-permute-start.5 = (f32[576,128]{1,0:T(8,128)}, f32[576,128]{1,0:T(8,128)S(1)}, u32[]{:S(2)}, u32[]{:S(2)}) collective-permute-start(f32[576,128]{1,0:T(8,128)} %get-tuple-element.50), channel_id=1, source_target_pairs={{0,2},{2,0},{1,3},{3,1},{4,6},{6,4},{5,7},{7,5},{8,10},{10,8},{9,1... | collective-permute-start | bytes 884744 | tf_op jit(solution)/shard_map/ppermute | solution.py:372
  67.4 16.4 %copy-start.10 = (f32[576,128]{1,0:T(8,128)}, f32[576,128]{1,0:T(8,128)S(1)}, u32[]{:S(2)}) copy-start(f32[576,128]{1,0:T(8,128)S(1)} %collective-permute-done.2.refs_2_) | copy-start | bytes 884740
  67.4 16.4 %collective-permute-start.3 = (f32[576,128]{1,0:T(8,128)S(1)}, f32[576,128]{1,0:T(8,128)S(1)}, u32[]{:S(2)}, u32[]{:S(2)}) collective-permute-start(f32[576,128]{1,0:T(8,128)S(1)} %collective-permute-done.2.refs_2_), channel_id=1, source_target_pairs={{0,1},{1,0},{2,3},{3,2},{4,5},{5,4},{6,7},{7,6},{8,9},{9,8},{10,11... | collective-permute-start | bytes 884744 | tf_op jit(solution)/shard_map/ppermute | solution.py:372
  81.8 10.8 %copy-start.8 = (f32[576,128]{1,0:T(8,128)}, f32[576,128]{1,0:T(8,128)S(1)}, u32[]{:S(2)}) copy-start(f32[576,128]{1,0:T(8,128)S(1)} %collective-permute-done.5.refs_4_) | copy-start | bytes 884740
  81.8 10.8 %collective-permute-start.6 = (f32[576,128]{1,0:T(8,128)S(1)}, f32[576,128]{1,0:T(8,128)S(1)}, u32[]{:S(2)}, u32[]{:S(2)}) collective-permute-start(f32[576,128]{1,0:T(8,128)S(1)} %collective-permute-done.5.refs_4_), channel_id=1, source_target_pairs={{0,1},{1,0},{2,3},{3,2},{4,5},{5,4},{6,7},{7,6},{8,9},{9,8},{10,11... | collective-permute-start | bytes 884744 | tf_op jit(solution)/shard_map/ppermute | solution.py:372
  97.5 11.1 %collective-permute-start.7 = (f32[256,128]{1,0:T(8,128)}, f32[256,128]{1,0:T(8,128)S(1)}, u32[]{:S(2)}, u32[]{:S(2)}) collective-permute-start(f32[256,128]{1,0:T(8,128)} %get-tuple-element.52), channel_id=1, source_target_pairs={{0,4},{4,0},{1,5},{5,1},{2,6},{6,2},{3,7},{7,3},{8,12},{12,8},{9,1... | collective-permute-start | bytes 393224 | tf_op jit(solution)/shard_map/ppermute | solution.py:372
  326.3 4.9 %copy-start = (f32[32,80,128]{2,1,0:T(8,128)}, f32[32,80,128]{2,1,0:T(8,128)S(1)}, u32[]{:S(2)}) copy-start(f32[32,80,128]{2,1,0:T(8,128)S(1)} %all_to_all.41) | copy-start | bytes 3932164
  326.3 4.9 %collective-permute-start.8 = (f32[20,128,128]{2,1,0:T(8,128)S(1)}, f32[20,128,128]{2,1,0:T(8,128)S(1)}, u32[]{:S(2)}, u32[]{:S(2)}) collective-permute-start(f32[20,128,128]{2,1,0:T(8,128)S(1)} %bitcast.18), channel_id=1, source_target_pairs={{0,32},{32,0},{1,33},{33,1},{2,34},{34,2},{3,35},{35,3},{4,36},{36... | collective-permute-start | bytes 3932168 | tf_op jit(solution)/shard_map/ppermute | solution.py:372
  331.2 1.1 copy-start.1
  340.0 13.3 %collective-permute-start.9 = (f32[768,128]{1,0:T(8,128)}, f32[768,128]{1,0:T(8,128)S(1)}, u32[]{:S(2)}, u32[]{:S(2)}) collective-permute-start(f32[768,128]{1,0:T(8,128)} %get-tuple-element.60), channel_id=1, source_target_pairs={{0,64},{64,0},{1,65},{65,1},{2,66},{66,2},{3,67},{67,3},{4,68},{68... | collective-permute-start | bytes 1179656 | tf_op jit(solution)/shard_map/ppermute | solution.py:372
  353.3 3.6 copy-start.6
  353.3 3.6 collective-permute-start.10
  356.9 0.8 copy-start.7
  364.2 15.1 %collective-permute-start.11 = (f32[6,128,128]{2,1,0:T(8,128)}, f32[6,128,128]{2,1,0:T(8,128)S(1)}, u32[]{:S(2)}, u32[]{:S(2)}) collective-permute-start(f32[6,128,128]{2,1,0:T(8,128)} %get-tuple-element.64.refs_0_), channel_id=1, source_target_pairs={{0,128},{128,0},{1,129},{129,1},{2,130},{130,2},{3,131},{131,3},{4... | collective-permute-start | bytes 1179656 | tf_op jit(solution)/shard_map/ppermute | solution.py:372
  379.3 0.7 copy-start.5
  385.1 11.8 %collective-permute-start.12 = (f32[2,128,128]{2,1,0:T(8,128)}, f32[2,128,128]{2,1,0:T(8,128)S(1)}, u32[]{:S(2)}, u32[]{:S(2)}) collective-permute-start(f32[2,128,128]{2,1,0:T(8,128)} %get-tuple-element.68.refs_0_), channel_id=1, source_target_pairs={{0,256},{256,0},{1,257},{257,1},{2,258},{258,2},{3,259},{259,3},{4... | collective-permute-start | bytes 393224 | tf_op jit(solution)/shard_map/ppermute | solution.py:372
  396.1 6.0 %copy-start.13 = (f32[9,128,128]{2,1,0:T(8,128)}, f32[9,128,128]{2,1,0:T(8,128)S(1)}, u32[]{:S(2)}) copy-start(f32[9,128,128]{2,1,0:T(8,128)S(1)} %slice_dynamic-update-slice_fusion) | copy-start | bytes 1769476
  (3 other events, 2.1 us)

commit v4 on v3

--- a/solution.py
+++ b/solution.py
@@ -17,12 +17,27 @@
     return tuple("b%d" % bit for bit in reversed(range(low, high)))
 
 
+def exact(a, b):
+    return jnp.dot(a, b, precision=HI, preferred_element_type=jnp.float32)
+
+
+def parts(value):
+    high = value.astype(jnp.bfloat16)
+    return high, (value - high.astype(jnp.float32)).astype(jnp.bfloat16)
+
+
 def dot(a, b):
-    return jnp.dot(a, b, precision=HI, preferred_element_type=jnp.float32)
+    a_high, a_low = parts(a)
+    b_high, b_low = parts(b)
+
+    def one(x, y):
+        return jnp.dot(x, y, preferred_element_type=jnp.float32)
+
+    return one(a_high, b_high) + (one(a_high, b_low) + one(a_low, b_high))
 
 
 def tdot(a, b):
-    return lax.dot_general(a, b, (((0,), (0,)), ((), ())), precision=HI, preferred_element_type=jnp.float32)
+    return dot(a.T, b)
 
 
 def quick(a, b):
@@ -44,8 +59,8 @@
     value = start
     for _ in range(rounds):
         value = value + quick(value, one - quick(matrix, value))
-    for _ in range(2):
-        rest = one - dot(matrix, value)
+    for product in (dot, exact):
+        rest = one - product(matrix, value)
         value = value + quick(value, rest)
     out_ref[...] = value
     left = jnp.sum(rest * rest)
@@ -61,8 +76,8 @@
         def body(state):
             step, _ = state
             now = out_ref[...]
-            rest = eye() - dot(matrix, now)
-            out_ref[...] = now + dot(now, rest)
+            rest = eye() - exact(matrix, now)
+            out_ref[...] = now + exact(now, rest)
             return step + 1, jnp.sum(rest * rest)
 
         lax.while_loop(more, body, (jnp.int32(0), jnp.float32(1.0)))
@@ -84,33 +99,18 @@
     return jnp.concatenate(blocks, axis=1)
 
 
-class Fetch:
-    def __init__(self, source, low, cuts, buffer, sems):
-        self.buffer = buffer
-        self.copies = [
-            pltpu.make_async_copy(source.at[pl.ds(low + at, end - at)], buffer.at[pl.ds(at, end - at)], sems.at[i])
-            for i, (at, end) in enumerate(zip(cuts[:-1], cuts[1:]))
-        ]
-        self.waited = 0
+class Operand:
+    def __init__(self, ref):
+        self.buffer = ref
 
     def need(self, pieces=None):
-        pieces = len(self.copies) if pieces is None else pieces
-        while self.waited < pieces:
-            self.copies[self.waited].wait()
-            self.waited += 1
         return self.buffer
 
 
 def call(body, name, outs, *args, flags=None, full=0, inverse=True):
-    arrays, lows, cuts = [], [], []
-    for arg in args:
-        array, low, cut = arg if isinstance(arg, tuple) else (arg, 0, (0, arg.shape[0]))
-        arrays.append(array)
-        lows.append(low)
-        cuts.append(cut)
+    arrays = [pltpu.with_memory_space_constraint(arg[0] if isinstance(arg, tuple) else arg, pltpu.VMEM) for arg in args]
     count = len(arrays)
-    scratch = [pltpu.VMEM((cut[-1],) + array.shape[1:], jnp.float32) for array, cut in zip(arrays, cuts)]
-    scratch += [pltpu.SemaphoreType.DMA((len(cut) - 1,)) for cut in cuts]
+    scratch = []
     if inverse:
         scratch.append(pltpu.VMEM((N, N), jnp.float32))
     if full:
@@ -121,23 +121,22 @@
         flag_ref = None
         if flags is not None:
             flag_ref, refs = refs[0], refs[1:]
-        sources, refs = refs[:count], refs[count:]
-        targets, refs = refs[: len(results)], refs[len(results) :]
-        buffers, sems, extra = refs[:count], refs[count : 2 * count], refs[2 * count :]
-        fetches = [Fetch(*one) for one in zip(sources, lows, cuts, buffers, sems)]
-        for piece in range(max(len(cut) - 1 for cut in cuts)):
-            for fetch in fetches:
-                if piece < len(fetch.copies):
-                    fetch.copies[piece].start()
-        body(flag_ref, fetches, targets, *extra)
-        for fetch in fetches:
-            fetch.need()
-
-    specs = [pl.BlockSpec(memory_space=pl.ANY) for _ in arrays]
+        operands = []
+        for arg, ref in zip(args, refs[:count]):
+            if isinstance(arg, tuple):
+                ref = ref.at[pl.ds(arg[1], arg[2][-1])]
+            operands.append(Operand(ref))
+        refs = refs[count:]
+        body(flag_ref, operands, refs[: len(results)], *refs[len(results) :])
+
+    specs = [pl.BlockSpec(memory_space=pltpu.VMEM) for _ in arrays]
     if flags is not None:
         specs = [pl.BlockSpec(memory_space=pltpu.SMEM)] + specs
         arrays = [flags] + arrays
-    return pl.pallas_call(kernel, out_shape=outs, in_specs=specs, scratch_shapes=scratch, name=name)(*arrays)
+    params = pltpu.CompilerParams(vmem_limit_bytes=16 << 20)
+    return pl.pallas_call(
+        kernel, out_shape=outs, in_specs=specs, scratch_shapes=scratch, compiler_params=params, name=name
+    )(*arrays)
 
 
 def stacked_first(array):
@@ -245,21 +244,13 @@
 
 
 def finish(level, own_g, other_g, panels, work_f, right_f, outs, inv_ref):
-    count = work_f.buffer.shape[0]
-    before = []
-
-    def rest():
-        own_p, other_p = panels()
-        work, right = work_f.need(), right_f.need()
-        for k in range(right.shape[0]):
-            before.append(tdot(right[k], wide(work, 0, count)))
-        return own_p, other_p
-
-    _, coef = solve(level, own_g, other_g, rest, inv_ref)
-    for k, product in enumerate(before):
-        spread(outs[1], k * (count - 1), product[:, N:] - dot(product[:, :N], coef))
-    work = work_f.buffer
-    spread(outs[0], 0, wide(work, 1, count) - dot(work[0], coef))
+    work, right = work_f.need(), right_f.need()
+    count = work.shape[0]
+    _, coef = solve(level, own_g, other_g, panels, inv_ref)
+    later = wide(work, 1, count) - dot(work[0], coef)
+    for k in range(right.shape[0]):
+        spread(outs[1], k * (count - 1), tdot(right[k], later))
+    spread(outs[0], 0, later)
 
 
 def octet_body(flag_ref, fetches, outs, inv_ref):
@@ -361,11 +352,11 @@
 
 
 def blocks(count):
-    return jax.ShapeDtypeStruct((count, N, N), jnp.float32)
+    return pltpu.VMEM((count, N, N), jnp.float32)
 
 
 def flat(rows, cols=N):
-    return jax.ShapeDtypeStruct((rows, cols), jnp.float32)
+    return pltpu.VMEM((rows, cols), jnp.float32)
 
 
 def partner(value, bit):
@@ -411,12 +402,16 @@
     work, *panels = call(
         leaf_body, "leaf", (blocks(10), blocks(10), blocks(10), blocks(10)), diag_blocks, left_bases, sources, some_right(0, 3)
     )
-    others = [partner(panel, 0) for panel in panels]
+    others = [partner(panels[0], 0)]
+    panels[1], others[0] = tie(panels[1], others[0])
+    others.append(partner(panels[1], 0))
     done.append(work[0])
     coef, other_coef, work = call(
         pair_body, "pair", (flat(N, 9 * N), flat(N, 9 * N), blocks(9)), stacked_first(panels[0]), stacked_first(others[0]), work
     )
     done.append(work[0])
+    panels[2], others[1], coef = tie(panels[2], others[1], coef)
+    others.append(partner(panels[2], 0))
     fronts, mine = [], []
     for k in (1, 2):
         front, part = call(
@@ -424,10 +419,12 @@
         )
         fronts.append(front)
         mine.append(partner(part, 1))
-    swapped = [partner(part, 0) for part in mine]
+    swapped = [partner(mine[0], 0)]
     coef, other_coef, work = call(
         quad_body, "quad", (flat(N, 8 * N), flat(N, 8 * N), blocks(8)), fronts[0], mine[0], swapped[0], work, flags=flags, full=9 * N
     )
+    coef, mine[1] = tie(coef, mine[1])
+    swapped.append(partner(mine[1], 0))
     done.append(work[0])
     front, part = call(
         quad_merge_body,

time: 406 us -> 348 us (0.86)
  Pallas kernels: 86.6 us -> 43 us
  blocking collectives: 195 us -> 158 us
  waiting for transfers between devices: 57.1 us -> 84.9 us
  local copies, waits for them, and re-layouts: 15.7 us -> 7.89 us
    pallas_call x16, Pallas kernels: 86.6 us -> 43 us  [call(): pl.pallas_call(kernel, out_shape=outs, in_specs=specs, scratch_shapes=scr...]
    all_to_all x7, blocking collectives: 195 us -> 158 us  [exchange(): return lax.all_to_all(value, names, 0, 0)]
    ppermute x13, waiting for transfers between devices: 57.1 us -> 84.9 us  [partner(): return lax.ppermute(value, 'b%d' % bit, [(0, 1), (1, 0)])]
    unnamed x36 -> x29, local copies, waits for them, and re-layouts: 14 us -> 7.56 us
  transfers between devices with their start and end apart: 13 -> 13, of which waited for: 10 -> 12; matrix products, arithmetic and copies ran while one was open for 2% -> 0% of each run, Pallas kernels for 7% -> 4%
where the time goes in v4:
time: 348 us; the launch traced here: 345 us
  blocking collectives  158 us (45%)
  waiting for transfers between devices  84.9 us (24%)
  starting transfers between devices  48.4 us (14%)
  Pallas kernels  43 us (12%)
  local copies, waits for them, and re-layouts  7.89 us (2%)
    all_to_all x7, blocking collectives, exchange(): return lax.all_to_all(value, names, 0, 0)  158 us
    ppermute x13, waiting for transfers between devices, partner(): return lax.ppermute(value, 'b%d' % bit, [(0, 1), (1, 0)])  84.9 us
    ppermute x13, starting transfers between devices, partner(): return lax.ppermute(value, 'b%d' % bit, [(0, 1), (1, 0)])  48.4 us
    pallas_call x16, Pallas kernels, call(): pl.pallas_call(kernel, out_shape=outs, in_specs=specs, scratch_shapes=scr...  43 us
    unnamed x29, local copies, waits for them, and re-layouts  7.56 us
  transfers between devices with their start and end apart: 13, of which 12 were waited for; matrix products, arithmetic and copies ran while one was open for 0% of the time, Pallas kernels for 4%

profile of v4, /device:TPU:6, one launch (start us, length us, event | category | flops | bytes accessed | tf_op | source)
XLA Modules:
  0.0 345.0 jit_solution(863430780872246958)
XLA Ops:
  11.8 14.9 %collective-permute-done.refs_1_ = f32[10,128,128]{2,1,0:T(8,128)S(1)} collective-permute-done((f32[10,128,128]{2,1,0:T(8,128)S(1)}, f32[10,128,128]{2,1,0:T(8,128)S(1)}, u32[]{:S(2)}, u32[]{:S(2)}) %collective-permute-start) | collective-permute-done | bytes 655392 | tf_op jit(solution)/shard_map/ppermute | solution.py:363
  30.2 4.3 %pair.1 = (f32[128,1152]{1,0:T(8,128)S(1)}, f32[128,1152]{1,0:T(8,128)S(1)}, f32[9,128,128]{2,1,0:T(8,128)S(1)}) custom-call(f32[10,128,128]{2,1,0:T(8,128)S(1)} %get-tuple-element.47.refs_0_, f32[10,128,128]{2,1,0:T(8,128)S(1)} %collective-permute-done.refs_1_, f32[10,128,128]{2,1,0:T(8,128)S(1)} %get-tuple-element.50.refs_2_), custom_call_target="tpu_custom_call" | custom-call | tf_op jit(solution)/shard_map/pair/pallas_call | solution.py:137
  34.6 9.7 %collective-permute-done.1.refs_4_ = f32[10,128,128]{2,1,0:T(8,128)S(1)} collective-permute-done((f32[10,128,128]{2,1,0:T(8,128)S(1)}, f32[10,128,128]{2,1,0:T(8,128)S(1)}, u32[]{:S(2)}, u32[]{:S(2)}) %collective-permute-start.1) | collective-permute-done | bytes 655392 | tf_op jit(solution)/shard_map/ppermute | solution.py:363
  52.1 4.5 %collective-permute-start.2 = (f32[576,128]{1,0:T(8,128)S(1)}, f32[576,128]{1,0:T(8,128)S(1)}, u32[]{:S(2)}, u32[]{:S(2)}) collective-permute-start(f32[576,128]{1,0:T(8,128)S(1)} %get-tuple-element.56), channel_id=1, source_target_pairs={{0,2},{2,0},{1,3},{3,1},{4,6},{6,4},{5,7},{7,5},{8,10},{10,8},{9,1... | collective-permute-start | bytes 884744 | tf_op jit(solution)/shard_map/ppermute | solution.py:363
  56.6 10.6 %collective-permute-done.2.refs_2_ = f32[576,128]{1,0:T(8,128)S(1)} collective-permute-done((f32[576,128]{1,0:T(8,128)S(1)}, f32[576,128]{1,0:T(8,128)S(1)}, u32[]{:S(2)}, u32[]{:S(2)}) %collective-permute-start.2) | collective-permute-done | bytes 294944 | tf_op jit(solution)/shard_map/ppermute | solution.py:363
  67.1 5.4 %collective-permute-start.3 = (f32[576,128]{1,0:T(8,128)S(1)}, f32[576,128]{1,0:T(8,128)S(1)}, u32[]{:S(2)}, u32[]{:S(2)}) collective-permute-start(f32[576,128]{1,0:T(8,128)S(1)} %collective-permute-done.2.refs_2_), channel_id=1, source_target_pairs={{0,1},{1,0},{2,3},{3,2},{4,5},{5,4},{6,7},{7,6},{8,9},{9,8},{10,11... | collective-permute-start | bytes 884744 | tf_op jit(solution)/shard_map/ppermute | solution.py:363
  79.9 4.3 %quad.1 = (f32[128,1024]{1,0:T(8,128)S(1)}, f32[128,1024]{1,0:T(8,128)S(1)}, f32[8,128,128]{2,1,0:T(8,128)S(1)}) custom-call(s32[9]{0:T(128)S(1)} %stack.42.refs_0_, f32[1152,128]{1,0:T(8,128)S(1)} %get-tuple-element.55.refs_1_, f32[576,128]{1,0:T(8,128)S(1)} %collective-permute-done.2.refs_2_, f32[576,128]{1,0:T(8,128)S(1)} %collective-permute-done.3.refs_3_, ...), custom_call_target="tpu_custom_call" | custom-call | tf_op jit(solution)/shard_map/quad/pallas_call | solution.py:137
  84.2 5.0 %collective-permute-done.5.refs_4_ = f32[576,128]{1,0:T(8,128)S(1)} collective-permute-done((f32[576,128]{1,0:T(8,128)S(1)}, f32[576,128]{1,0:T(8,128)S(1)}, u32[]{:S(2)}, u32[]{:S(2)}) %collective-permute-start.5) | collective-permute-done | bytes 294944 | tf_op jit(solution)/shard_map/ppermute | solution.py:363
  91.1 7.0 %collective-permute-done.6.refs_5_ = f32[576,128]{1,0:T(8,128)S(1)} collective-permute-done((f32[576,128]{1,0:T(8,128)S(1)}, f32[576,128]{1,0:T(8,128)S(1)}, u32[]{:S(2)}, u32[]{:S(2)}) %collective-permute-start.6) | collective-permute-done | bytes 294944 | tf_op jit(solution)/shard_map/ppermute | solution.py:363
  99.3 6.1 %collective-permute-start.7 = (f32[256,128]{1,0:T(8,128)S(1)}, f32[256,128]{1,0:T(8,128)S(1)}, u32[]{:S(2)}, u32[]{:S(2)}) collective-permute-start(f32[256,128]{1,0:T(8,128)S(1)} %get-tuple-element.66), channel_id=1, source_target_pairs={{0,4},{4,0},{1,5},{5,1},{2,6},{6,2},{3,7},{7,3},{8,12},{12,8},{9,1... | collective-permute-start | bytes 393224 | tf_op jit(solution)/shard_map/ppermute | solution.py:363
  105.4 5.0 %collective-permute-done.7 = f32[256,128]{1,0:T(8,128)S(1)} collective-permute-done((f32[256,128]{1,0:T(8,128)S(1)}, f32[256,128]{1,0:T(8,128)S(1)}, u32[]{:S(2)}, u32[]{:S(2)}) %collective-permute-start.7) | collective-permute-done | bytes 131104 | tf_op jit(solution)/shard_map/ppermute | solution.py:363
  110.4 13.6 %all_to_all.35 = f32[4,256,128]{2,1,0:T(8,128)S(1)} all-to-all(f32[4,256,128]{2,1,0:T(8,128)S(1)} %broadcast_in_dim.8), channel_id=1, replica_groups=mesh['b8'=2,'b7'=2,'b6'=2,'b5'=2,'b4'=2,'b3'=2,'b2'=2,'b1'=2,'b0'=2] {'b..., dimensions={0} | all-to-all | bytes 1048576 | tf_op jit(solution)/shard_map/all_to_all | solution.py:367
  127.8 19.0 %all_to_all.36 = f32[16,56,128]{2,1,0:T(8,128)S(1)} all-to-all(f32[16,56,128]{2,1,0:T(8,128)S(1)} %bitcast.22), channel_id=1, replica_groups=mesh['b8'=2,'b7'=2,'b6'=2,'b5'=2,'b4'=2,'b3'=2,'b2'=2,'b1'=2,'b0'=2] {'b..., dimensions={0} | all-to-all | bytes 917504 | tf_op jit(solution)/shard_map/all_to_all | solution.py:367
  146.9 22.6 %all_to_all.37.refs_1_ = f32[16,2,56,128]{3,2,1,0:T(8,128)S(1)} all-to-all(f32[16,2,56,128]{3,2,1,0:T(8,128)S(1)} %broadcast_in_dim.9), channel_id=1, replica_groups=mesh['b8'=2,'b7'=2,'b6'=2,'b5'=2,'b4'=2,'b3'=2,'b2'=2,'b1'=2,'b0'=2] {'b..., dimensions={0} | all-to-all | bytes 1835008 | tf_op jit(solution)/shard_map/all_to_all | solution.py:367
  169.4 4.4 %level3.1 = (f32[6,128,128]{2,1,0:T(8,128)S(1)}, f32[6,128,128]{2,1,0:T(8,128)S(1)}) custom-call(s32[9]{0:T(128)S(1)} %stack.42.refs_0_, f32[16,2,56,128]{3,2,1,0:T(8,128)S(1)} %all_to_all.37.refs_1_, f32[7,128,128]{2,1,0:T(8,128)S(1)} %get-tuple-element.69.refs_2_, f32[9,128,128]{2,1,0:T(8,128)S(1)} %copy-done.1), custom_call_target="tpu_custom_call" | custom-call | tf_op jit(solution)/shard_map/level3/pallas_call | solution.py:137
  173.8 20.0 %all_to_all.38 = f32[32,24,128]{2,1,0:T(8,128)S(1)} all-to-all(f32[32,24,128]{2,1,0:T(8,128)S(1)} %bitcast.23), channel_id=1, replica_groups=mesh['b8'=2,'b7'=2,'b6'=2,'b5'=2,'b4'=2,'b3'=2,'b2'=2,'b1'=2,'b0'=2] {'b..., dimensions={0} | all-to-all | bytes 786432 | tf_op jit(solution)/shard_map/all_to_all | solution.py:367
  193.9 21.9 %all_to_all.39.refs_1_ = f32[32,2,24,128]{3,2,1,0:T(8,128)S(1)} all-to-all(f32[32,2,24,128]{3,2,1,0:T(8,128)S(1)} %broadcast_in_dim.10), channel_id=1, replica_groups=mesh['b8'=2,'b7'=2,'b6'=2,'b5'=2,'b4'=2,'b3'=2,'b2'=2,'b1'=2,'b0'=2] {'b..., dimensions={0} | all-to-all | bytes 1572864 | tf_op jit(solution)/shard_map/all_to_all | solution.py:367
  215.8 4.1 %level4.1 = (f32[5,128,128]{2,1,0:T(8,128)S(1)}, f32[20,128,128]{2,1,0:T(8,128)S(1)}) custom-call(s32[9]{0:T(128)S(1)} %stack.42.refs_0_, f32[32,2,24,128]{3,2,1,0:T(8,128)S(1)} %all_to_all.39.refs_1_, f32[6,128,128]{2,1,0:T(8,128)S(1)} %get-tuple-element.71.refs_2_, f32[9,128,128]{2,1,0:T(8,128)S(1)} %copy-done.1), custom_call_target="tpu_custom_call" | custom-call | tf_op jit(solution)/shard_map/level4/pallas_call | solution.py:137
  219.9 30.6 %all_to_all.40 = f32[32,80,128]{2,1,0:T(8,128)} all-to-all(f32[32,80,128]{2,1,0:T(8,128)S(1)} %bitcast.21), channel_id=1, replica_groups=mesh['b8'=2,'b7'=2,'b6'=2,'b5'=2,'b4'=2,'b3'=2,'b2'=2,'b1'=2,'b0'=2] {'b..., dimensions={0} | all-to-all | bytes 2621440 | tf_op jit(solution)/shard_map/all_to_all | solution.py:367
  252.0 30.6 %all_to_all.41 = f32[32,80,128]{2,1,0:T(8,128)S(1)} all-to-all(f32[32,80,128]{2,1,0:T(8,128)S(1)} %broadcast_in_dim.11), channel_id=1, replica_groups=mesh['b8'=2,'b7'=2,'b6'=2,'b5'=2,'b4'=2,'b3'=2,'b2'=2,'b1'=2,'b0'=2] {'b..., dimensions={0} | all-to-all | bytes 2621440 | tf_op jit(solution)/shard_map/all_to_all | solution.py:367
  287.5 4.0 %front5.1 = (f32[4,128,128]{2,1,0:T(8,128)S(1)}, f32[1536,128]{1,0:T(8,128)S(1)}, f32[768,128]{1,0:T(8,128)S(1)}) custom-call(s32[9]{0:T(128)S(1)} %stack.42.refs_0_, f32[20,128,128]{2,1,0:T(8,128)S(1)} %bitcast.19, f32[20,128,128]{2,1,0:T(8,128)S(1)} %collective-permute-done.8.refs_2_), custom_call_target="tpu_custom_call" | custom-call | tf_op jit(solution)/shard_map/front5/pallas_call | solution.py:137
  294.6 10.0 %collective-permute-done.9.refs_2_ = f32[768,128]{1,0:T(8,128)S(1)} collective-permute-done((f32[768,128]{1,0:T(8,128)S(1)}, f32[768,128]{1,0:T(8,128)S(1)}, u32[]{:S(2)}, u32[]{:S(2)}) %collective-permute-start.9) | collective-permute-done | bytes 393248 | tf_op jit(solution)/shard_map/ppermute | solution.py:363
  315.6 11.0 %collective-permute-done.11.refs_1_ = f32[6,128,128]{2,1,0:T(8,128)S(1)} collective-permute-done((f32[6,128,128]{2,1,0:T(8,128)S(1)}, f32[6,128,128]{2,1,0:T(8,128)S(1)}, u32[]{:S(2)}, u32[]{:S(2)}) %collective-permute-start.11) | collective-permute-done | bytes 393248 | tf_op jit(solution)/shard_map/ppermute | solution.py:363
  329.5 8.3 %collective-permute-start.12 = (f32[2,128,128]{2,1,0:T(8,128)S(1)}, f32[2,128,128]{2,1,0:T(8,128)S(1)}, u32[]{:S(2)}, u32[]{:S(2)}) collective-permute-start(f32[2,128,128]{2,1,0:T(8,128)S(1)} %get-tuple-element.82.refs_0_), channel_id=1, source_target_pairs={{0,256},{256,0},{1,257},{257,1},{2,258},{258,2},{3,259},{259,3},{4... | collective-permute-start | bytes 393224 | tf_op jit(solution)/shard_map/ppermute | solution.py:363
  (63 shorter events, 67.3 us)
Async XLA Ops:
  0.6 1.1 copy-start
  1.7 1.1 copy-start.6
  2.8 0.8 copy-start.7
  3.6 0.8 copy-start.8
  8.3 36.7 %copy-start.2 = (f32[10,128,128]{2,1,0:T(8,128)}, f32[10,128,128]{2,1,0:T(8,128)S(1)}, u32[]{:S(2)}) copy-start(f32[10,128,128]{2,1,0:T(8,128)S(1)} %get-tuple-element.48.refs_3_) | copy-start | bytes 1966084
  8.4 18.4 %collective-permute-start = (f32[10,128,128]{2,1,0:T(8,128)S(1)}, f32[10,128,128]{2,1,0:T(8,128)S(1)}, u32[]{:S(2)}, u32[]{:S(2)}) collective-permute-start(f32[10,128,128]{2,1,0:T(8,128)S(1)} %get-tuple-element.47.refs_0_), channel_id=1, source_target_pairs={{0,1},{1,0},{2,3},{3,2},{4,5},{5,4},{6,7},{7,6},{8,9},{9,8},{10,11... | collective-permute-start | bytes 1966088 | tf_op jit(solution)/shard_map/ppermute | solution.py:363
  26.7 17.5 %collective-permute-start.1 = (f32[10,128,128]{2,1,0:T(8,128)S(1)}, f32[10,128,128]{2,1,0:T(8,128)S(1)}, u32[]{:S(2)}, u32[]{:S(2)}) collective-permute-start(f32[10,128,128]{2,1,0:T(8,128)S(1)} %get-tuple-element.48.refs_3_), channel_id=1, source_target_pairs={{0,1},{1,0},{2,3},{3,2},{4,5},{5,4},{6,7},{7,6},{8,9},{9,8},{10,11... | collective-permute-start | bytes 1966088 | tf_op jit(solution)/shard_map/ppermute | solution.py:363
  44.2 0.9 copy-start.4
  45.1 27.5 %collective-permute-start.4 = (f32[10,128,128]{2,1,0:T(8,128)S(1)}, f32[10,128,128]{2,1,0:T(8,128)}, u32[]{:S(2)}, u32[]{:S(2)}) collective-permute-start(f32[10,128,128]{2,1,0:T(8,128)S(1)} %get-tuple-element.59.refs_3_), channel_id=1, source_target_pairs={{0,1},{1,0},{2,3},{3,2},{4,5},{5,4},{6,7},{7,6},{8,9},{9,8},{10,11... | collective-permute-start | bytes 1966088 | tf_op jit(solution)/shard_map/ppermute | solution.py:363
  48.7 1.1 copy-start.3
  49.8 1.1 copy-start.5
  52.1 15.1 %collective-permute-start.2 = (f32[576,128]{1,0:T(8,128)S(1)}, f32[576,128]{1,0:T(8,128)S(1)}, u32[]{:S(2)}, u32[]{:S(2)}) collective-permute-start(f32[576,128]{1,0:T(8,128)S(1)} %get-tuple-element.56), channel_id=1, source_target_pairs={{0,2},{2,0},{1,3},{3,1},{4,6},{6,4},{5,7},{7,5},{8,10},{10,8},{9,1... | collective-permute-start | bytes 884744 | tf_op jit(solution)/shard_map/ppermute | solution.py:363
  67.1 12.8 %collective-permute-start.3 = (f32[576,128]{1,0:T(8,128)S(1)}, f32[576,128]{1,0:T(8,128)S(1)}, u32[]{:S(2)}, u32[]{:S(2)}) collective-permute-start(f32[576,128]{1,0:T(8,128)S(1)} %collective-permute-done.2.refs_2_), channel_id=1, source_target_pairs={{0,1},{1,0},{2,3},{3,2},{4,5},{5,4},{6,7},{7,6},{8,9},{9,8},{10,11... | collective-permute-start | bytes 884744 | tf_op jit(solution)/shard_map/ppermute | solution.py:363
  74.3 14.9 %collective-permute-start.5 = (f32[576,128]{1,0:T(8,128)S(1)}, f32[576,128]{1,0:T(8,128)S(1)}, u32[]{:S(2)}, u32[]{:S(2)}) collective-permute-start(f32[576,128]{1,0:T(8,128)S(1)} %get-tuple-element.60), channel_id=1, source_target_pairs={{0,2},{2,0},{1,3},{3,1},{4,6},{6,4},{5,7},{7,5},{8,10},{10,8},{9,1... | collective-permute-start | bytes 884744 | tf_op jit(solution)/shard_map/ppermute | solution.py:363
  89.2 8.9 %collective-permute-start.6 = (f32[576,128]{1,0:T(8,128)S(1)}, f32[576,128]{1,0:T(8,128)S(1)}, u32[]{:S(2)}, u32[]{:S(2)}) collective-permute-start(f32[576,128]{1,0:T(8,128)S(1)} %collective-permute-done.5.refs_4_), channel_id=1, source_target_pairs={{0,1},{1,0},{2,3},{3,2},{4,5},{5,4},{6,7},{7,6},{8,9},{9,8},{10,11... | collective-permute-start | bytes 884744 | tf_op jit(solution)/shard_map/ppermute | solution.py:363
  99.3 24.8 %copy-start.1 = (f32[9,128,128]{2,1,0:T(8,128)S(1)}, f32[9,128,128]{2,1,0:T(8,128)}, u32[]{:S(2)}) copy-start(f32[9,128,128]{2,1,0:T(8,128)} %refs_3_.7) | copy-start | bytes 1769476
  99.3 11.1 %collective-permute-start.7 = (f32[256,128]{1,0:T(8,128)S(1)}, f32[256,128]{1,0:T(8,128)S(1)}, u32[]{:S(2)}, u32[]{:S(2)}) collective-permute-start(f32[256,128]{1,0:T(8,128)S(1)} %get-tuple-element.66), channel_id=1, source_target_pairs={{0,4},{4,0},{1,5},{5,1},{2,6},{6,2},{3,7},{7,3},{8,12},{12,8},{9,1... | collective-permute-start | bytes 393224 | tf_op jit(solution)/shard_map/ppermute | solution.py:363
  282.6 4.9 %collective-permute-start.8 = (f32[20,128,128]{2,1,0:T(8,128)S(1)}, f32[20,128,128]{2,1,0:T(8,128)S(1)}, u32[]{:S(2)}, u32[]{:S(2)}) collective-permute-start(f32[20,128,128]{2,1,0:T(8,128)S(1)} %bitcast.18), channel_id=1, source_target_pairs={{0,32},{32,0},{1,33},{33,1},{2,34},{34,2},{3,35},{35,3},{4,36},{36... | collective-permute-start | bytes 3932168 | tf_op jit(solution)/shard_map/ppermute | solution.py:363
  291.5 13.0 %collective-permute-start.9 = (f32[768,128]{1,0:T(8,128)S(1)}, f32[768,128]{1,0:T(8,128)S(1)}, u32[]{:S(2)}, u32[]{:S(2)}) collective-permute-start(f32[768,128]{1,0:T(8,128)S(1)} %get-tuple-element.74), channel_id=1, source_target_pairs={{0,64},{64,0},{1,65},{65,1},{2,66},{66,2},{3,67},{67,3},{4,68},{68... | collective-permute-start | bytes 1179656 | tf_op jit(solution)/shard_map/ppermute | solution.py:363
  304.6 3.6 %collective-permute-start.10 = (f32[768,128]{1,0:T(8,128)S(1)}, f32[768,128]{1,0:T(8,128)S(1)}, u32[]{:S(2)}, u32[]{:S(2)}) collective-permute-start(f32[768,128]{1,0:T(8,128)S(1)} %collective-permute-done.9.refs_2_), channel_id=1, source_target_pairs={{0,32},{32,0},{1,33},{33,1},{2,34},{34,2},{3,35},{35,3},{4,36},{36... | collective-permute-start | bytes 1179656 | tf_op jit(solution)/shard_map/ppermute | solution.py:363
  312.0 14.6 %collective-permute-start.11 = (f32[6,128,128]{2,1,0:T(8,128)S(1)}, f32[6,128,128]{2,1,0:T(8,128)S(1)}, u32[]{:S(2)}, u32[]{:S(2)}) collective-permute-start(f32[6,128,128]{2,1,0:T(8,128)S(1)} %get-tuple-element.78.refs_0_), channel_id=1, source_target_pairs={{0,128},{128,0},{1,129},{129,1},{2,130},{130,2},{3,131},{131,3},{4... | collective-permute-start | bytes 1179656 | tf_op jit(solution)/shard_map/ppermute | solution.py:363
  329.5 12.1 %collective-permute-start.12 = (f32[2,128,128]{2,1,0:T(8,128)S(1)}, f32[2,128,128]{2,1,0:T(8,128)S(1)}, u32[]{:S(2)}, u32[]{:S(2)}) collective-permute-start(f32[2,128,128]{2,1,0:T(8,128)S(1)} %get-tuple-element.82.refs_0_), channel_id=1, source_target_pairs={{0,256},{256,0},{1,257},{257,1},{2,258},{258,2},{3,259},{259,3},{4... | collective-permute-start | bytes 393224 | tf_op jit(solution)/shard_map/ppermute | solution.py:363
  338.1 6.9 %copy-start.9 = (f32[9,128,128]{2,1,0:T(8,128)}, f32[9,128,128]{2,1,0:T(8,128)S(1)}, u32[]{:S(2)}) copy-start(f32[9,128,128]{2,1,0:T(8,128)S(1)} %slice_dynamic-update-slice_fusion) | copy-start | bytes 1769476

commit v5 on v4

--- a/solution.py
+++ b/solution.py
@@ -143,10 +143,6 @@
     return (array, 0, (0, 1, array.shape[0]))
 
 
-def flat_first(array):
-    return (array, 0, (0, N, array.shape[0]))
-
-
 def flat_wide(ref, first, last):
     return side([ref[i * N : (i + 1) * N] for i in range(first, last)])
 
@@ -156,20 +152,36 @@
         ref[(base + i) * N : (base + i + 1) * N] = value[:, i * N : (i + 1) * N]
 
 
-def leaf_body(flag_ref, fetches, outs, inv_ref):
-    diag_f, left_f, source_f, right_f = fetches
-    diag = diag_f.need()[...]
-    bound = jnp.max(jnp.sum(jnp.abs(diag), axis=0, keepdims=True), axis=1, keepdims=True)
-    start = eye() * (2.0 / (1.0 + bound))
-    left = left_f.need()
-    source = source_f.need()
-    right = right_f.need()
-    invert(diag, start, 6, inv_ref)
+def leaf_kernel(diag_any, left_any, source_any, right_any, work_ref, first_ref, second_ref, diag, left, source, right, sems, inv_ref):
+    rows = right.shape[0]
+    pairs = ((diag_any, diag), (left_any, left), (source_any, source), (right_any.at[pl.ds(0, rows)], right))
+    copies = [pltpu.make_async_copy(*pair, sems.at[i]) for i, pair in enumerate(pairs)]
+    for copy in copies:
+        copy.start()
+    copies[0].wait()
+    block = diag[...]
+    bound = jnp.max(jnp.sum(jnp.abs(block), axis=0, keepdims=True), axis=1, keepdims=True)
+    invert(block, eye() * (2.0 / (1.0 + bound)), 6, inv_ref)
+    for copy in copies[1:]:
+        copy.wait()
     rhs = jnp.concatenate([left[i] for i in range(left.shape[0])] + [source[...]], axis=1)
     work = dot(inv_ref[...], rhs)
-    spread(outs[0], 0, work)
-    for k in range(right.shape[0]):
-        spread(outs[1 + k], 0, tdot(right[k], work))
+    spread(work_ref, 0, work)
+    spread(first_ref, 0, tdot(right[0], work))
+    spread(second_ref, 0, tdot(right[1], work))
+
+
+def leaf(diag_blocks, left_bases, sources, right_bases):
+    shapes = (diag_blocks.shape, left_bases.shape, sources.shape, (2,) + right_bases.shape[1:])
+    return pl.pallas_call(
+        leaf_kernel,
+        out_shape=(jax.ShapeDtypeStruct((10, N, N), jnp.float32), blocks(10), blocks(10)),
+        in_specs=[pl.BlockSpec(memory_space=pltpu.HBM)] * 4,
+        scratch_shapes=[pltpu.VMEM(shape, jnp.float32) for shape in shapes]
+        + [pltpu.SemaphoreType.DMA((4,)), pltpu.VMEM((N, N), jnp.float32)],
+        compiler_params=pltpu.CompilerParams(vmem_limit_bytes=125 << 19),
+        name="leaf",
+    )(diag_blocks, left_bases, sources, right_bases)
 
 
 def solve(level, own_g, other_g, rest, inv_ref):
@@ -182,20 +194,16 @@
 
 
 def pair_body(flag_ref, fetches, outs, inv_ref):
-    own_f, other_f, work_f = fetches
-    count = work_f.buffer.shape[0]
-    own_g, other_g = own_f.need(1)[0], other_f.need(1)[0]
-
-    def rest():
-        own, other = wide(own_f.need(), 1, count), wide(other_f.need(), 1, count)
-        work_f.need()
-        return own, other
-
-    own_p, coef = solve(0, own_g, other_g, rest, inv_ref)
+    own, other = (fetch.need() for fetch in fetches)
+    count = own.shape[0]
+    own_p, coef = solve(0, own[0], other[0], lambda: (wide(own, 1, count), wide(other, 1, count)), inv_ref)
     outs[0][...] = coef
-    outs[1][...] = own_p - dot(own_g, coef)
-    work = work_f.buffer
-    spread(outs[2], 0, wide(work, 1, count) - dot(work[0], coef))
+    outs[1][...] = own_p - dot(own[0], coef)
+
+
+def pair_apply_body(flag_ref, fetches, outs):
+    work, coef = (fetch.need() for fetch in fetches)
+    spread(outs[0], 0, wide(work, 1, work.shape[0]) - dot(work[0], coef[...]))
 
 
 def merge_body(flag_ref, fetches, outs):
@@ -215,34 +223,6 @@
     return full_ref
 
 
-def quad_body(flag_ref, fetches, outs, inv_ref, full_ref):
-    own_f, mine_f, swapped_f, work_f = fetches
-    count = work_f.buffer.shape[0]
-    other = join(flag_ref[0], mine_f, swapped_f, full_ref)
-    own = own_f.need()
-
-    def rest():
-        work_f.need()
-        return flat_wide(own, 1, count), flat_wide(other, 1, count)
-
-    own_p, coef = solve(1, own[:N], other[:N], rest, inv_ref)
-    outs[0][...] = coef
-    outs[1][...] = own_p - dot(own[:N], coef)
-    work = work_f.buffer
-    spread(outs[2], 0, wide(work, 1, count) - dot(work[0], coef))
-
-
-def quad_merge_body(flag_ref, fetches, outs, full_ref):
-    coef_f, other_coef_f, own_f, mine_f, swapped_f = fetches
-    other = join(flag_ref[0], mine_f, swapped_f, full_ref)
-    own, coef, other_coef = own_f.need(), coef_f.need(), other_coef_f.need()
-    count = own.shape[0] // N
-    merged = flat_wide(own, 1, count) + flat_wide(other, 1, count) - dot(own[:N], coef[...]) - dot(other[:N], other_coef[...])
-    put_flat(outs[0], 0, merged)
-    rows = outs[1].shape[0]
-    outs[1][...] = outs[0][pl.ds(pl.multiple_of((2 * flag_ref[1] + flag_ref[0]) * rows, 8), rows)]
-
-
 def finish(level, own_g, other_g, panels, work_f, right_f, outs, inv_ref):
     work, right = work_f.need(), right_f.need()
     count = work.shape[0]
@@ -253,15 +233,16 @@
     spread(outs[0], 0, later)
 
 
-def octet_body(flag_ref, fetches, outs, inv_ref):
-    own_f, other_f, work_f, right_f = fetches
+def quad_body(flag_ref, fetches, outs, inv_ref, full_ref):
+    own_f, mine_f, swapped_f, work_f, right_f = fetches
     count = work_f.buffer.shape[0]
-    own_g, other_g = own_f.need(1)[:N], other_f.need(1)[:N]
+    other = join(flag_ref[0], mine_f, swapped_f, full_ref)
+    own = own_f.need()
 
     def panels():
-        return flat_wide(own_f.need(), 1, count), flat_wide(other_f.need(), 1, count)
-
-    finish(2, own_g, other_g, panels, work_f, right_f, outs, inv_ref)
+        return flat_wide(own, 1, count), flat_wide(other, 1, count)
+
+    finish(1, own[:N], other[:N], panels, work_f, right_f, outs, inv_ref)
 
 
 def level_body(level, flag_ref, fetches, outs, inv_ref):
@@ -399,54 +380,26 @@
     def some_right(low, high):
         return (right_bases, low, (0, high - low))
 
-    work, *panels = call(
-        leaf_body, "leaf", (blocks(10), blocks(10), blocks(10), blocks(10)), diag_blocks, left_bases, sources, some_right(0, 3)
+    work, first, second = leaf(diag_blocks, left_bases, sources, right_bases)
+    first_other = partner(first, 0)
+    second, first_other = tie(second, first_other)
+    second_other = partner(second, 0)
+    done.append(work[0])
+    coef, other_coef = call(pair_body, "pair", (flat(N, 9 * N), flat(N, 9 * N)), first, first_other)
+    front, part = call(
+        merge_body, "merge", (flat(9 * N), flat(9 * N // 2)), coef, other_coef, second, second_other, flags=flags, inverse=False
     )
-    others = [partner(panels[0], 0)]
-    panels[1], others[0] = tie(panels[1], others[0])
-    others.append(partner(panels[1], 0))
-    done.append(work[0])
-    coef, other_coef, work = call(
-        pair_body, "pair", (flat(N, 9 * N), flat(N, 9 * N), blocks(9)), stacked_first(panels[0]), stacked_first(others[0]), work
+    mine = partner(part, 1)
+    work = call(pair_apply_body, "apply0", blocks(9), work, coef, inverse=False)
+    done.append(work[0])
+    mine, work = tie(mine, work)
+    swapped = partner(mine, 0)
+    work, panel = call(
+        quad_body, "quad", (blocks(8), blocks(8)), front, mine, swapped, work, some_right(2, 3), flags=flags, full=9 * N
     )
     done.append(work[0])
-    panels[2], others[1], coef = tie(panels[2], others[1], coef)
-    others.append(partner(panels[2], 0))
-    fronts, mine = [], []
-    for k in (1, 2):
-        front, part = call(
-            merge_body, "merge%d" % k, (flat(9 * N), flat(9 * N // 2)), coef, other_coef, panels[k], others[k], flags=flags, inverse=False
-        )
-        fronts.append(front)
-        mine.append(partner(part, 1))
-    swapped = [partner(mine[0], 0)]
-    coef, other_coef, work = call(
-        quad_body, "quad", (flat(N, 8 * N), flat(N, 8 * N), blocks(8)), fronts[0], mine[0], swapped[0], work, flags=flags, full=9 * N
-    )
-    coef, mine[1] = tie(coef, mine[1])
-    swapped.append(partner(mine[1], 0))
-    done.append(work[0])
-    front, part = call(
-        quad_merge_body,
-        "quadmerge",
-        (flat(8 * N), flat(2 * N)),
-        coef,
-        other_coef,
-        fronts[1],
-        mine[1],
-        swapped[1],
-        flags=flags,
-        full=9 * N,
-        inverse=False,
-    )
-    part = partner(part, 2)
-    other = exchange(jnp.broadcast_to(part[None], (4, 2 * N, N)), axes(0, 2)).reshape(8 * N, N)
-    work, panel = call(
-        octet_body, "octet", (blocks(7), blocks(7)), flat_first(front), flat_first(other), work, some_right(3, 4)
-    )
-    done.append(work[0])
-
-    for level in range(3, TOP):
+
+    for level in range(2, TOP):
         count = targets - level
         both = half_sums(panel, level)
         size, _, piece, _ = both.shape

time: 348 us -> 375 us (1.078)
  blocking collectives: 158 us -> 223 us
  starting transfers between devices: 48.4 us -> 32.2 us
  waiting for transfers between devices: 84.9 us -> 72.6 us
  local copies, waits for them, and re-layouts: 7.89 us -> 1.1 us
    all_to_all x7 -> x8, blocking collectives: 158 us -> 223 us  [exchange(): return lax.all_to_all(value, names, 0, 0)]
    ppermute x13 -> x9, starting transfers between devices: 48.4 us -> 32.2 us  [partner(): return lax.ppermute(value, 'b%d' % bit, [(0, 1), (1, 0)])]
    ppermute x13 -> x9, waiting for transfers between devices: 84.9 us -> 72.6 us  [partner(): return lax.ppermute(value, 'b%d' % bit, [(0, 1), (1, 0)])]
    unnamed x29 -> x15, local copies, waits for them, and re-layouts: 7.56 us -> 0.71 us
    pallas_call x16 -> x14, Pallas kernels: 43 us -> 37.1 us  [call(): pl.pallas_call(kernel, out_shape=outs, in_specs=specs, scratch_shapes=scr...]
    pallas_call x0 -> x1, Pallas kernels: none -> 4.63 us  [leaf(): pl.pallas_call(leaf_kernel, out_shape=(jax.ShapeDtypeStruct((10, N, N), j...]
  transfers between devices with their start and end apart: 13 -> 9, of which waited for: 12 -> 9; matrix products, arithmetic and copies ran while one was open for 0% -> 0% of each run, Pallas kernels for 4% -> 1%
where the time goes in v5:
time: 375 us; the launch traced here: 374 us
  blocking collectives  223 us (59%)
  waiting for transfers between devices  72.6 us (19%)
  Pallas kernels  41.7 us (11%)
  starting transfers between devices  32.2 us (9%)
    all_to_all x8, blocking collectives, exchange(): return lax.all_to_all(value, names, 0, 0)  223 us
    ppermute x9, waiting for transfers between devices, partner(): return lax.ppermute(value, 'b%d' % bit, [(0, 1), (1, 0)])  72.6 us
    pallas_call x14, Pallas kernels, call(): pl.pallas_call(kernel, out_shape=outs, in_specs=specs, scratch_shapes=scr...  37.1 us
    ppermute x9, starting transfers between devices, partner(): return lax.ppermute(value, 'b%d' % bit, [(0, 1), (1, 0)])  32.2 us
  transfers between devices with their start and end apart: 9, of which 9 were waited for; matrix products, arithmetic and copies ran while one was open for 0% of the time, Pallas kernels for 1%

profile of v5, /device:TPU:6, one launch (start us, length us, event | category | flops | bytes accessed | tf_op | source)
XLA Modules:
  0.0 373.6 jit_solution(9650234035903816355)
XLA Ops:
  0.6 4.6 %leaf.1 = (f32[10,128,128]{2,1,0:T(8,128)}, f32[10,128,128]{2,1,0:T(8,128)S(1)}, f32[10,128,128]{2,1,0:T(8,128)S(1)}) custom-call(f32[128,128]{1,0:T(8,128)} %diag_any.1, f32[9,128,128]{2,1,0:T(8,128)} %left_any.1, f32[128,128]{1,0:T(8,128)} %source_any.1, f32[9,128,128]{2,1,0:T(8,128)} %refs_3_.5), custom_call_target="tpu_custom_call" | custom-call | tf_op jit(solution)/shard_map/leaf/pallas_call | solution.py:176
  8.8 14.9 %collective-permute-done.refs_1_ = f32[10,128,128]{2,1,0:T(8,128)S(1)} collective-permute-done((f32[10,128,128]{2,1,0:T(8,128)S(1)}, f32[10,128,128]{2,1,0:T(8,128)S(1)}, u32[]{:S(2)}, u32[]{:S(2)}) %collective-permute-start) | collective-permute-done | bytes 655392 | tf_op jit(solution)/shard_map/ppermute | solution.py:344
  27.2 4.3 %pair.1 = (f32[128,1152]{1,0:T(8,128)S(1)}, f32[128,1152]{1,0:T(8,128)S(1)}) custom-call(f32[10,128,128]{2,1,0:T(8,128)S(1)} %get-tuple-element.35.refs_0_, f32[10,128,128]{2,1,0:T(8,128)S(1)} %collective-permute-done.refs_1_), custom_call_target="tpu_custom_call" | custom-call | tf_op jit(solution)/shard_map/pair/pallas_call | solution.py:137
  31.5 9.6 %collective-permute-done.1.refs_4_ = f32[10,128,128]{2,1,0:T(8,128)S(1)} collective-permute-done((f32[10,128,128]{2,1,0:T(8,128)S(1)}, f32[10,128,128]{2,1,0:T(8,128)S(1)}, u32[]{:S(2)}, u32[]{:S(2)}) %collective-permute-start.1) | collective-permute-done | bytes 655392 | tf_op jit(solution)/shard_map/ppermute | solution.py:344
  42.3 4.6 %collective-permute-start.2 = (f32[576,128]{1,0:T(8,128)S(1)}, f32[576,128]{1,0:T(8,128)S(1)}, u32[]{:S(2)}, u32[]{:S(2)}) collective-permute-start(f32[576,128]{1,0:T(8,128)S(1)} %get-tuple-element.42), channel_id=1, source_target_pairs={{0,2},{2,0},{1,3},{3,1},{4,6},{6,4},{5,7},{7,5},{8,10},{10,8},{9,1... | collective-permute-start | bytes 884744 | tf_op jit(solution)/shard_map/ppermute | solution.py:344
  47.4 11.2 %collective-permute-done.2.refs_2_ = f32[576,128]{1,0:T(8,128)S(1)} collective-permute-done((f32[576,128]{1,0:T(8,128)S(1)}, f32[576,128]{1,0:T(8,128)S(1)}, u32[]{:S(2)}, u32[]{:S(2)}) %collective-permute-start.2) | collective-permute-done | bytes 294944 | tf_op jit(solution)/shard_map/ppermute | solution.py:344
  61.2 7.2 %collective-permute-done.3.refs_3_ = f32[576,128]{1,0:T(8,128)S(1)} collective-permute-done((f32[576,128]{1,0:T(8,128)S(1)}, f32[576,128]{1,0:T(8,128)S(1)}, u32[]{:S(2)}, u32[]{:S(2)}) %collective-permute-start.3) | collective-permute-done | bytes 294944 | tf_op jit(solution)/shard_map/ppermute | solution.py:344
  68.4 4.4 %quad.1 = (f32[8,128,128]{2,1,0:T(8,128)S(1)}, f32[8,128,128]{2,1,0:T(8,128)S(1)}) custom-call(s32[9]{0:T(128)S(1)} %stack.42.refs_0_, f32[1152,128]{1,0:T(8,128)S(1)} %get-tuple-element.41.refs_1_, f32[576,128]{1,0:T(8,128)S(1)} %collective-permute-done.2.refs_2_, f32[576,128]{1,0:T(8,128)S(1)} %collective-permute-done.3.refs_3_, ...), custom_call_target="tpu_custom_call" | custom-call | tf_op jit(solution)/shard_map/quad/pallas_call | solution.py:137
  72.9 24.5 %all_to_all.40 = f32[8,128,128]{2,1,0:T(8,128)S(1)} all-to-all(f32[8,128,128]{2,1,0:T(8,128)S(1)} %get-tuple-element.46), channel_id=1, replica_groups=mesh['b8'=2,'b7'=2,'b6'=2,'b5'=2,'b4'=2,'b3'=2,'b2'=2,'b1'=2,'b0'=2] {'b..., dimensions={0} | all-to-all | bytes 1048576 | tf_op jit(solution)/shard_map/all_to_all | solution.py:348
  97.5 29.4 %all_to_all.41.refs_1_ = f32[8,2,128,128]{3,2,1,0:T(8,128)S(1)} all-to-all(f32[8,2,128,128]{3,2,1,0:T(8,128)S(1)} %broadcast_in_dim.8), channel_id=1, replica_groups=mesh['b8'=2,'b7'=2,'b6'=2,'b5'=2,'b4'=2,'b3'=2,'b2'=2,'b1'=2,'b0'=2] {'b..., dimensions={0} | all-to-all | bytes 2097152 | tf_op jit(solution)/shard_map/all_to_all | solution.py:348
  126.9 4.3 %level2.1 = (f32[7,128,128]{2,1,0:T(8,128)S(1)}, f32[7,128,128]{2,1,0:T(8,128)S(1)}) custom-call(s32[9]{0:T(128)S(1)} %stack.42.refs_0_, f32[8,2,128,128]{3,2,1,0:T(8,128)S(1)} %all_to_all.41.refs_1_, f32[8,128,128]{2,1,0:T(8,128)S(1)} %get-tuple-element.47.refs_2_, f32[9,128,128]{2,1,0:T(8,128)S(1)} %copy-done), custom_call_target="tpu_custom_call" | custom-call | tf_op jit(solution)/shard_map/level2/pallas_call | solution.py:137
  131.2 16.0 %all_to_all.42 = f32[16,56,128]{2,1,0:T(8,128)S(1)} all-to-all(f32[16,56,128]{2,1,0:T(8,128)S(1)} %bitcast.22), channel_id=1, replica_groups=mesh['b8'=2,'b7'=2,'b6'=2,'b5'=2,'b4'=2,'b3'=2,'b2'=2,'b1'=2,'b0'=2] {'b..., dimensions={0} | all-to-all | bytes 917504 | tf_op jit(solution)/shard_map/all_to_all | solution.py:348
  147.3 27.2 %all_to_all.43.refs_1_ = f32[16,2,56,128]{3,2,1,0:T(8,128)S(1)} all-to-all(f32[16,2,56,128]{3,2,1,0:T(8,128)S(1)} %broadcast_in_dim.9), channel_id=1, replica_groups=mesh['b8'=2,'b7'=2,'b6'=2,'b5'=2,'b4'=2,'b3'=2,'b2'=2,'b1'=2,'b0'=2] {'b..., dimensions={0} | all-to-all | bytes 1835008 | tf_op jit(solution)/shard_map/all_to_all | solution.py:348
  174.5 4.2 %level3.1 = (f32[6,128,128]{2,1,0:T(8,128)S(1)}, f32[6,128,128]{2,1,0:T(8,128)S(1)}) custom-call(s32[9]{0:T(128)S(1)} %stack.42.refs_0_, f32[16,2,56,128]{3,2,1,0:T(8,128)S(1)} %all_to_all.43.refs_1_, f32[7,128,128]{2,1,0:T(8,128)S(1)} %get-tuple-element.49.refs_2_, f32[9,128,128]{2,1,0:T(8,128)S(1)} %copy-done), custom_call_target="tpu_custom_call" | custom-call | tf_op jit(solution)/shard_map/level3/pallas_call | solution.py:137
  178.7 22.3 %all_to_all.44 = f32[32,24,128]{2,1,0:T(8,128)S(1)} all-to-all(f32[32,24,128]{2,1,0:T(8,128)S(1)} %bitcast.23), channel_id=1, replica_groups=mesh['b8'=2,'b7'=2,'b6'=2,'b5'=2,'b4'=2,'b3'=2,'b2'=2,'b1'=2,'b0'=2] {'b..., dimensions={0} | all-to-all | bytes 786432 | tf_op jit(solution)/shard_map/all_to_all | solution.py:348
  201.1 27.0 %all_to_all.45.refs_1_ = f32[32,2,24,128]{3,2,1,0:T(8,128)S(1)} all-to-all(f32[32,2,24,128]{3,2,1,0:T(8,128)S(1)} %broadcast_in_dim.10), channel_id=1, replica_groups=mesh['b8'=2,'b7'=2,'b6'=2,'b5'=2,'b4'=2,'b3'=2,'b2'=2,'b1'=2,'b0'=2] {'b..., dimensions={0} | all-to-all | bytes 1572864 | tf_op jit(solution)/shard_map/all_to_all | solution.py:348
  228.1 4.1 %level4.1 = (f32[5,128,128]{2,1,0:T(8,128)S(1)}, f32[20,128,128]{2,1,0:T(8,128)S(1)}) custom-call(s32[9]{0:T(128)S(1)} %stack.42.refs_0_, f32[32,2,24,128]{3,2,1,0:T(8,128)S(1)} %all_to_all.45.refs_1_, f32[6,128,128]{2,1,0:T(8,128)S(1)} %get-tuple-element.51.refs_2_, f32[9,128,128]{2,1,0:T(8,128)S(1)} %copy-done), custom_call_target="tpu_custom_call" | custom-call | tf_op jit(solution)/shard_map/level4/pallas_call | solution.py:137
  232.2 38.6 %all_to_all.46 = f32[32,80,128]{2,1,0:T(8,128)} all-to-all(f32[32,80,128]{2,1,0:T(8,128)S(1)} %bitcast.21), channel_id=1, replica_groups=mesh['b8'=2,'b7'=2,'b6'=2,'b5'=2,'b4'=2,'b3'=2,'b2'=2,'b1'=2,'b0'=2] {'b..., dimensions={0} | all-to-all | bytes 2621440 | tf_op jit(solution)/shard_map/all_to_all | solution.py:348
  272.3 38.5 %all_to_all.47 = f32[32,80,128]{2,1,0:T(8,128)S(1)} all-to-all(f32[32,80,128]{2,1,0:T(8,128)S(1)} %broadcast_in_dim.11), channel_id=1, replica_groups=mesh['b8'=2,'b7'=2,'b6'=2,'b5'=2,'b4'=2,'b3'=2,'b2'=2,'b1'=2,'b0'=2] {'b..., dimensions={0} | all-to-all | bytes 2621440 | tf_op jit(solution)/shard_map/all_to_all | solution.py:348
  315.7 4.0 %front5.1 = (f32[4,128,128]{2,1,0:T(8,128)S(1)}, f32[1536,128]{1,0:T(8,128)S(1)}, f32[768,128]{1,0:T(8,128)S(1)}) custom-call(s32[9]{0:T(128)S(1)} %stack.42.refs_0_, f32[20,128,128]{2,1,0:T(8,128)S(1)} %bitcast.20, f32[20,128,128]{2,1,0:T(8,128)S(1)} %collective-permute-done.4.refs_2_), custom_call_target="tpu_custom_call" | custom-call | tf_op jit(solution)/shard_map/front5/pallas_call | solution.py:137
  322.8 10.0 %collective-permute-done.5.refs_2_ = f32[768,128]{1,0:T(8,128)S(1)} collective-permute-done((f32[768,128]{1,0:T(8,128)S(1)}, f32[768,128]{1,0:T(8,128)S(1)}, u32[]{:S(2)}, u32[]{:S(2)}) %collective-permute-start.5) | collective-permute-done | bytes 393248 | tf_op jit(solution)/shard_map/ppermute | solution.py:344
  343.8 11.0 %collective-permute-done.7.refs_1_ = f32[6,128,128]{2,1,0:T(8,128)S(1)} collective-permute-done((f32[6,128,128]{2,1,0:T(8,128)S(1)}, f32[6,128,128]{2,1,0:T(8,128)S(1)}, u32[]{:S(2)}, u32[]{:S(2)}) %collective-permute-start.7) | collective-permute-done | bytes 393248 | tf_op jit(solution)/shard_map/ppermute | solution.py:344
  357.8 8.2 %collective-permute-start.8 = (f32[2,128,128]{2,1,0:T(8,128)S(1)}, f32[2,128,128]{2,1,0:T(8,128)S(1)}, u32[]{:S(2)}, u32[]{:S(2)}) collective-permute-start(f32[2,128,128]{2,1,0:T(8,128)S(1)} %get-tuple-element.62.refs_0_), channel_id=1, source_target_pairs={{0,256},{256,0},{1,257},{257,1},{2,258},{258,2},{3,259},{259,3},{4... | collective-permute-start | bytes 393224 | tf_op jit(solution)/shard_map/ppermute | solution.py:344
  366.2 4.1 %collective-permute-done.8.refs_1_ = f32[2,128,128]{2,1,0:T(8,128)S(1)} collective-permute-done((f32[2,128,128]{2,1,0:T(8,128)S(1)}, f32[2,128,128]{2,1,0:T(8,128)S(1)}, u32[]{:S(2)}, u32[]{:S(2)}) %collective-permute-start.8) | collective-permute-done | bytes 131104 | tf_op jit(solution)/shard_map/ppermute | solution.py:344
  (42 shorter events, 38.4 us)
Async XLA Ops:
  5.3 18.4 %collective-permute-start = (f32[10,128,128]{2,1,0:T(8,128)S(1)}, f32[10,128,128]{2,1,0:T(8,128)S(1)}, u32[]{:S(2)}, u32[]{:S(2)}) collective-permute-start(f32[10,128,128]{2,1,0:T(8,128)S(1)} %get-tuple-element.35.refs_0_), channel_id=1, source_target_pairs={{0,1},{1,0},{2,3},{3,2},{4,5},{5,4},{6,7},{7,6},{8,9},{9,8},{10,11... | collective-permute-start | bytes 1966088 | tf_op jit(solution)/shard_map/ppermute | solution.py:344
  23.6 17.5 %collective-permute-start.1 = (f32[10,128,128]{2,1,0:T(8,128)S(1)}, f32[10,128,128]{2,1,0:T(8,128)S(1)}, u32[]{:S(2)}, u32[]{:S(2)}) collective-permute-start(f32[10,128,128]{2,1,0:T(8,128)S(1)} %get-tuple-element.40.refs_3_), channel_id=1, source_target_pairs={{0,1},{1,0},{2,3},{3,2},{4,5},{5,4},{6,7},{7,6},{8,9},{9,8},{10,11... | collective-permute-start | bytes 1966088 | tf_op jit(solution)/shard_map/ppermute | solution.py:344
  31.5 15.5 %copy-start.1 = (f32[10,128,128]{2,1,0:T(8,128)S(1)}, f32[10,128,128]{2,1,0:T(8,128)}, u32[]{:S(2)}) copy-start(f32[10,128,128]{2,1,0:T(8,128)} %get-tuple-element.43.refs_0_) | copy-start | bytes 1966084
  42.3 26.1 %copy-start = (f32[9,128,128]{2,1,0:T(8,128)S(1)}, f32[9,128,128]{2,1,0:T(8,128)}, u32[]{:S(2)}) copy-start(f32[9,128,128]{2,1,0:T(8,128)} %refs_3_.5) | copy-start | bytes 1769476
  42.3 16.3 %collective-permute-start.2 = (f32[576,128]{1,0:T(8,128)S(1)}, f32[576,128]{1,0:T(8,128)S(1)}, u32[]{:S(2)}, u32[]{:S(2)}) collective-permute-start(f32[576,128]{1,0:T(8,128)S(1)} %get-tuple-element.42), channel_id=1, source_target_pairs={{0,2},{2,0},{1,3},{3,1},{4,6},{6,4},{5,7},{7,5},{8,10},{10,8},{9,1... | collective-permute-start | bytes 884744 | tf_op jit(solution)/shard_map/ppermute | solution.py:344
  58.6 9.8 %collective-permute-start.3 = (f32[576,128]{1,0:T(8,128)S(1)}, f32[576,128]{1,0:T(8,128)S(1)}, u32[]{:S(2)}, u32[]{:S(2)}) collective-permute-start(f32[576,128]{1,0:T(8,128)S(1)} %collective-permute-done.2.refs_2_), channel_id=1, source_target_pairs={{0,1},{1,0},{2,3},{3,2},{4,5},{5,4},{6,7},{7,6},{8,9},{9,8},{10,11... | collective-permute-start | bytes 884744 | tf_op jit(solution)/shard_map/ppermute | solution.py:344
  310.8 4.9 %collective-permute-start.4 = (f32[20,128,128]{2,1,0:T(8,128)S(1)}, f32[20,128,128]{2,1,0:T(8,128)S(1)}, u32[]{:S(2)}, u32[]{:S(2)}) collective-permute-start(f32[20,128,128]{2,1,0:T(8,128)S(1)} %bitcast.19), channel_id=1, source_target_pairs={{0,32},{32,0},{1,33},{33,1},{2,34},{34,2},{3,35},{35,3},{4,36},{36... | collective-permute-start | bytes 3932168 | tf_op jit(solution)/shard_map/ppermute | solution.py:344
  319.7 13.0 %collective-permute-start.5 = (f32[768,128]{1,0:T(8,128)S(1)}, f32[768,128]{1,0:T(8,128)S(1)}, u32[]{:S(2)}, u32[]{:S(2)}) collective-permute-start(f32[768,128]{1,0:T(8,128)S(1)} %get-tuple-element.54), channel_id=1, source_target_pairs={{0,64},{64,0},{1,65},{65,1},{2,66},{66,2},{3,67},{67,3},{4,68},{68... | collective-permute-start | bytes 1179656 | tf_op jit(solution)/shard_map/ppermute | solution.py:344
  332.8 3.6 collective-permute-start.6
  340.2 14.6 %collective-permute-start.7 = (f32[6,128,128]{2,1,0:T(8,128)S(1)}, f32[6,128,128]{2,1,0:T(8,128)S(1)}, u32[]{:S(2)}, u32[]{:S(2)}) collective-permute-start(f32[6,128,128]{2,1,0:T(8,128)S(1)} %get-tuple-element.58.refs_0_), channel_id=1, source_target_pairs={{0,128},{128,0},{1,129},{129,1},{2,130},{130,2},{3,131},{131,3},{4... | collective-permute-start | bytes 1179656 | tf_op jit(solution)/shard_map/ppermute | solution.py:344
  357.8 12.5 %collective-permute-start.8 = (f32[2,128,128]{2,1,0:T(8,128)S(1)}, f32[2,128,128]{2,1,0:T(8,128)S(1)}, u32[]{:S(2)}, u32[]{:S(2)}) collective-permute-start(f32[2,128,128]{2,1,0:T(8,128)S(1)} %get-tuple-element.62.refs_0_), channel_id=1, source_target_pairs={{0,256},{256,0},{1,257},{257,1},{2,258},{258,2},{3,259},{259,3},{4... | collective-permute-start | bytes 393224 | tf_op jit(solution)/shard_map/ppermute | solution.py:344
  366.2 7.4 %copy-start.2 = (f32[9,128,128]{2,1,0:T(8,128)}, f32[9,128,128]{2,1,0:T(8,128)S(1)}, u32[]{:S(2)}) copy-start(f32[9,128,128]{2,1,0:T(8,128)S(1)} %slice_dynamic-update-slice_fusion) | copy-start | bytes 1769476

commit v6 on v5

--- a/solution.py
+++ b/solution.py
@@ -9,6 +9,7 @@
 BITS = 9
 NAMES = tuple("b%d" % bit for bit in reversed(range(BITS)))
 TOP = 5
+STAGGER = 3000
 ROUNDS = (9, 7, 6, 6, 5, 5, 5, 5, 5)
 N = 128
 
@@ -152,7 +153,7 @@
         ref[(base + i) * N : (base + i + 1) * N] = value[:, i * N : (i + 1) * N]
 
 
-def leaf_kernel(diag_any, left_any, source_any, right_any, work_ref, first_ref, second_ref, diag, left, source, right, sems, inv_ref):
+def leaf_kernel(flag_ref, diag_any, left_any, source_any, right_any, work_ref, first_ref, second_ref, diag, left, source, right, sems, inv_ref):
     rows = right.shape[0]
     pairs = ((diag_any, diag), (left_any, left), (source_any, source), (right_any.at[pl.ds(0, rows)], right))
     copies = [pltpu.make_async_copy(*pair, sems.at[i]) for i, pair in enumerate(pairs)]
@@ -170,18 +171,22 @@
     spread(first_ref, 0, tdot(right[0], work))
     spread(second_ref, 0, tdot(right[1], work))
 
-
-def leaf(diag_blocks, left_bases, sources, right_bases):
+    @pl.when(flag_ref[5] == 0)
+    def _():
+        pl.delay(STAGGER)
+
+
+def leaf(flags, diag_blocks, left_bases, sources, right_bases):
     shapes = (diag_blocks.shape, left_bases.shape, sources.shape, (2,) + right_bases.shape[1:])
     return pl.pallas_call(
         leaf_kernel,
         out_shape=(jax.ShapeDtypeStruct((10, N, N), jnp.float32), blocks(10), blocks(10)),
-        in_specs=[pl.BlockSpec(memory_space=pltpu.HBM)] * 4,
+        in_specs=[pl.BlockSpec(memory_space=pltpu.SMEM)] + [pl.BlockSpec(memory_space=pltpu.HBM)] * 4,
         scratch_shapes=[pltpu.VMEM(shape, jnp.float32) for shape in shapes]
         + [pltpu.SemaphoreType.DMA((4,)), pltpu.VMEM((N, N), jnp.float32)],
         compiler_params=pltpu.CompilerParams(vmem_limit_bytes=125 << 19),
         name="leaf",
-    )(diag_blocks, left_bases, sources, right_bases)
+    )(flags, diag_blocks, left_bases, sources, right_bases)
 
 
 def solve(level, own_g, other_g, rest, inv_ref):
@@ -380,7 +385,7 @@
     def some_right(low, high):
         return (right_bases, low, (0, high - low))
 
-    work, first, second = leaf(diag_blocks, left_bases, sources, right_bases)
+    work, first, second = leaf(flags, diag_blocks, left_bases, sources, right_bases)
     first_other = partner(first, 0)
     second, first_other = tie(second, first_other)
     second_other = partner(second, 0)

time: 375 us -> 334 us (0.89)
  blocking collectives: 223 us -> 188 us
  waiting for transfers between devices: 72.6 us -> 62.1 us
  Pallas kernels: 41.7 us -> 46.2 us
    all_to_all x8, blocking collectives: 223 us -> 188 us  [exchange(): return lax.all_to_all(value, names, 0, 0)]
    ppermute x9, waiting for transfers between devices: 72.6 us -> 62.1 us  [partner(): return lax.ppermute(value, 'b%d' % bit, [(0, 1), (1, 0)])]
    pallas_call x1, Pallas kernels: 4.63 us -> 9.16 us  [leaf(): pl.pallas_call(leaf_kernel, out_shape=(jax.ShapeDtypeStruct((10, N, N), j...]
  transfers between devices with their start and end apart: 9 -> 9, of which waited for: 9 -> 9; matrix products, arithmetic and copies ran while one was open for 0% -> 0% of each run, Pallas kernels for 1% -> 2%
where the time goes in v6:
time: 334 us; the launch traced here: 333 us
  blocking collectives  188 us (56%)
  waiting for transfers between devices  62.1 us (19%)
  Pallas kernels  46.2 us (14%)
  starting transfers between devices  32.3 us (10%)
    all_to_all x8, blocking collectives, exchange(): return lax.all_to_all(value, names, 0, 0)  188 us
    ppermute x9, waiting for transfers between devices, partner(): return lax.ppermute(value, 'b%d' % bit, [(0, 1), (1, 0)])  62.1 us
    pallas_call x14, Pallas kernels, call(): pl.pallas_call(kernel, out_shape=outs, in_specs=specs, scratch_shapes=scr...  37 us
    ppermute x9, starting transfers between devices, partner(): return lax.ppermute(value, 'b%d' % bit, [(0, 1), (1, 0)])  32.3 us
    pallas_call x1, Pallas kernels, leaf(): pl.pallas_call(leaf_kernel, out_shape=(jax.ShapeDtypeStruct((10, N, N), j...  9.16 us
  transfers between devices with their start and end apart: 9, of which 9 were waited for; matrix products, arithmetic and copies ran while one was open for 0% of the time, Pallas kernels for 2%

profile of v6, /device:TPU:6, one launch (start us, length us, event | category | flops | bytes accessed | tf_op | source)
XLA Modules:
  0.0 332.9 jit_solution(13906046742949461810)
XLA Ops:
  1.3 9.2 %leaf.1 = (f32[10,128,128]{2,1,0:T(8,128)}, f32[10,128,128]{2,1,0:T(8,128)S(1)}, f32[10,128,128]{2,1,0:T(8,128)S(1)}) custom-call(s32[9]{0:T(128)} %stack.42.flag_ref.refs_0_, f32[128,128]{1,0:T(8,128)} %diag_any.1, f32[9,128,128]{2,1,0:T(8,128)} %left_any.1, f32[128,128]{1,0:T(8,128)} %source_any.1, f32[9,128,128]{2,1,0:T(8,128)} %refs_3_.5), custom_call_target="tpu_custom_call" | custom-call | tf_op jit(solution)/shard_map/leaf/pallas_call | solution.py:181
  13.9 11.9 %collective-permute-done.refs_1_ = f32[10,128,128]{2,1,0:T(8,128)S(1)} collective-permute-done((f32[10,128,128]{2,1,0:T(8,128)S(1)}, f32[10,128,128]{2,1,0:T(8,128)S(1)}, u32[]{:S(2)}, u32[]{:S(2)}) %collective-permute-start) | collective-permute-done | bytes 655392 | tf_op jit(solution)/shard_map/ppermute | solution.py:349
  29.3 4.3 %pair.1 = (f32[128,1152]{1,0:T(8,128)S(1)}, f32[128,1152]{1,0:T(8,128)S(1)}) custom-call(f32[10,128,128]{2,1,0:T(8,128)S(1)} %get-tuple-element.35.refs_0_, f32[10,128,128]{2,1,0:T(8,128)S(1)} %collective-permute-done.refs_1_), custom_call_target="tpu_custom_call" | custom-call | tf_op jit(solution)/shard_map/pair/pallas_call | solution.py:138
  33.6 6.7 %collective-permute-done.1.refs_4_ = f32[10,128,128]{2,1,0:T(8,128)S(1)} collective-permute-done((f32[10,128,128]{2,1,0:T(8,128)S(1)}, f32[10,128,128]{2,1,0:T(8,128)S(1)}, u32[]{:S(2)}, u32[]{:S(2)}) %collective-permute-start.1) | collective-permute-done | bytes 655392 | tf_op jit(solution)/shard_map/ppermute | solution.py:349
  41.5 4.6 %collective-permute-start.2 = (f32[576,128]{1,0:T(8,128)S(1)}, f32[576,128]{1,0:T(8,128)S(1)}, u32[]{:S(2)}, u32[]{:S(2)}) collective-permute-start(f32[576,128]{1,0:T(8,128)S(1)} %get-tuple-element.42), channel_id=1, source_target_pairs={{0,2},{2,0},{1,3},{3,1},{4,6},{6,4},{5,7},{7,5},{8,10},{10,8},{9,1... | collective-permute-start | bytes 884744 | tf_op jit(solution)/shard_map/ppermute | solution.py:349
  46.6 8.2 %collective-permute-done.2.refs_2_ = f32[576,128]{1,0:T(8,128)S(1)} collective-permute-done((f32[576,128]{1,0:T(8,128)S(1)}, f32[576,128]{1,0:T(8,128)S(1)}, u32[]{:S(2)}, u32[]{:S(2)}) %collective-permute-start.2) | collective-permute-done | bytes 294944 | tf_op jit(solution)/shard_map/ppermute | solution.py:349
  57.4 6.0 %collective-permute-done.3.refs_3_ = f32[576,128]{1,0:T(8,128)S(1)} collective-permute-done((f32[576,128]{1,0:T(8,128)S(1)}, f32[576,128]{1,0:T(8,128)S(1)}, u32[]{:S(2)}, u32[]{:S(2)}) %collective-permute-start.3) | collective-permute-done | bytes 294944 | tf_op jit(solution)/shard_map/ppermute | solution.py:349
  63.4 4.4 %quad.1 = (f32[8,128,128]{2,1,0:T(8,128)S(1)}, f32[8,128,128]{2,1,0:T(8,128)S(1)}) custom-call(s32[9]{0:T(128)S(1)} %copy-done.2, f32[1152,128]{1,0:T(8,128)S(1)} %get-tuple-element.41.refs_1_, f32[576,128]{1,0:T(8,128)S(1)} %collective-permute-done.2.refs_2_, f32[576,128]{1,0:T(8,128)S(1)} %collective-permute-done.3.refs_3_, ...), custom_call_target="tpu_custom_call" | custom-call | tf_op jit(solution)/shard_map/quad/pallas_call | solution.py:138
  67.8 20.9 %all_to_all.40 = f32[8,128,128]{2,1,0:T(8,128)S(1)} all-to-all(f32[8,128,128]{2,1,0:T(8,128)S(1)} %get-tuple-element.46), channel_id=1, replica_groups=mesh['b8'=2,'b7'=2,'b6'=2,'b5'=2,'b4'=2,'b3'=2,'b2'=2,'b1'=2,'b0'=2] {'b..., dimensions={0} | all-to-all | bytes 1048576 | tf_op jit(solution)/shard_map/all_to_all | solution.py:353
  88.8 26.6 %all_to_all.41.refs_1_ = f32[8,2,128,128]{3,2,1,0:T(8,128)S(1)} all-to-all(f32[8,2,128,128]{3,2,1,0:T(8,128)S(1)} %broadcast_in_dim.8), channel_id=1, replica_groups=mesh['b8'=2,'b7'=2,'b6'=2,'b5'=2,'b4'=2,'b3'=2,'b2'=2,'b1'=2,'b0'=2] {'b..., dimensions={0} | all-to-all | bytes 2097152 | tf_op jit(solution)/shard_map/all_to_all | solution.py:353
  115.4 4.3 %level2.1 = (f32[7,128,128]{2,1,0:T(8,128)S(1)}, f32[7,128,128]{2,1,0:T(8,128)S(1)}) custom-call(s32[9]{0:T(128)S(1)} %copy-done.2, f32[8,2,128,128]{3,2,1,0:T(8,128)S(1)} %all_to_all.41.refs_1_, f32[8,128,128]{2,1,0:T(8,128)S(1)} %get-tuple-element.47.refs_2_, f32[9,128,128]{2,1,0:T(8,128)S(1)} %copy-done), custom_call_target="tpu_custom_call" | custom-call | tf_op jit(solution)/shard_map/level2/pallas_call | solution.py:138
  119.8 14.9 %all_to_all.42 = f32[16,56,128]{2,1,0:T(8,128)S(1)} all-to-all(f32[16,56,128]{2,1,0:T(8,128)S(1)} %bitcast.22), channel_id=1, replica_groups=mesh['b8'=2,'b7'=2,'b6'=2,'b5'=2,'b4'=2,'b3'=2,'b2'=2,'b1'=2,'b0'=2] {'b..., dimensions={0} | all-to-all | bytes 917504 | tf_op jit(solution)/shard_map/all_to_all | solution.py:353
  134.8 22.5 %all_to_all.43.refs_1_ = f32[16,2,56,128]{3,2,1,0:T(8,128)S(1)} all-to-all(f32[16,2,56,128]{3,2,1,0:T(8,128)S(1)} %broadcast_in_dim.9), channel_id=1, replica_groups=mesh['b8'=2,'b7'=2,'b6'=2,'b5'=2,'b4'=2,'b3'=2,'b2'=2,'b1'=2,'b0'=2] {'b..., dimensions={0} | all-to-all | bytes 1835008 | tf_op jit(solution)/shard_map/all_to_all | solution.py:353
  157.2 4.2 %level3.1 = (f32[6,128,128]{2,1,0:T(8,128)S(1)}, f32[6,128,128]{2,1,0:T(8,128)S(1)}) custom-call(s32[9]{0:T(128)S(1)} %copy-done.2, f32[16,2,56,128]{3,2,1,0:T(8,128)S(1)} %all_to_all.43.refs_1_, f32[7,128,128]{2,1,0:T(8,128)S(1)} %get-tuple-element.49.refs_2_, f32[9,128,128]{2,1,0:T(8,128)S(1)} %copy-done), custom_call_target="tpu_custom_call" | custom-call | tf_op jit(solution)/shard_map/level3/pallas_call | solution.py:138
  161.4 20.0 %all_to_all.44 = f32[32,24,128]{2,1,0:T(8,128)S(1)} all-to-all(f32[32,24,128]{2,1,0:T(8,128)S(1)} %bitcast.23), channel_id=1, replica_groups=mesh['b8'=2,'b7'=2,'b6'=2,'b5'=2,'b4'=2,'b3'=2,'b2'=2,'b1'=2,'b0'=2] {'b..., dimensions={0} | all-to-all | bytes 786432 | tf_op jit(solution)/shard_map/all_to_all | solution.py:353
  181.5 22.3 %all_to_all.45.refs_1_ = f32[32,2,24,128]{3,2,1,0:T(8,128)S(1)} all-to-all(f32[32,2,24,128]{3,2,1,0:T(8,128)S(1)} %broadcast_in_dim.10), channel_id=1, replica_groups=mesh['b8'=2,'b7'=2,'b6'=2,'b5'=2,'b4'=2,'b3'=2,'b2'=2,'b1'=2,'b0'=2] {'b..., dimensions={0} | all-to-all | bytes 1572864 | tf_op jit(solution)/shard_map/all_to_all | solution.py:353
  203.9 4.1 %level4.1 = (f32[5,128,128]{2,1,0:T(8,128)S(1)}, f32[20,128,128]{2,1,0:T(8,128)S(1)}) custom-call(s32[9]{0:T(128)S(1)} %copy-done.2, f32[32,2,24,128]{3,2,1,0:T(8,128)S(1)} %all_to_all.45.refs_1_, f32[6,128,128]{2,1,0:T(8,128)S(1)} %get-tuple-element.51.refs_2_, f32[9,128,128]{2,1,0:T(8,128)S(1)} %copy-done), custom_call_target="tpu_custom_call" | custom-call | tf_op jit(solution)/shard_map/level4/pallas_call | solution.py:138
  208.0 30.4 %all_to_all.46 = f32[32,80,128]{2,1,0:T(8,128)} all-to-all(f32[32,80,128]{2,1,0:T(8,128)S(1)} %bitcast.21), channel_id=1, replica_groups=mesh['b8'=2,'b7'=2,'b6'=2,'b5'=2,'b4'=2,'b3'=2,'b2'=2,'b1'=2,'b0'=2] {'b..., dimensions={0} | all-to-all | bytes 2621440 | tf_op jit(solution)/shard_map/all_to_all | solution.py:353
  239.9 30.6 %all_to_all.47 = f32[32,80,128]{2,1,0:T(8,128)S(1)} all-to-all(f32[32,80,128]{2,1,0:T(8,128)S(1)} %broadcast_in_dim.11), channel_id=1, replica_groups=mesh['b8'=2,'b7'=2,'b6'=2,'b5'=2,'b4'=2,'b3'=2,'b2'=2,'b1'=2,'b0'=2] {'b..., dimensions={0} | all-to-all | bytes 2621440 | tf_op jit(solution)/shard_map/all_to_all | solution.py:353
  275.4 4.0 %front5.1 = (f32[4,128,128]{2,1,0:T(8,128)S(1)}, f32[1536,128]{1,0:T(8,128)S(1)}, f32[768,128]{1,0:T(8,128)S(1)}) custom-call(s32[9]{0:T(128)S(1)} %copy-done.2, f32[20,128,128]{2,1,0:T(8,128)S(1)} %bitcast.20, f32[20,128,128]{2,1,0:T(8,128)S(1)} %collective-permute-done.4.refs_2_), custom_call_target="tpu_custom_call" | custom-call | tf_op jit(solution)/shard_map/front5/pallas_call | solution.py:138
  282.4 10.1 %collective-permute-done.5.refs_2_ = f32[768,128]{1,0:T(8,128)S(1)} collective-permute-done((f32[768,128]{1,0:T(8,128)S(1)}, f32[768,128]{1,0:T(8,128)S(1)}, u32[]{:S(2)}, u32[]{:S(2)}) %collective-permute-start.5) | collective-permute-done | bytes 393248 | tf_op jit(solution)/shard_map/ppermute | solution.py:349
  296.0 3.8 %front6.1 = (f32[3,128,128]{2,1,0:T(8,128)S(1)}, f32[6,128,128]{2,1,0:T(8,128)S(1)}) custom-call(s32[9]{0:T(128)S(1)} %copy-done.2, f32[1536,128]{1,0:T(8,128)S(1)} %get-tuple-element.53.refs_1_, f32[768,128]{1,0:T(8,128)S(1)} %collective-permute-done.5.refs_2_, f32[768,128]{1,0:T(8,128)S(1)} %collective-permute-done.6.refs_3_), custom_call_target="tpu_custom_call" | custom-call | tf_op jit(solution)/shard_map/front6/pallas_call | solution.py:138
  303.5 10.9 %collective-permute-done.7.refs_1_ = f32[6,128,128]{2,1,0:T(8,128)S(1)} collective-permute-done((f32[6,128,128]{2,1,0:T(8,128)S(1)}, f32[6,128,128]{2,1,0:T(8,128)S(1)}, u32[]{:S(2)}, u32[]{:S(2)}) %collective-permute-start.7) | collective-permute-done | bytes 393248 | tf_op jit(solution)/shard_map/ppermute | solution.py:349
  317.4 8.3 %collective-permute-start.8 = (f32[2,128,128]{2,1,0:T(8,128)S(1)}, f32[2,128,128]{2,1,0:T(8,128)S(1)}, u32[]{:S(2)}, u32[]{:S(2)}) collective-permute-start(f32[2,128,128]{2,1,0:T(8,128)S(1)} %get-tuple-element.62.refs_0_), channel_id=1, source_target_pairs={{0,256},{256,0},{1,257},{257,1},{2,258},{258,2},{3,259},{259,3},{4... | collective-permute-start | bytes 393224 | tf_op jit(solution)/shard_map/ppermute | solution.py:349
  (44 shorter events, 38.7 us)
Async XLA Ops:
  1.3 39.0 %copy-start.2 = (s32[9]{0:T(128)S(1)}, s32[9]{0:T(128)}, u32[]{:S(2)}) copy-start(s32[9]{0:T(128)} %stack.42.flag_ref.refs_0_) | copy-start | bytes 112
  10.4 15.4 %collective-permute-start = (f32[10,128,128]{2,1,0:T(8,128)S(1)}, f32[10,128,128]{2,1,0:T(8,128)S(1)}, u32[]{:S(2)}, u32[]{:S(2)}) collective-permute-start(f32[10,128,128]{2,1,0:T(8,128)S(1)} %get-tuple-element.35.refs_0_), channel_id=1, source_target_pairs={{0,1},{1,0},{2,3},{3,2},{4,5},{5,4},{6,7},{7,6},{8,9},{9,8},{10,11... | collective-permute-start | bytes 1966088 | tf_op jit(solution)/shard_map/ppermute | solution.py:349
  25.8 14.5 %collective-permute-start.1 = (f32[10,128,128]{2,1,0:T(8,128)S(1)}, f32[10,128,128]{2,1,0:T(8,128)S(1)}, u32[]{:S(2)}, u32[]{:S(2)}) collective-permute-start(f32[10,128,128]{2,1,0:T(8,128)S(1)} %get-tuple-element.40.refs_3_), channel_id=1, source_target_pairs={{0,1},{1,0},{2,3},{3,2},{4,5},{5,4},{6,7},{7,6},{8,9},{9,8},{10,11... | collective-permute-start | bytes 1966088 | tf_op jit(solution)/shard_map/ppermute | solution.py:349
  33.5 12.6 %copy-start.1 = (f32[10,128,128]{2,1,0:T(8,128)S(1)}, f32[10,128,128]{2,1,0:T(8,128)}, u32[]{:S(2)}) copy-start(f32[10,128,128]{2,1,0:T(8,128)} %get-tuple-element.43.refs_0_) | copy-start | bytes 1966084
  41.5 21.9 %copy-start = (f32[9,128,128]{2,1,0:T(8,128)S(1)}, f32[9,128,128]{2,1,0:T(8,128)}, u32[]{:S(2)}) copy-start(f32[9,128,128]{2,1,0:T(8,128)} %refs_3_.5) | copy-start | bytes 1769476
  41.5 13.3 %collective-permute-start.2 = (f32[576,128]{1,0:T(8,128)S(1)}, f32[576,128]{1,0:T(8,128)S(1)}, u32[]{:S(2)}, u32[]{:S(2)}) collective-permute-start(f32[576,128]{1,0:T(8,128)S(1)} %get-tuple-element.42), channel_id=1, source_target_pairs={{0,2},{2,0},{1,3},{3,1},{4,6},{6,4},{5,7},{7,5},{8,10},{10,8},{9,1... | collective-permute-start | bytes 884744 | tf_op jit(solution)/shard_map/ppermute | solution.py:349
  54.8 8.6 %collective-permute-start.3 = (f32[576,128]{1,0:T(8,128)S(1)}, f32[576,128]{1,0:T(8,128)S(1)}, u32[]{:S(2)}, u32[]{:S(2)}) collective-permute-start(f32[576,128]{1,0:T(8,128)S(1)} %collective-permute-done.2.refs_2_), channel_id=1, source_target_pairs={{0,1},{1,0},{2,3},{3,2},{4,5},{5,4},{6,7},{7,6},{8,9},{9,8},{10,11... | collective-permute-start | bytes 884744 | tf_op jit(solution)/shard_map/ppermute | solution.py:349
  270.5 4.9 %collective-permute-start.4 = (f32[20,128,128]{2,1,0:T(8,128)S(1)}, f32[20,128,128]{2,1,0:T(8,128)S(1)}, u32[]{:S(2)}, u32[]{:S(2)}) collective-permute-start(f32[20,128,128]{2,1,0:T(8,128)S(1)} %bitcast.19), channel_id=1, source_target_pairs={{0,32},{32,0},{1,33},{33,1},{2,34},{34,2},{3,35},{35,3},{4,36},{36... | collective-permute-start | bytes 3932168 | tf_op jit(solution)/shard_map/ppermute | solution.py:349
  279.4 13.1 %collective-permute-start.5 = (f32[768,128]{1,0:T(8,128)S(1)}, f32[768,128]{1,0:T(8,128)S(1)}, u32[]{:S(2)}, u32[]{:S(2)}) collective-permute-start(f32[768,128]{1,0:T(8,128)S(1)} %get-tuple-element.54), channel_id=1, source_target_pairs={{0,64},{64,0},{1,65},{65,1},{2,66},{66,2},{3,67},{67,3},{4,68},{68... | collective-permute-start | bytes 1179656 | tf_op jit(solution)/shard_map/ppermute | solution.py:349
  292.4 3.6 %collective-permute-start.6 = (f32[768,128]{1,0:T(8,128)S(1)}, f32[768,128]{1,0:T(8,128)S(1)}, u32[]{:S(2)}, u32[]{:S(2)}) collective-permute-start(f32[768,128]{1,0:T(8,128)S(1)} %collective-permute-done.5.refs_2_), channel_id=1, source_target_pairs={{0,32},{32,0},{1,33},{33,1},{2,34},{34,2},{3,35},{35,3},{4,36},{36... | collective-permute-start | bytes 1179656 | tf_op jit(solution)/shard_map/ppermute | solution.py:349
  299.8 14.6 %collective-permute-start.7 = (f32[6,128,128]{2,1,0:T(8,128)S(1)}, f32[6,128,128]{2,1,0:T(8,128)S(1)}, u32[]{:S(2)}, u32[]{:S(2)}) collective-permute-start(f32[6,128,128]{2,1,0:T(8,128)S(1)} %get-tuple-element.58.refs_0_), channel_id=1, source_target_pairs={{0,128},{128,0},{1,129},{129,1},{2,130},{130,2},{3,131},{131,3},{4... | collective-permute-start | bytes 1179656 | tf_op jit(solution)/shard_map/ppermute | solution.py:349
  317.4 12.2 %collective-permute-start.8 = (f32[2,128,128]{2,1,0:T(8,128)S(1)}, f32[2,128,128]{2,1,0:T(8,128)S(1)}, u32[]{:S(2)}, u32[]{:S(2)}) collective-permute-start(f32[2,128,128]{2,1,0:T(8,128)S(1)} %get-tuple-element.62.refs_0_), channel_id=1, source_target_pairs={{0,256},{256,0},{1,257},{257,1},{2,258},{258,2},{3,259},{259,3},{4... | collective-permute-start | bytes 393224 | tf_op jit(solution)/shard_map/ppermute | solution.py:349
  325.9 7.0 %copy-start.3 = (f32[9,128,128]{2,1,0:T(8,128)}, f32[9,128,128]{2,1,0:T(8,128)S(1)}, u32[]{:S(2)}) copy-start(f32[9,128,128]{2,1,0:T(8,128)S(1)} %slice_dynamic-update-slice_fusion) | copy-start | bytes 1769476

commit v7 on v6

--- a/solution.py
+++ b/solution.py
@@ -9,7 +9,7 @@
 BITS = 9
 NAMES = tuple("b%d" % bit for bit in reversed(range(BITS)))
 TOP = 5
-STAGGER = 3000
+STAGGER = 4000
 ROUNDS = (9, 7, 6, 6, 5, 5, 5, 5, 5)
 N = 128
 

time: 334 us -> 364 us (1.090)
  starting transfers between devices: 32.3 us -> 68 us
  blocking collectives: 188 us -> 177 us
    ppermute x9, starting transfers between devices: 32.3 us -> 68 us  [partner(): return lax.ppermute(value, 'b%d' % bit, [(0, 1), (1, 0)])]
    all_to_all x8, blocking collectives: 188 us -> 177 us  [exchange(): return lax.all_to_all(value, names, 0, 0)]
  transfers between devices with their start and end apart: 9 -> 9, of which waited for: 9 -> 9; matrix products, arithmetic and copies ran while one was open for 0% -> 0% of each run, Pallas kernels for 2% -> 1%
where the time goes in v7:
time: 364 us; the launch traced here: 360 us
  blocking collectives  177 us (49%)
  starting transfers between devices  68 us (19%)
  waiting for transfers between devices  64.6 us (18%)
  Pallas kernels  47.2 us (13%)
    all_to_all x8, blocking collectives, exchange(): return lax.all_to_all(value, names, 0, 0)  177 us
    ppermute x9, starting transfers between devices, partner(): return lax.ppermute(value, 'b%d' % bit, [(0, 1), (1, 0)])  68 us
    ppermute x9, waiting for transfers between devices, partner(): return lax.ppermute(value, 'b%d' % bit, [(0, 1), (1, 0)])  64.6 us
    pallas_call x14, Pallas kernels, call(): pl.pallas_call(kernel, out_shape=outs, in_specs=specs, scratch_shapes=scr...  37 us
    pallas_call x1, Pallas kernels, leaf(): pl.pallas_call(leaf_kernel, out_shape=(jax.ShapeDtypeStruct((10, N, N), j...  10.2 us
  transfers between devices with their start and end apart: 9, of which 9 were waited for; matrix products, arithmetic and copies ran while one was open for 0% of the time, Pallas kernels for 1%

profile of v7, /device:TPU:6, one launch (start us, length us, event | category | flops | bytes accessed | tf_op | source)
XLA Modules:
  0.0 360.4 jit_solution(111373754522288565)
XLA Ops:
  1.3 10.2 %leaf.1 = (f32[10,128,128]{2,1,0:T(8,128)}, f32[10,128,128]{2,1,0:T(8,128)S(1)}, f32[10,128,128]{2,1,0:T(8,128)S(1)}) custom-call(s32[9]{0:T(128)} %stack.42.flag_ref.refs_0_, f32[128,128]{1,0:T(8,128)} %diag_any.1, f32[9,128,128]{2,1,0:T(8,128)} %left_any.1, f32[128,128]{1,0:T(8,128)} %source_any.1, f32[9,128,128]{2,1,0:T(8,128)} %refs_3_.5), custom_call_target="tpu_custom_call" | custom-call | tf_op jit(solution)/shard_map/leaf/pallas_call | solution.py:181
  14.9 11.4 %collective-permute-done.refs_1_ = f32[10,128,128]{2,1,0:T(8,128)S(1)} collective-permute-done((f32[10,128,128]{2,1,0:T(8,128)S(1)}, f32[10,128,128]{2,1,0:T(8,128)S(1)}, u32[]{:S(2)}, u32[]{:S(2)}) %collective-permute-start) | collective-permute-done | bytes 655392 | tf_op jit(solution)/shard_map/ppermute | solution.py:349
  29.8 4.3 %pair.1 = (f32[128,1152]{1,0:T(8,128)S(1)}, f32[128,1152]{1,0:T(8,128)S(1)}) custom-call(f32[10,128,128]{2,1,0:T(8,128)S(1)} %get-tuple-element.35.refs_0_, f32[10,128,128]{2,1,0:T(8,128)S(1)} %collective-permute-done.refs_1_), custom_call_target="tpu_custom_call" | custom-call | tf_op jit(solution)/shard_map/pair/pallas_call | solution.py:138
  34.1 5.7 %collective-permute-done.1.refs_4_ = f32[10,128,128]{2,1,0:T(8,128)S(1)} collective-permute-done((f32[10,128,128]{2,1,0:T(8,128)S(1)}, f32[10,128,128]{2,1,0:T(8,128)S(1)}, u32[]{:S(2)}, u32[]{:S(2)}) %collective-permute-start.1) | collective-permute-done | bytes 655392 | tf_op jit(solution)/shard_map/ppermute | solution.py:349
  41.1 4.8 %collective-permute-start.2 = (f32[576,128]{1,0:T(8,128)S(1)}, f32[576,128]{1,0:T(8,128)S(1)}, u32[]{:S(2)}, u32[]{:S(2)}) collective-permute-start(f32[576,128]{1,0:T(8,128)S(1)} %get-tuple-element.42), channel_id=1, source_target_pairs={{0,2},{2,0},{1,3},{3,1},{4,6},{6,4},{5,7},{7,5},{8,10},{10,8},{9,1... | collective-permute-start | bytes 884744 | tf_op jit(solution)/shard_map/ppermute | solution.py:349
  46.3 7.7 %collective-permute-done.2.refs_2_ = f32[576,128]{1,0:T(8,128)S(1)} collective-permute-done((f32[576,128]{1,0:T(8,128)S(1)}, f32[576,128]{1,0:T(8,128)S(1)}, u32[]{:S(2)}, u32[]{:S(2)}) %collective-permute-start.2) | collective-permute-done | bytes 294944 | tf_op jit(solution)/shard_map/ppermute | solution.py:349
  56.6 6.0 %collective-permute-done.3.refs_3_ = f32[576,128]{1,0:T(8,128)S(1)} collective-permute-done((f32[576,128]{1,0:T(8,128)S(1)}, f32[576,128]{1,0:T(8,128)S(1)}, u32[]{:S(2)}, u32[]{:S(2)}) %collective-permute-start.3) | collective-permute-done | bytes 294944 | tf_op jit(solution)/shard_map/ppermute | solution.py:349
  62.6 4.4 %quad.1 = (f32[8,128,128]{2,1,0:T(8,128)S(1)}, f32[8,128,128]{2,1,0:T(8,128)S(1)}) custom-call(s32[9]{0:T(128)S(1)} %copy-done.2, f32[1152,128]{1,0:T(8,128)S(1)} %get-tuple-element.41.refs_1_, f32[576,128]{1,0:T(8,128)S(1)} %collective-permute-done.2.refs_2_, f32[576,128]{1,0:T(8,128)S(1)} %collective-permute-done.3.refs_3_, ...), custom_call_target="tpu_custom_call" | custom-call | tf_op jit(solution)/shard_map/quad/pallas_call | solution.py:138
  67.0 20.3 %all_to_all.40 = f32[8,128,128]{2,1,0:T(8,128)S(1)} all-to-all(f32[8,128,128]{2,1,0:T(8,128)S(1)} %get-tuple-element.46), channel_id=1, replica_groups=mesh['b8'=2,'b7'=2,'b6'=2,'b5'=2,'b4'=2,'b3'=2,'b2'=2,'b1'=2,'b0'=2] {'b..., dimensions={0} | all-to-all | bytes 1048576 | tf_op jit(solution)/shard_map/all_to_all | solution.py:353
  87.4 24.4 %all_to_all.41.refs_1_ = f32[8,2,128,128]{3,2,1,0:T(8,128)S(1)} all-to-all(f32[8,2,128,128]{3,2,1,0:T(8,128)S(1)} %broadcast_in_dim.8), channel_id=1, replica_groups=mesh['b8'=2,'b7'=2,'b6'=2,'b5'=2,'b4'=2,'b3'=2,'b2'=2,'b1'=2,'b0'=2] {'b..., dimensions={0} | all-to-all | bytes 2097152 | tf_op jit(solution)/shard_map/all_to_all | solution.py:353
  111.9 4.3 %level2.1 = (f32[7,128,128]{2,1,0:T(8,128)S(1)}, f32[7,128,128]{2,1,0:T(8,128)S(1)}) custom-call(s32[9]{0:T(128)S(1)} %copy-done.2, f32[8,2,128,128]{3,2,1,0:T(8,128)S(1)} %all_to_all.41.refs_1_, f32[8,128,128]{2,1,0:T(8,128)S(1)} %get-tuple-element.47.refs_2_, f32[9,128,128]{2,1,0:T(8,128)S(1)} %copy-done), custom_call_target="tpu_custom_call" | custom-call | tf_op jit(solution)/shard_map/level2/pallas_call | solution.py:138
  116.2 14.4 %all_to_all.42 = f32[16,56,128]{2,1,0:T(8,128)S(1)} all-to-all(f32[16,56,128]{2,1,0:T(8,128)S(1)} %bitcast.22), channel_id=1, replica_groups=mesh['b8'=2,'b7'=2,'b6'=2,'b5'=2,'b4'=2,'b3'=2,'b2'=2,'b1'=2,'b0'=2] {'b..., dimensions={0} | all-to-all | bytes 917504 | tf_op jit(solution)/shard_map/all_to_all | solution.py:353
  130.6 20.6 %all_to_all.43.refs_1_ = f32[16,2,56,128]{3,2,1,0:T(8,128)S(1)} all-to-all(f32[16,2,56,128]{3,2,1,0:T(8,128)S(1)} %broadcast_in_dim.9), channel_id=1, replica_groups=mesh['b8'=2,'b7'=2,'b6'=2,'b5'=2,'b4'=2,'b3'=2,'b2'=2,'b1'=2,'b0'=2] {'b..., dimensions={0} | all-to-all | bytes 1835008 | tf_op jit(solution)/shard_map/all_to_all | solution.py:353
  151.3 4.2 %level3.1 = (f32[6,128,128]{2,1,0:T(8,128)S(1)}, f32[6,128,128]{2,1,0:T(8,128)S(1)}) custom-call(s32[9]{0:T(128)S(1)} %copy-done.2, f32[16,2,56,128]{3,2,1,0:T(8,128)S(1)} %all_to_all.43.refs_1_, f32[7,128,128]{2,1,0:T(8,128)S(1)} %get-tuple-element.49.refs_2_, f32[9,128,128]{2,1,0:T(8,128)S(1)} %copy-done), custom_call_target="tpu_custom_call" | custom-call | tf_op jit(solution)/shard_map/level3/pallas_call | solution.py:138
  155.5 19.7 %all_to_all.44 = f32[32,24,128]{2,1,0:T(8,128)S(1)} all-to-all(f32[32,24,128]{2,1,0:T(8,128)S(1)} %bitcast.23), channel_id=1, replica_groups=mesh['b8'=2,'b7'=2,'b6'=2,'b5'=2,'b4'=2,'b3'=2,'b2'=2,'b1'=2,'b0'=2] {'b..., dimensions={0} | all-to-all | bytes 786432 | tf_op jit(solution)/shard_map/all_to_all | solution.py:353
  175.3 21.6 %all_to_all.45.refs_1_ = f32[32,2,24,128]{3,2,1,0:T(8,128)S(1)} all-to-all(f32[32,2,24,128]{3,2,1,0:T(8,128)S(1)} %broadcast_in_dim.10), channel_id=1, replica_groups=mesh['b8'=2,'b7'=2,'b6'=2,'b5'=2,'b4'=2,'b3'=2,'b2'=2,'b1'=2,'b0'=2] {'b..., dimensions={0} | all-to-all | bytes 1572864 | tf_op jit(solution)/shard_map/all_to_all | solution.py:353
  196.9 4.1 %level4.1 = (f32[5,128,128]{2,1,0:T(8,128)S(1)}, f32[20,128,128]{2,1,0:T(8,128)S(1)}) custom-call(s32[9]{0:T(128)S(1)} %copy-done.2, f32[32,2,24,128]{3,2,1,0:T(8,128)S(1)} %all_to_all.45.refs_1_, f32[6,128,128]{2,1,0:T(8,128)S(1)} %get-tuple-element.51.refs_2_, f32[9,128,128]{2,1,0:T(8,128)S(1)} %copy-done), custom_call_target="tpu_custom_call" | custom-call | tf_op jit(solution)/shard_map/level4/pallas_call | solution.py:138
  201.0 27.8 %all_to_all.46 = f32[32,80,128]{2,1,0:T(8,128)} all-to-all(f32[32,80,128]{2,1,0:T(8,128)S(1)} %bitcast.21), channel_id=1, replica_groups=mesh['b8'=2,'b7'=2,'b6'=2,'b5'=2,'b4'=2,'b3'=2,'b2'=2,'b1'=2,'b0'=2] {'b..., dimensions={0} | all-to-all | bytes 2621440 | tf_op jit(solution)/shard_map/all_to_all | solution.py:353
  230.4 27.6 %all_to_all.47 = f32[32,80,128]{2,1,0:T(8,128)S(1)} all-to-all(f32[32,80,128]{2,1,0:T(8,128)S(1)} %broadcast_in_dim.11), channel_id=1, replica_groups=mesh['b8'=2,'b7'=2,'b6'=2,'b5'=2,'b4'=2,'b3'=2,'b2'=2,'b1'=2,'b0'=2] {'b..., dimensions={0} | all-to-all | bytes 2621440 | tf_op jit(solution)/shard_map/all_to_all | solution.py:353
  262.9 4.0 %front5.1 = (f32[4,128,128]{2,1,0:T(8,128)S(1)}, f32[1536,128]{1,0:T(8,128)S(1)}, f32[768,128]{1,0:T(8,128)S(1)}) custom-call(s32[9]{0:T(128)S(1)} %copy-done.2, f32[20,128,128]{2,1,0:T(8,128)S(1)} %bitcast.20, f32[20,128,128]{2,1,0:T(8,128)S(1)} %collective-permute-done.4.refs_2_), custom_call_target="tpu_custom_call" | custom-call | tf_op jit(solution)/shard_map/front5/pallas_call | solution.py:138
  270.0 10.0 %collective-permute-done.5.refs_2_ = f32[768,128]{1,0:T(8,128)S(1)} collective-permute-done((f32[768,128]{1,0:T(8,128)S(1)}, f32[768,128]{1,0:T(8,128)S(1)}, u32[]{:S(2)}, u32[]{:S(2)}) %collective-permute-start.5) | collective-permute-done | bytes 393248 | tf_op jit(solution)/shard_map/ppermute | solution.py:349
  287.4 45.1 %collective-permute-start.7 = (f32[6,128,128]{2,1,0:T(8,128)S(1)}, f32[6,128,128]{2,1,0:T(8,128)S(1)}, u32[]{:S(2)}, u32[]{:S(2)}) collective-permute-start(f32[6,128,128]{2,1,0:T(8,128)S(1)} %get-tuple-element.58.refs_0_), channel_id=1, source_target_pairs={{0,128},{128,0},{1,129},{129,1},{2,130},{130,2},{3,131},{131,3},{4... | collective-permute-start | bytes 1179656 | tf_op jit(solution)/shard_map/ppermute | solution.py:349
  332.8 9.1 %collective-permute-done.7.refs_1_ = f32[6,128,128]{2,1,0:T(8,128)S(1)} collective-permute-done((f32[6,128,128]{2,1,0:T(8,128)S(1)}, f32[6,128,128]{2,1,0:T(8,128)S(1)}, u32[]{:S(2)}, u32[]{:S(2)}) %collective-permute-start.7) | collective-permute-done | bytes 393248 | tf_op jit(solution)/shard_map/ppermute | solution.py:349
  347.1 10.0 %collective-permute-done.8.refs_1_ = f32[2,128,128]{2,1,0:T(8,128)S(1)} collective-permute-done((f32[2,128,128]{2,1,0:T(8,128)S(1)}, f32[2,128,128]{2,1,0:T(8,128)S(1)}, u32[]{:S(2)}, u32[]{:S(2)}) %collective-permute-start.8) | collective-permute-done | bytes 131104 | tf_op jit(solution)/shard_map/ppermute | solution.py:349
  (44 shorter events, 37.5 us)
Async XLA Ops:
  1.3 38.6 %copy-start.2 = (s32[9]{0:T(128)S(1)}, s32[9]{0:T(128)}, u32[]{:S(2)}) copy-start(s32[9]{0:T(128)} %stack.42.flag_ref.refs_0_) | copy-start | bytes 112
  11.4 14.9 %collective-permute-start = (f32[10,128,128]{2,1,0:T(8,128)S(1)}, f32[10,128,128]{2,1,0:T(8,128)S(1)}, u32[]{:S(2)}, u32[]{:S(2)}) collective-permute-start(f32[10,128,128]{2,1,0:T(8,128)S(1)} %get-tuple-element.35.refs_0_), channel_id=1, source_target_pairs={{0,1},{1,0},{2,3},{3,2},{4,5},{5,4},{6,7},{7,6},{8,9},{9,8},{10,11... | collective-permute-start | bytes 1966088 | tf_op jit(solution)/shard_map/ppermute | solution.py:349
  26.3 13.5 %collective-permute-start.1 = (f32[10,128,128]{2,1,0:T(8,128)S(1)}, f32[10,128,128]{2,1,0:T(8,128)S(1)}, u32[]{:S(2)}, u32[]{:S(2)}) collective-permute-start(f32[10,128,128]{2,1,0:T(8,128)S(1)} %get-tuple-element.40.refs_3_), channel_id=1, source_target_pairs={{0,1},{1,0},{2,3},{3,2},{4,5},{5,4},{6,7},{7,6},{8,9},{9,8},{10,11... | collective-permute-start | bytes 1966088 | tf_op jit(solution)/shard_map/ppermute | solution.py:349
  34.1 11.8 %copy-start.1 = (f32[10,128,128]{2,1,0:T(8,128)S(1)}, f32[10,128,128]{2,1,0:T(8,128)}, u32[]{:S(2)}) copy-start(f32[10,128,128]{2,1,0:T(8,128)} %get-tuple-element.43.refs_0_) | copy-start | bytes 1966084
  41.0 21.5 %copy-start = (f32[9,128,128]{2,1,0:T(8,128)S(1)}, f32[9,128,128]{2,1,0:T(8,128)}, u32[]{:S(2)}) copy-start(f32[9,128,128]{2,1,0:T(8,128)} %refs_3_.5) | copy-start | bytes 1769476
  41.1 12.9 %collective-permute-start.2 = (f32[576,128]{1,0:T(8,128)S(1)}, f32[576,128]{1,0:T(8,128)S(1)}, u32[]{:S(2)}, u32[]{:S(2)}) collective-permute-start(f32[576,128]{1,0:T(8,128)S(1)} %get-tuple-element.42), channel_id=1, source_target_pairs={{0,2},{2,0},{1,3},{3,1},{4,6},{6,4},{5,7},{7,5},{8,10},{10,8},{9,1... | collective-permute-start | bytes 884744 | tf_op jit(solution)/shard_map/ppermute | solution.py:349
  54.0 8.6 %collective-permute-start.3 = (f32[576,128]{1,0:T(8,128)S(1)}, f32[576,128]{1,0:T(8,128)S(1)}, u32[]{:S(2)}, u32[]{:S(2)}) collective-permute-start(f32[576,128]{1,0:T(8,128)S(1)} %collective-permute-done.2.refs_2_), channel_id=1, source_target_pairs={{0,1},{1,0},{2,3},{3,2},{4,5},{5,4},{6,7},{7,6},{8,9},{9,8},{10,11... | collective-permute-start | bytes 884744 | tf_op jit(solution)/shard_map/ppermute | solution.py:349
  258.0 4.9 %collective-permute-start.4 = (f32[20,128,128]{2,1,0:T(8,128)S(1)}, f32[20,128,128]{2,1,0:T(8,128)S(1)}, u32[]{:S(2)}, u32[]{:S(2)}) collective-permute-start(f32[20,128,128]{2,1,0:T(8,128)S(1)} %bitcast.19), channel_id=1, source_target_pairs={{0,32},{32,0},{1,33},{33,1},{2,34},{34,2},{3,35},{35,3},{4,36},{36... | collective-permute-start | bytes 3932168 | tf_op jit(solution)/shard_map/ppermute | solution.py:349
  266.9 13.0 %collective-permute-start.5 = (f32[768,128]{1,0:T(8,128)S(1)}, f32[768,128]{1,0:T(8,128)S(1)}, u32[]{:S(2)}, u32[]{:S(2)}) collective-permute-start(f32[768,128]{1,0:T(8,128)S(1)} %get-tuple-element.54), channel_id=1, source_target_pairs={{0,64},{64,0},{1,65},{65,1},{2,66},{66,2},{3,67},{67,3},{4,68},{68... | collective-permute-start | bytes 1179656 | tf_op jit(solution)/shard_map/ppermute | solution.py:349
  280.0 3.6 %collective-permute-start.6 = (f32[768,128]{1,0:T(8,128)S(1)}, f32[768,128]{1,0:T(8,128)S(1)}, u32[]{:S(2)}, u32[]{:S(2)}) collective-permute-start(f32[768,128]{1,0:T(8,128)S(1)} %collective-permute-done.5.refs_2_), channel_id=1, source_target_pairs={{0,32},{32,0},{1,33},{33,1},{2,34},{34,2},{3,35},{35,3},{4,36},{36... | collective-permute-start | bytes 1179656 | tf_op jit(solution)/shard_map/ppermute | solution.py:349
  287.4 54.5 %collective-permute-start.7 = (f32[6,128,128]{2,1,0:T(8,128)S(1)}, f32[6,128,128]{2,1,0:T(8,128)S(1)}, u32[]{:S(2)}, u32[]{:S(2)}) collective-permute-start(f32[6,128,128]{2,1,0:T(8,128)S(1)} %get-tuple-element.58.refs_0_), channel_id=1, source_target_pairs={{0,128},{128,0},{1,129},{129,1},{2,130},{130,2},{3,131},{131,3},{4... | collective-permute-start | bytes 1179656 | tf_op jit(solution)/shard_map/ppermute | solution.py:349
  344.9 12.2 %collective-permute-start.8 = (f32[2,128,128]{2,1,0:T(8,128)S(1)}, f32[2,128,128]{2,1,0:T(8,128)S(1)}, u32[]{:S(2)}, u32[]{:S(2)}) collective-permute-start(f32[2,128,128]{2,1,0:T(8,128)S(1)} %get-tuple-element.62.refs_0_), channel_id=1, source_target_pairs={{0,256},{256,0},{1,257},{257,1},{2,258},{258,2},{3,259},{259,3},{4... | collective-permute-start | bytes 393224 | tf_op jit(solution)/shard_map/ppermute | solution.py:349
  347.1 13.4 %copy-start.3 = (f32[9,128,128]{2,1,0:T(8,128)}, f32[9,128,128]{2,1,0:T(8,128)S(1)}, u32[]{:S(2)}) copy-start(f32[9,128,128]{2,1,0:T(8,128)S(1)} %slice_dynamic-update-slice_fusion) | copy-start | bytes 1769476
